TPU v7x, 512 devices: a whole 4x8x8 slice. The times are simulated.
512 devices in a mesh: pix: 64 (over z, y), mode: 8 (over x, core).
Axes of the slice: x: 4, y: 8, z: 8, core: 2. Of those that a mesh axis runs over, the one named last changes fastest.
Arguments:
- frames: bfloat16 [4, 32768, 2048], P(None, 'pix', 'mode'), may hold values from 0 to 4
- ref_pixels: int32 [64], replicated, may hold values from 0 to 32767
Outputs:
- gram_band: float32 [2, 2048, 1024], P(None, 'mode', 'pix')
- gram_diag: float32 [2, 2048, 256], P(None, 'mode', 'pix')
Inputs may be any that keep to these rules, and one draw needn't show every extreme that they name: `ref_pixels`: indices of reference pixels; an index may appear more than once.
All inputs are finite; a program needn't handle non-finite values.
Results may differ from a plain program's by a relative error of at most 0.0088.
Values may be sent and summed in bfloat16 or wider, within the bound.
No kernel may reach another device: no remote copies, remote signals or barrier semaphores. Data moves between devices by JAX's collectives and lax.ppermute only.
A program may use at most 64 MiB of HBM per device.

v0:
```python
import math

import jax
import jax.numpy as jnp
from jax import lax
from jax.sharding import PartitionSpec as P


def unit_phase(sums):
    magnitude = jnp.maximum(jnp.sqrt(sums[0] * sums[0] + sums[1] * sums[1]), 1.0)
    return sums / magnitude[None, :]


def rotate(gram_real, gram_imag, phase_rows, phase_cols, pixel_scale):
    row_real = phase_rows[0][:, None]
    row_imag = phase_rows[1][:, None]
    col_real = phase_cols[0][None, :]
    col_imag = phase_cols[1][None, :]
    unit_real = row_real * col_real + row_imag * col_imag
    unit_imag = row_imag * col_real - row_real * col_imag
    return jnp.stack(
        [
            (unit_real * gram_real - unit_imag * gram_imag) * pixel_scale,
            (unit_real * gram_imag + unit_imag * gram_real) * pixel_scale,
        ]
    )


def shards(frames, ref_pixels):
    pix_count = lax.axis_size("pix")
    mode_count = lax.axis_size("mode")
    pix_index = lax.axis_index("pix")
    mode_index = lax.axis_index("mode")
    pixel_rows = frames.shape[1]
    block_width = frames.shape[2]
    full_tiles = mode_count // 2 + 1
    full_width = full_tiles * block_width
    frame_float = frames.astype(jnp.float32)
    real_part = (frame_float[0] - frame_float[2]).astype(jnp.bfloat16)
    imag_part = (frame_float[3] - frame_float[1]).astype(jnp.bfloat16)
    fields = jnp.stack([real_part, imag_part])
    positions = pix_index * pixel_rows + lax.iota(jnp.int32, pixel_rows)
    counts = jnp.sum(
        (ref_pixels[:, None] == positions[None, :]).astype(jnp.float32), axis=0
    ).astype(jnp.bfloat16)
    local_ref = jnp.einsum("p,cpm->cm", counts, fields, preferred_element_type=jnp.float32)
    own_ref = lax.psum(local_ref, "pix")
    phase_all = lax.all_gather(unit_phase(own_ref), "mode", axis=1, tiled=True)
    phase_own = lax.dynamic_slice_in_dim(phase_all, mode_index * block_width, block_width, 1)
    phase_twice = jnp.concatenate([phase_all, phase_all], axis=1)
    phase_full = lax.dynamic_slice_in_dim(phase_twice, mode_index * block_width, full_width, 1)
    whole_fields = lax.all_gather(fields, "mode", axis=2, tiled=True)
    tiled = whole_fields.reshape(2, pixel_rows, mode_count, block_width)
    picked = (mode_index + lax.iota(jnp.int32, full_tiles)) % mode_count
    band_fields = jnp.take(tiled, picked, axis=2).reshape(2, pixel_rows, full_width)
    contract = (((0,), (0,)), ((), ()))
    own_real = fields[0]
    own_imag = fields[1]
    band_real = band_fields[0]
    band_imag = band_fields[1]
    gram_real = lax.dot_general(
        own_real, band_real, contract, preferred_element_type=jnp.float32
    ) + lax.dot_general(own_imag, band_imag, contract, preferred_element_type=jnp.float32)
    gram_imag = lax.dot_general(
        own_real, band_imag, contract, preferred_element_type=jnp.float32
    ) - lax.dot_general(own_imag, band_real, contract, preferred_element_type=jnp.float32)
    pixel_scale = 1.0 / math.sqrt(pix_count * pixel_rows)
    rotated_terms = rotate(gram_real, gram_imag, phase_own, phase_full, pixel_scale)
    diag_out, band_out = (
        lax.psum_scatter(rotated_terms[:, :, :block_width], "pix", scatter_dimension=2, tiled=True),
        lax.psum_scatter(rotated_terms[:, :, block_width:], "pix", scatter_dimension=2, tiled=True),
    )
    return (band_out, diag_out)


def solution(mesh):
    placed = (P(None, "pix", "mode"), P())
    return jax.shard_map(
        shards,
        mesh=mesh,
        in_specs=placed,
        out_specs=(P(None, "mode", "pix"), P(None, "mode", "pix")),
        check_vma=False,
    )
```

profile of v0, /device:TPU:6, one launch (start us, length us, event | category | flops | bytes accessed | tf_op | source)
XLA Modules:
  0.0 359.8 jit_solution(8418311574635005420)
XLA Ops:
  7.2 0.0 all-gather.2.cloned.1.call-start
  7.2 1.5 copy.24
  8.7 0.3 convert_element_type.27
  9.0 0.2 fusion.2
  9.2 0.8 pad_maximum_fusion.1
  10.0 0.0 all-reduce.5.cloned.1.call-start
  10.1 0.1 convert_reduce_fusion
  10.2 1.3 fusion.17
  11.5 149.9 %psum.7 = f32[2,256]{1,0:T(2,128)S(1)} all-reduce(f32[2,256]{1,0:T(2,128)S(1)} %bitcast.41), channel_id=1, replica_groups=mesh['pix'=64,'mode'=8] {'pix'}, use_global_device_ids=true, to_apply=%region_1.0 | all-reduce | flops 512 | bytes 4096 | tf_op jit(solution)/shard_map/psum | solution.py:47
  161.4 11.0 %all_gather.6 = f32[2,2048]{1,0:T(2,128)S(1)} all-gather(f32[2,256]{1,0:T(2,128)S(1)} %broadcast_divide_fusion), channel_id=1, replica_groups=mesh['pix'=64,'mode'=8] {'mode'}, dimensions={1}, use_global_device_ids=true | all-gather | bytes 18432 | tf_op jit(solution)/shard_map/all_gather | solution.py:48
  172.4 0.1 constant_dynamic-slice_fusion.2
  172.6 0.0 all-gather.2.cloned.1.call-done
  172.6 6.2 %copy.25 = bf16[2,512,8,256]{3,1,2,0:T(8,128)(2,1)} copy(bf16[2,512,8,256]{1,3,2,0:T(8,128)(2,1)} %bitcast.40) | data formatting | bytes 8388608 | tf_op jit(solution)/shard_map/reshape | solution.py:53
  178.9 2.9 gather_fusion
  181.8 0.3 select_bitcast_fusion
  182.1 1.3 fusion.14
  183.4 0.7 copy.26
  184.1 1.6 fusion.7
  185.8 1.6 copy.27
  187.4 0.5 fusion.5
  187.9 0.6 convolution_subtract_fusion
  188.5 0.7 copy-done
  189.2 0.9 multiply_bitcast_fusion
  190.2 0.3 fusion
  190.5 2.4 copy.28
  192.8 1.0 copy.29
  193.9 1.3 dynamic-slice
  196.5 153.8 %all-reduce.5.cloned.1.call-done = (f32[2,256,1024]{1,0,2:T(2,128)}, f32[2,256,256]{1,0,2:T(2,128)}) async-done(((f32[2,256,1024]{1,0,2:T(2,128)}, f32[2,256,256]{1,0,2:T(2,128)}), (f32[2,256,1024]{1,0,2:T(2,128)}, f32[2,256,256]{1,0,2:T(2,128)})) %all-reduce.5.cloned.1.call-update) | async-done | bytes 2621456
  350.2 0.8 constant_dynamic-slice_fusion.1
  351.0 0.6 copy.30
  351.6 0.7 constant_dynamic-slice_fusion
  352.3 0.6 copy.31
  (16 shorter events, 0.2 us)
Async XLA Ops:
  7.2 165.5 %all-gather.2.cloned.1.call-start = ((), (), s32[]{:S(2)}) async-start(), calls=%async_computation | async-start | bytes 4718592 | tf_op jit(solution)/shard_map/all_gather | solution.py:52
  9.2 0.9 copy-start.1
  10.0 340.2 %all-reduce.5.cloned.1.call-start = ((), (), s32[]{:S(2)}) async-start(), calls=%async_computation.1 | async-start | bytes 5242880
  187.9 1.3 copy-start
Sparse Core Ops, SparseCore 0:
  10.2 40.1 all-gather.1
  194.0 156.1 all-reduce.4
where the time goes:
time: 360 us
  blocking collectives  161 us (45%)
  waiting for transfers between devices  154 us (43%)
  local copies, waits for them, and re-layouts  22.4 us (6%)
  between operations  15.5 us (4%)
  matrix products  4.9 us (1%)
    unnamed x3, waiting for transfers between devices  154 us
    psum x1, blocking collectives, shards(): own_ref = lax.psum(local_ref, 'pix')  150 us
    all_gather x1, blocking collectives, shards(): phase_all = lax.all_gather(unit_phase(own_ref), 'mode', axis=1, tiled=True)  11 us
  transfers between devices with their start and end apart: 2, of which 1 were waited for; matrix products, arithmetic and copies ran while one was open for 1% of the time, Pallas kernels for 0%

commit v1 on v0

v1 whole, which is shorter than its diff:
```python
import math

import jax
import jax.numpy as jnp
from jax import lax
from jax.experimental import pallas as pl
from jax.experimental.pallas import tpu as pltpu
from jax.sharding import PartitionSpec as P

BF16 = jnp.bfloat16
F32 = jnp.float32
VMEM = pl.BlockSpec(memory_space=pltpu.VMEM)
SMEM = pl.BlockSpec(memory_space=pltpu.SMEM)
REF_ROWS = 8


def cost(flops, nbytes):
    return pl.CostEstimate(flops=flops, bytes_accessed=nbytes, transcendentals=0)


def dot_pixels(cols, rows):
    return lax.dot_general(cols, rows, (((0,), (0,)), ((), ())), preferred_element_type=F32)


def gram_t(col_real, col_imag, row_real, row_imag, row_imag_neg):
    real = dot_pixels(col_real, row_real) + dot_pixels(col_imag, row_imag)
    imag = dot_pixels(col_imag, row_real) + dot_pixels(col_real, row_imag_neg)
    return real, imag


def fields_kernel(frames_ref, fields_ref):
    fields_ref[0] = (frames_ref[0].astype(F32) - frames_ref[2].astype(F32)).astype(BF16)
    fields_ref[1] = (frames_ref[3].astype(F32) - frames_ref[1].astype(F32)).astype(BF16)


def early_kernel(base_ref, fields_ref, pixels_ref, out_ref):
    dests, slot_rows, width = out_ref.shape
    diag_cols = width // dests
    real, imag = fields_ref[0], fields_ref[1]
    positions = base_ref[0] + lax.broadcasted_iota(jnp.int32, (pixels_ref.shape[0], real.shape[0]), 1)
    counts = jnp.sum((pixels_ref[...] == positions).astype(F32), axis=0, keepdims=True)
    counts = jnp.broadcast_to(counts, (8, real.shape[0])).astype(BF16)
    ref_real = jnp.dot(counts, real, preferred_element_type=F32)
    ref_imag = jnp.dot(counts, imag, preferred_element_type=F32)
    row = lax.broadcasted_iota(jnp.int32, ref_real.shape, 0)
    high_real = ref_real.astype(BF16).astype(F32)
    high_imag = ref_imag.astype(BF16).astype(F32)
    refs = jnp.where(row == 0, high_real, ref_real - high_real)
    refs = jnp.where(row == 2, high_imag, refs)
    refs = jnp.where(row == 3, ref_imag - high_imag, refs)
    refs = jnp.where(row > 3, 0.0, refs)
    diag_real, diag_imag = gram_t(real, imag, real, imag, -imag)
    rows = jnp.concatenate(
        [diag_real, diag_imag, refs, jnp.zeros((128 - refs.shape[0], width), F32)], axis=0
    ).astype(BF16)
    slot_at = lax.broadcasted_iota(jnp.int32, (dests * slot_rows, rows.shape[0]), 0)
    source = lax.broadcasted_iota(jnp.int32, (dests * slot_rows, rows.shape[0]), 1)
    dest, slot = slot_at // slot_rows, slot_at % slot_rows
    diag_source = (slot // diag_cols) * width + dest * diag_cols + slot % diag_cols
    wanted = jnp.where(slot < 2 * diag_cols, diag_source, 2 * width + slot - 2 * diag_cols)
    pick = jnp.where(wanted == source, 1.0, 0.0).astype(BF16)
    placed = jnp.dot(pick, rows, preferred_element_type=F32)
    out_ref[...] = placed.reshape(dests, slot_rows, width).astype(BF16)


def band_kernel(own_ref, one_ref, two_ref, three_ref, four_ref, out_ref):
    row_real, row_imag = own_ref[0], own_ref[1]
    row_imag_neg = -row_imag
    width = row_real.shape[1]
    part_cols = out_ref.shape[1] // 2
    tile_dests = width // part_cols
    for at, block in enumerate((one_ref, two_ref, three_ref, four_ref)):
        real, imag = gram_t(block[0], block[1], row_real, row_imag, row_imag_neg)
        dests = pl.ds(at * tile_dests, tile_dests)
        out_ref[dests, :part_cols, :] = real.reshape(tile_dests, part_cols, width).astype(BF16)
        out_ref[dests, part_cols:, :] = imag.reshape(tile_dests, part_cols, width).astype(BF16)


def unit_phase(real, imag):
    magnitude = jnp.maximum(jnp.sqrt(real * real + imag * imag), 1.0)
    return real / magnitude, imag / magnitude


def pick_lanes(values, start, count):
    lanes = values.shape[1]
    lane = lax.broadcasted_iota(jnp.int32, (count, lanes), 1)
    row = lax.broadcasted_iota(jnp.int32, (count, lanes), 0)
    return jnp.sum(jnp.where(lane == start + row, values, 0.0), axis=1, keepdims=True)


def rotate(real, imag, row_phase, col_phase, pixel_scale):
    unit_real = row_phase[0] * col_phase[0] + row_phase[1] * col_phase[1]
    unit_imag = row_phase[1] * col_phase[0] - row_phase[0] * col_phase[1]
    return (
        (unit_real * real - unit_imag * imag) * pixel_scale,
        (unit_real * imag + unit_imag * real) * pixel_scale,
    )


def final_kernel(pixel_scale, starts_ref, early_ref, own_ref, other_ref, band_ref, band_out, diag_out):
    part_cols, diag_cols = band_out.shape[1], diag_out.shape[1]
    band = jnp.sum(band_ref[...].astype(F32), axis=0)
    diag = jnp.sum(early_ref[...].astype(F32), axis=0)[: 2 * diag_cols]
    row_phase = unit_phase(own_ref[0:1, :], own_ref[1:2, :])
    other_phase = unit_phase(other_ref[0:1, :], other_ref[1:2, :])
    col_phase = [pick_lanes(part, starts_ref[0], part_cols) for part in other_phase]
    band_out[0], band_out[1] = rotate(band[:part_cols], band[part_cols:], row_phase, col_phase, pixel_scale)
    diag_phase = [pick_lanes(part, starts_ref[1], diag_cols) for part in row_phase]
    diag_out[0], diag_out[1] = rotate(diag[:diag_cols], diag[diag_cols:], row_phase, diag_phase, pixel_scale)


def shards(frames, ref_pixels):
    pix_count = lax.axis_size("pix")
    mode_count = lax.axis_size("mode")
    pix_index = lax.axis_index("pix")
    mode_index = lax.axis_index("mode")
    pixel_rows, width = frames.shape[1:]
    tiles = mode_count // 2
    tile_dests = pix_count // tiles
    part_cols = width // tile_dests
    diag_cols = width // pix_count
    slot_rows = 2 * diag_cols + REF_ROWS
    field_bytes = 2 * pixel_rows * width * 2
    tile_flops = 8 * pixel_rows * width * width

    def shift(array, step):
        pairs = [((m + step) % mode_count, m) for m in range(mode_count)]
        return lax.ppermute(array, "mode", pairs)

    def swap(array):
        return lax.ppermute(array, "mode", [(m ^ 1, m) for m in range(mode_count)])

    fields = pl.pallas_call(
        fields_kernel,
        out_shape=jax.ShapeDtypeStruct((2, pixel_rows, width), BF16),
        in_specs=[VMEM],
        out_specs=VMEM,
        cost_estimate=cost(4 * pixel_rows * width, 3 * field_bytes),
    )(frames)
    two = shift(fields, 2)
    four = shift(fields, 4)

    early = pl.pallas_call(
        early_kernel,
        out_shape=jax.ShapeDtypeStruct((pix_count, slot_rows, width), BF16),
        in_specs=[SMEM, VMEM, VMEM],
        out_specs=VMEM,
        cost_estimate=cost(4 * tile_flops, 2 * field_bytes),
        compiler_params=pltpu.CompilerParams(vmem_limit_bytes=32 << 20),
    )((pix_index * pixel_rows).reshape(1), fields, ref_pixels[:, None])
    early = lax.all_to_all(early, "pix", 0, 0, tiled=True)
    ref_terms = jnp.sum(early[:, 2 * diag_cols : 2 * diag_cols + 4, :].astype(F32), axis=0)
    own_ref = ref_terms.reshape(2, 2, width).sum(axis=1)
    pairs = []
    for p in range(pix_count):
        step = p // tile_dests + 1
        for m in range(mode_count):
            pairs.append((p * mode_count + (m + step) % mode_count, p * mode_count + m))
    other_ref = lax.ppermute(own_ref, ("pix", "mode"), pairs)

    first_core = mode_index % 2 == 0
    one = swap(jnp.where(first_core, two, fields))
    three = swap(jnp.where(first_core, four, two))
    band = pl.pallas_call(
        band_kernel,
        out_shape=jax.ShapeDtypeStruct((pix_count, 2 * part_cols, width), BF16),
        in_specs=[VMEM] * 5,
        out_specs=VMEM,
        cost_estimate=cost(tiles * tile_flops, 8 * field_bytes),
        compiler_params=pltpu.CompilerParams(vmem_limit_bytes=32 << 20),
    )(fields, one, two, three, four)
    band = lax.all_to_all(band, "pix", 0, 0, tiled=True)

    starts = jnp.stack([(pix_index % tile_dests) * part_cols, pix_index * diag_cols])
    scale = 1.0 / math.sqrt(pix_count * pixel_rows)
    band_out, diag_out = pl.pallas_call(
        lambda *refs: final_kernel(scale, *refs),
        out_shape=(
            jax.ShapeDtypeStruct((2, part_cols, width), F32),
            jax.ShapeDtypeStruct((2, diag_cols, width), F32),
        ),
        in_specs=[SMEM] + [VMEM] * 4,
        out_specs=(VMEM, VMEM),
        cost_estimate=cost(4 * field_bytes, 6 * field_bytes),
        compiler_params=pltpu.CompilerParams(vmem_limit_bytes=32 << 20),
    )(starts, early, own_ref, other_ref, band)
    return jnp.transpose(band_out, (0, 2, 1)), jnp.transpose(diag_out, (0, 2, 1))


def solution(mesh):
    return jax.shard_map(
        shards,
        mesh=mesh,
        in_specs=(P(None, "pix", "mode"), P()),
        out_specs=(P(None, "mode", "pix"), P(None, "mode", "pix")),
        check_vma=False,
    )
```

time: 360 us -> 87.9 us (0.24)
  blocking collectives: 161 us -> 0 us
  waiting for transfers between devices: 154 us -> 40.4 us
  starting transfers between devices: 0.08 us -> 36.5 us
  local copies, waits for them, and re-layouts: 22.4 us -> 1.81 us
  between operations: 15.5 us -> 0.74 us
  Pallas kernels: 0 us -> 7.73 us
  matrix products: 4.9 us -> 0 us
    unnamed x3 -> x0, waiting for transfers between devices: 154 us -> none
    psum x1 -> x0, blocking collectives: 150 us -> none  [shards(): own_ref = lax.psum(local_ref, 'pix')]
    all_to_all x0 -> x2, waiting for transfers between devices: none -> 35.7 us  [the longest x1 26.9 us: shards(): band = lax.all_to_all(band, 'pix', 0, 0, tiled=True)]
    all_to_all x0 -> x2, starting transfers between devices: none -> 19.1 us  [the longest x1 11.3 us: shards(): early = lax.all_to_all(early, 'pix', 0, 0, tiled=True)]
    ppermute x0 -> x5, starting transfers between devices: none -> 17.4 us  [the longest x2 11.1 us: shift(): return lax.ppermute(array, 'mode', pairs)]
    all_gather x1 -> x0, blocking collectives: 11 us -> none  [shards(): phase_all = lax.all_gather(unit_phase(own_ref), 'mode', axis=1, tiled=True)]
    pallas_call x0 -> x4, Pallas kernels: none -> 7.73 us  [the longest x1 2.26 us: shards(): pl.pallas_call(band_kernel, out_shape=jax.ShapeDtypeStruct((pix_count, 2...]
    slice x7 -> x0, local copies, waits for them, and re-layouts: 7.1 us -> none  [the longest x1 2.37 us: shards(): rotated_terms[:, :, block_width:]]
  transfers between devices with their start and end apart: 2 -> 7, of which waited for: 1 -> 5; matrix products, arithmetic and copies ran while one was open for 1% -> 0% of each run, Pallas kernels for 0% -> 5%
where the time goes in v1:
time: 87.9 us; the launch traced here: 87.4 us
  waiting for transfers between devices  40.4 us (46%)
  starting transfers between devices  36.5 us (42%)
  Pallas kernels  7.73 us (9%)
  local copies, waits for them, and re-layouts  1.81 us (2%)
    all_to_all x1, waiting for transfers between devices, shards(): band = lax.all_to_all(band, 'pix', 0, 0, tiled=True)  26.9 us
    all_to_all x1, starting transfers between devices, shards(): early = lax.all_to_all(early, 'pix', 0, 0, tiled=True)  11.3 us
    ppermute x2, starting transfers between devices, shift(): return lax.ppermute(array, 'mode', pairs)  11.1 us
    all_to_all x1, waiting for transfers between devices, shards(): early = lax.all_to_all(early, 'pix', 0, 0, tiled=True)  8.85 us
    all_to_all x1, starting transfers between devices, shards(): band = lax.all_to_all(band, 'pix', 0, 0, tiled=True)  7.76 us
    ppermute x2, starting transfers between devices, swap(): return lax.ppermute(array, 'mode', [(m ^ 1, m) for m in range(mode_count)])  4.33 us
    pallas_call x1, Pallas kernels, shards(): pl.pallas_call(band_kernel, out_shape=jax.ShapeDtypeStruct((pix_count, 2...  2.26 us
    pallas_call x1, Pallas kernels, shards(): pl.pallas_call(fields_kernel, out_shape=jax.ShapeDtypeStruct((2, pixel_ro...  2.15 us
  transfers between devices with their start and end apart: 7, of which 5 were waited for; matrix products, arithmetic and copies ran while one was open for 0% of the time, Pallas kernels for 5%

profile of v1, /device:TPU:6, one launch (start us, length us, event | category | flops | bytes accessed | tf_op | source)
XLA Modules:
  0.0 87.4 jit_solution(817659546291319312)
XLA Ops:
  0.6 2.1 %shard_map.41.fields_ref.own_ref = bf16[2,512,256]{2,1,0:T(8,128)(2,1)} custom-call(bf16[4,512,256]{2,1,0:T(8,128)(2,1)} %frames_ref.1), custom_call_target="tpu_custom_call" | custom-call | flops 524288 | bytes 1572864 | tf_op jit(solution)/shard_map/pallas_call | solution.py:133
  2.8 2.7 %collective-permute-start.1 = (bf16[2,512,256]{2,1,0:T(8,128)(2,1)}, bf16[2,512,256]{2,1,0:T(8,128)(2,1)S(1)}, u32[]{:S(2)}, u32[]{:S(2)}) collective-permute-start(bf16[2,512,256]{2,1,0:T(8,128)(2,1)} %shard_map.41.fields_ref.own_ref), channel_id=1, source_target_pairs={{2,0},{3,1},{4,2},{5,3},{6,4},{7,5},{0,6},{1,7},{10,8},{11,9},{12,... | collective-permute-start | bytes 1572872 | tf_op jit(solution)/shard_map/ppermute | solution.py:128
  5.5 8.4 %collective-permute-start.3 = (bf16[2,512,256]{2,1,0:T(8,128)(2,1)}, bf16[2,512,256]{2,1,0:T(8,128)(2,1)S(1)}, u32[]{:S(2)}, u32[]{:S(2)}) collective-permute-start(bf16[2,512,256]{2,1,0:T(8,128)(2,1)} %shard_map.41.fields_ref.own_ref), channel_id=1, source_target_pairs={{4,0},{5,1},{6,2},{7,3},{0,4},{1,5},{2,6},{3,7},{12,8},{13,9},{14,... | collective-permute-start | bytes 1572872 | tf_op jit(solution)/shard_map/ppermute | solution.py:128
  13.9 0.0 copy-start.2
  13.9 0.6 copy-done.2
  14.6 0.1 copy.5.pixels_ref
  14.7 0.0 copy-start
  14.7 1.0 %copy-done = bf16[2,512,256]{2,1,0:T(8,128)(2,1)S(1)} copy-done((bf16[2,512,256]{2,1,0:T(8,128)(2,1)S(1)}, bf16[2,512,256]{2,1,0:T(8,128)(2,1)}, u32[]{:S(2)}) %copy-start) | copy-done | bytes 524312
  15.7 1.9 %shard_map.42 = bf16[64,16,256]{2,1,0:T(8,128)(2,1)} custom-call(s32[1]{0:T(128)} %bitcast.2.base_ref, bf16[2,512,256]{2,1,0:T(8,128)(2,1)S(1)} %copy-done, s32[64,1]{1,0:T(8,128)S(1)} %copy.5.pixels_ref), custom_call_target="tpu_custom_call" | custom-call | flops 1073741824 | bytes 1048576 | tf_op jit(solution)/shard_map/pallas_call | solution.py:143
  17.6 0.0 copy-start.1
  17.6 11.3 %all-to-all-start = ((bf16[64,16,256]{2,1,0:T(8,128)(2,1)}), bf16[64,16,256]{2,1,0:T(8,128)(2,1)S(1)}, u32[]{:S(2)}, u32[]{:S(2)}) async-start(bf16[64,16,256]{2,1,0:T(8,128)(2,1)} %shard_map.42), calls=%async_computation | async-start | bytes 1048576 | tf_op jit(solution)/shard_map/all_to_all | solution.py:151
  29.0 2.0 %collective-permute-done.1.two_ref = bf16[2,512,256]{2,1,0:T(8,128)(2,1)S(1)} collective-permute-done((bf16[2,512,256]{2,1,0:T(8,128)(2,1)}, bf16[2,512,256]{2,1,0:T(8,128)(2,1)S(1)}, u32[]{:S(2)}, u32[]{:S(2)}) %collective-permute-start.1) | collective-permute-done | bytes 524320 | tf_op jit(solution)/shard_map/ppermute | solution.py:128
  31.0 0.0 collective-permute-done.3.four_ref
  31.0 0.0 copy-done.1
  31.0 0.1 broadcast_select_fusion
  31.1 1.9 %collective-permute-start.2 = (bf16[2,512,256]{2,1,0:T(8,128)(2,1)S(1)}, bf16[2,512,256]{2,1,0:T(8,128)(2,1)S(1)}, u32[]{:S(2)}, u32[]{:S(2)}) collective-permute-start(bf16[2,512,256]{2,1,0:T(8,128)(2,1)S(1)} %get-tuple-element.7), channel_id=1, source_target_pairs={{1,0},{0,1},{3,2},{2,3},{5,4},{4,5},{7,6},{6,7},{9,8},{8,9},{11,10... | collective-permute-start | bytes 1572872 | tf_op jit(solution)/shard_map/ppermute | solution.py:131
  33.0 2.4 %collective-permute-start.4 = (bf16[2,512,256]{2,1,0:T(8,128)(2,1)S(1)}, bf16[2,512,256]{2,1,0:T(8,128)(2,1)S(1)}, u32[]{:S(2)}, u32[]{:S(2)}) collective-permute-start(bf16[2,512,256]{2,1,0:T(8,128)(2,1)S(1)} %get-tuple-element.6), channel_id=1, source_target_pairs={{1,0},{0,1},{3,2},{2,3},{5,4},{4,5},{7,6},{6,7},{9,8},{8,9},{11,10... | collective-permute-start | bytes 1572872 | tf_op jit(solution)/shard_map/ppermute | solution.py:131
  35.4 0.0 collective-permute-done.2.one_ref
  35.4 1.5 %collective-permute-done.4.three_ref = bf16[2,512,256]{2,1,0:T(8,128)(2,1)S(1)} collective-permute-done((bf16[2,512,256]{2,1,0:T(8,128)(2,1)S(1)}, bf16[2,512,256]{2,1,0:T(8,128)(2,1)S(1)}, u32[]{:S(2)}, u32[]{:S(2)}) %collective-permute-start.4) | collective-permute-done | bytes 524320 | tf_op jit(solution)/shard_map/ppermute | solution.py:131
  36.9 2.3 %shard_map.43 = bf16[64,32,256]{2,1,0:T(8,128)(2,1)} custom-call(bf16[2,512,256]{2,1,0:T(8,128)(2,1)S(1)} %copy-done.1, bf16[2,512,256]{2,1,0:T(8,128)(2,1)S(1)} %collective-permute-done.2.one_ref, bf16[2,512,256]{2,1,0:T(8,128)(2,1)S(1)} %collective-permute-done.1.two_ref, bf16[2,512,256]{2,1,0:T(8,128)(2,1)S(1)} %collective-permute-done.4.three_ref, ...), custom_call_target="tpu_custom_call" | custom-call | flops 1073741824 | bytes 4194304 | tf_op jit(solution)/shard_map/pallas_call | solution.py:164
  39.2 8.8 %all-to-all-done.refs_1_ = bf16[64,16,256]{2,1,0:T(8,128)(2,1)S(1)} async-done(((bf16[64,16,256]{2,1,0:T(8,128)(2,1)}), bf16[64,16,256]{2,1,0:T(8,128)(2,1)S(1)}, u32[]{:S(2)}, u32[]{:S(2)}) %all-to-all-start) | async-done | bytes 524320 | tf_op jit(solution)/shard_map/all_to_all | solution.py:151
  48.0 7.8 %all-to-all-start.1 = ((bf16[64,32,256]{2,1,0:T(8,128)(2,1)}), bf16[64,32,256]{2,1,0:T(8,128)(2,1)S(1)}, u32[]{:S(2)}, u32[]{:S(2)}) async-start(bf16[64,32,256]{2,1,0:T(8,128)(2,1)} %shard_map.43), calls=%async_computation.1 | async-start | bytes 2097152 | tf_op jit(solution)/shard_map/all_to_all | solution.py:172
  55.8 0.1 convert_reduce_fusion
  56.0 1.9 %collective-permute-start = (f32[2,256]{1,0:T(2,128)S(1)}, f32[2,256]{1,0:T(2,128)S(1)}, u32[]{:S(2)}, u32[]{:S(2)}) collective-permute-start(f32[2,256]{1,0:T(2,128)S(1)} %reduce_sum.19.refs_2_), channel_id=1, source_target_pairs={{1,0},{2,1},{3,2},{4,3},{5,4},{6,5},{7,6},{0,7},{9,8},{10,9},{11,1... | collective-permute-start | bytes 6152 | tf_op jit(solution)/shard_map/ppermute | solution.py:159
  57.9 0.1 pad_add_fusion.refs_0_
  58.0 1.2 %collective-permute-done.refs_3_ = f32[2,256]{1,0:T(2,128)S(1)} collective-permute-done((f32[2,256]{1,0:T(2,128)S(1)}, f32[2,256]{1,0:T(2,128)S(1)}, u32[]{:S(2)}, u32[]{:S(2)}) %collective-permute-start) | collective-permute-done | bytes 2080 | tf_op jit(solution)/shard_map/ppermute | solution.py:159
  59.2 26.9 %all-to-all-done.1.refs_4_ = bf16[64,32,256]{2,1,0:T(8,128)(2,1)S(1)} async-done(((bf16[64,32,256]{2,1,0:T(8,128)(2,1)}), bf16[64,32,256]{2,1,0:T(8,128)(2,1)S(1)}, u32[]{:S(2)}, u32[]{:S(2)}) %all-to-all-start.1) | async-done | bytes 1048608 | tf_op jit(solution)/shard_map/all_to_all | solution.py:172
  86.0 1.4 %shard_map.44 = (f32[2,16,256]{2,1,0:T(8,128)}, f32[2,4,256]{2,1,0:T(4,128)}) custom-call(s32[2]{0:T(128)S(1)} %pad_add_fusion.refs_0_, bf16[64,16,256]{2,1,0:T(8,128)(2,1)S(1)} %all-to-all-done.refs_1_, f32[2,256]{1,0:T(2,128)S(1)} %reduce_sum.19.refs_2_, f32[2,256]{1,0:T(2,128)S(1)} %collective-permute-done.refs_3_, ...), custom_call_target="tpu_custom_call" | custom-call | flops 2097152 | bytes 3145728 | tf_op jit(solution)/shard_map/pallas_call | solution.py:176
  (2 shorter events, 0.0 us)
Async XLA Ops:
  2.8 28.2 %collective-permute-start.1 = (bf16[2,512,256]{2,1,0:T(8,128)(2,1)}, bf16[2,512,256]{2,1,0:T(8,128)(2,1)S(1)}, u32[]{:S(2)}, u32[]{:S(2)}) collective-permute-start(bf16[2,512,256]{2,1,0:T(8,128)(2,1)} %shard_map.41.fields_ref.own_ref), channel_id=1, source_target_pairs={{2,0},{3,1},{4,2},{5,3},{6,4},{7,5},{0,6},{1,7},{10,8},{11,9},{12,... | collective-permute-start | bytes 1572872 | tf_op jit(solution)/shard_map/ppermute | solution.py:128
  5.5 25.5 %collective-permute-start.3 = (bf16[2,512,256]{2,1,0:T(8,128)(2,1)}, bf16[2,512,256]{2,1,0:T(8,128)(2,1)S(1)}, u32[]{:S(2)}, u32[]{:S(2)}) collective-permute-start(bf16[2,512,256]{2,1,0:T(8,128)(2,1)} %shard_map.41.fields_ref.own_ref), channel_id=1, source_target_pairs={{4,0},{5,1},{6,2},{7,3},{0,4},{1,5},{2,6},{3,7},{12,8},{13,9},{14,... | collective-permute-start | bytes 1572872 | tf_op jit(solution)/shard_map/ppermute | solution.py:128
  13.9 0.7 copy-start.2
  14.7 1.0 %copy-start = (bf16[2,512,256]{2,1,0:T(8,128)(2,1)S(1)}, bf16[2,512,256]{2,1,0:T(8,128)(2,1)}, u32[]{:S(2)}) copy-start(bf16[2,512,256]{2,1,0:T(8,128)(2,1)} %shard_map.41.fields_ref.own_ref) | copy-start | bytes 1572868
  17.6 13.3 %copy-start.1 = (bf16[2,512,256]{2,1,0:T(8,128)(2,1)S(1)}, bf16[2,512,256]{2,1,0:T(8,128)(2,1)}, u32[]{:S(2)}) copy-start(bf16[2,512,256]{2,1,0:T(8,128)(2,1)} %shard_map.41.fields_ref.own_ref) | copy-start | bytes 1572868
  17.6 30.4 %all-to-all-start = ((bf16[64,16,256]{2,1,0:T(8,128)(2,1)}), bf16[64,16,256]{2,1,0:T(8,128)(2,1)S(1)}, u32[]{:S(2)}, u32[]{:S(2)}) async-start(bf16[64,16,256]{2,1,0:T(8,128)(2,1)} %shard_map.42), calls=%async_computation | async-start | bytes 1048576 | tf_op jit(solution)/shard_map/all_to_all | solution.py:151
  31.1 4.3 %collective-permute-start.2 = (bf16[2,512,256]{2,1,0:T(8,128)(2,1)S(1)}, bf16[2,512,256]{2,1,0:T(8,128)(2,1)S(1)}, u32[]{:S(2)}, u32[]{:S(2)}) collective-permute-start(bf16[2,512,256]{2,1,0:T(8,128)(2,1)S(1)} %get-tuple-element.7), channel_id=1, source_target_pairs={{1,0},{0,1},{3,2},{2,3},{5,4},{4,5},{7,6},{6,7},{9,8},{8,9},{11,10... | collective-permute-start | bytes 1572872 | tf_op jit(solution)/shard_map/ppermute | solution.py:131
  33.0 3.9 %collective-permute-start.4 = (bf16[2,512,256]{2,1,0:T(8,128)(2,1)S(1)}, bf16[2,512,256]{2,1,0:T(8,128)(2,1)S(1)}, u32[]{:S(2)}, u32[]{:S(2)}) collective-permute-start(bf16[2,512,256]{2,1,0:T(8,128)(2,1)S(1)} %get-tuple-element.6), channel_id=1, source_target_pairs={{1,0},{0,1},{3,2},{2,3},{5,4},{4,5},{7,6},{6,7},{9,8},{8,9},{11,10... | collective-permute-start | bytes 1572872 | tf_op jit(solution)/shard_map/ppermute | solution.py:131
  48.0 38.0 %all-to-all-start.1 = ((bf16[64,32,256]{2,1,0:T(8,128)(2,1)}), bf16[64,32,256]{2,1,0:T(8,128)(2,1)S(1)}, u32[]{:S(2)}, u32[]{:S(2)}) async-start(bf16[64,32,256]{2,1,0:T(8,128)(2,1)} %shard_map.43), calls=%async_computation.1 | async-start | bytes 2097152 | tf_op jit(solution)/shard_map/all_to_all | solution.py:172
  56.0 3.2 %collective-permute-start = (f32[2,256]{1,0:T(2,128)S(1)}, f32[2,256]{1,0:T(2,128)S(1)}, u32[]{:S(2)}, u32[]{:S(2)}) collective-permute-start(f32[2,256]{1,0:T(2,128)S(1)} %reduce_sum.19.refs_2_), channel_id=1, source_target_pairs={{1,0},{2,1},{3,2},{4,3},{5,4},{6,5},{7,6},{0,7},{9,8},{10,9},{11,1... | collective-permute-start | bytes 6152 | tf_op jit(solution)/shard_map/ppermute | solution.py:159

commit v2 on v1

--- a/solution.py
+++ b/solution.py
@@ -33,22 +33,32 @@
     fields_ref[1] = (frames_ref[3].astype(F32) - frames_ref[1].astype(F32)).astype(BF16)
 
 
-def early_kernel(base_ref, fields_ref, pixels_ref, out_ref):
+def split_terms(real, imag):
+    row = lax.broadcasted_iota(jnp.int32, real.shape, 0)
+    high_real = real.astype(BF16).astype(F32)
+    high_imag = imag.astype(BF16).astype(F32)
+    terms = jnp.where(row == 0, high_real, real - high_real)
+    terms = jnp.where(row == 2, high_imag, terms)
+    terms = jnp.where(row == 3, imag - high_imag, terms)
+    return jnp.where(row > 3, 0.0, terms)
+
+
+def ref_terms(counts, real, imag):
+    return split_terms(
+        jnp.dot(counts, real, preferred_element_type=F32),
+        jnp.dot(counts, imag, preferred_element_type=F32),
+    )
+
+
+def early_kernel(base_ref, fields_ref, pixels_ref, out_ref, counts_ref):
     dests, slot_rows, width = out_ref.shape
     diag_cols = width // dests
     real, imag = fields_ref[0], fields_ref[1]
     positions = base_ref[0] + lax.broadcasted_iota(jnp.int32, (pixels_ref.shape[0], real.shape[0]), 1)
     counts = jnp.sum((pixels_ref[...] == positions).astype(F32), axis=0, keepdims=True)
-    counts = jnp.broadcast_to(counts, (8, real.shape[0])).astype(BF16)
-    ref_real = jnp.dot(counts, real, preferred_element_type=F32)
-    ref_imag = jnp.dot(counts, imag, preferred_element_type=F32)
-    row = lax.broadcasted_iota(jnp.int32, ref_real.shape, 0)
-    high_real = ref_real.astype(BF16).astype(F32)
-    high_imag = ref_imag.astype(BF16).astype(F32)
-    refs = jnp.where(row == 0, high_real, ref_real - high_real)
-    refs = jnp.where(row == 2, high_imag, refs)
-    refs = jnp.where(row == 3, ref_imag - high_imag, refs)
-    refs = jnp.where(row > 3, 0.0, refs)
+    counts = jnp.broadcast_to(counts, counts_ref.shape).astype(BF16)
+    counts_ref[...] = counts
+    refs = ref_terms(counts, real, imag)
     diag_real, diag_imag = gram_t(real, imag, real, imag, -imag)
     rows = jnp.concatenate(
         [diag_real, diag_imag, refs, jnp.zeros((128 - refs.shape[0], width), F32)], axis=0
@@ -63,17 +73,33 @@
     out_ref[...] = placed.reshape(dests, slot_rows, width).astype(BF16)
 
 
-def band_kernel(own_ref, one_ref, two_ref, three_ref, four_ref, out_ref):
+def band_kernel(core_ref, own_ref, own_swap_ref, two_ref, two_swap_ref, four_ref, four_swap_ref, early_ref, counts_ref, out_ref):
     row_real, row_imag = own_ref[0], own_ref[1]
     row_imag_neg = -row_imag
     width = row_real.shape[1]
-    part_cols = out_ref.shape[1] // 2
+    slot_rows = early_ref.shape[1]
+    part_cols = (out_ref.shape[1] - slot_rows) // 2
     tile_dests = width // part_cols
-    for at, block in enumerate((one_ref, two_ref, three_ref, four_ref)):
-        real, imag = gram_t(block[0], block[1], row_real, row_imag, row_imag_neg)
+    first_core = core_ref[0] == 0
+    counts = counts_ref[...]
+
+    def tile(at, real, imag):
+        gram_real, gram_imag = gram_t(real, imag, row_real, row_imag, row_imag_neg)
+        refs = ref_terms(counts, real, imag)
         dests = pl.ds(at * tile_dests, tile_dests)
-        out_ref[dests, :part_cols, :] = real.reshape(tile_dests, part_cols, width).astype(BF16)
-        out_ref[dests, part_cols:, :] = imag.reshape(tile_dests, part_cols, width).astype(BF16)
+        out_ref[dests, :part_cols, :] = gram_real.reshape(tile_dests, part_cols, width).astype(BF16)
+        out_ref[dests, part_cols : 2 * part_cols, :] = gram_imag.reshape(tile_dests, part_cols, width).astype(BF16)
+        lower = jnp.concatenate([jnp.zeros_like(refs), pltpu.roll(refs, 4, 0)], axis=0)
+        early = early_ref[dests].astype(F32) + lower[None]
+        out_ref[dests, 2 * part_cols :, :] = early.astype(BF16)
+
+    def pick(a_ref, b_ref, part):
+        return jnp.where(first_core, a_ref[part], b_ref[part])
+
+    tile(0, pick(own_swap_ref, two_swap_ref, 0), pick(own_swap_ref, two_swap_ref, 1))
+    tile(1, two_ref[0], two_ref[1])
+    tile(2, pick(two_swap_ref, four_swap_ref, 0), pick(two_swap_ref, four_swap_ref, 1))
+    tile(3, four_ref[0], four_ref[1])
 
 
 def unit_phase(real, imag):
@@ -97,12 +123,13 @@
     )
 
 
-def final_kernel(pixel_scale, starts_ref, early_ref, own_ref, other_ref, band_ref, band_out, diag_out):
+def final_kernel(pixel_scale, starts_ref, parts_ref, band_out, diag_out):
     part_cols, diag_cols = band_out.shape[1], diag_out.shape[1]
-    band = jnp.sum(band_ref[...].astype(F32), axis=0)
-    diag = jnp.sum(early_ref[...].astype(F32), axis=0)[: 2 * diag_cols]
-    row_phase = unit_phase(own_ref[0:1, :], own_ref[1:2, :])
-    other_phase = unit_phase(other_ref[0:1, :], other_ref[1:2, :])
+    sums = jnp.sum(parts_ref[...].astype(F32), axis=0)
+    band, rest = sums[: 2 * part_cols], sums[2 * part_cols :]
+    diag, refs = rest[: 2 * diag_cols], rest[2 * diag_cols :]
+    row_phase = unit_phase(refs[0:1] + refs[1:2], refs[2:3] + refs[3:4])
+    other_phase = unit_phase(refs[4:5] + refs[5:6], refs[6:7] + refs[7:8])
     col_phase = [pick_lanes(part, starts_ref[0], part_cols) for part in other_phase]
     band_out[0], band_out[1] = rotate(band[:part_cols], band[part_cols:], row_phase, col_phase, pixel_scale)
     diag_phase = [pick_lanes(part, starts_ref[1], diag_cols) for part in row_phase]
@@ -127,8 +154,9 @@
         pairs = [((m + step) % mode_count, m) for m in range(mode_count)]
         return lax.ppermute(array, "mode", pairs)
 
-    def swap(array):
-        return lax.ppermute(array, "mode", [(m ^ 1, m) for m in range(mode_count)])
+    def swap(array, even=False, odd=False):
+        pairs = [(m, m ^ 1) for m in range(mode_count) if (odd if m % 2 else even)]
+        return lax.ppermute(array, "mode", pairs)
 
     fields = pl.pallas_call(
         fields_kernel,
@@ -137,39 +165,35 @@
         out_specs=VMEM,
         cost_estimate=cost(4 * pixel_rows * width, 3 * field_bytes),
     )(frames)
+    four = shift(fields, 4)
     two = shift(fields, 2)
-    four = shift(fields, 4)
-
-    early = pl.pallas_call(
+    own_swap = swap(fields, odd=True)
+
+    early, counts = pl.pallas_call(
         early_kernel,
-        out_shape=jax.ShapeDtypeStruct((pix_count, slot_rows, width), BF16),
+        out_shape=(
+            jax.ShapeDtypeStruct((pix_count, slot_rows, width), BF16),
+            jax.ShapeDtypeStruct((8, pixel_rows), BF16),
+        ),
         in_specs=[SMEM, VMEM, VMEM],
-        out_specs=VMEM,
+        out_specs=(VMEM, VMEM),
         cost_estimate=cost(4 * tile_flops, 2 * field_bytes),
         compiler_params=pltpu.CompilerParams(vmem_limit_bytes=32 << 20),
     )((pix_index * pixel_rows).reshape(1), fields, ref_pixels[:, None])
-    early = lax.all_to_all(early, "pix", 0, 0, tiled=True)
-    ref_terms = jnp.sum(early[:, 2 * diag_cols : 2 * diag_cols + 4, :].astype(F32), axis=0)
-    own_ref = ref_terms.reshape(2, 2, width).sum(axis=1)
-    pairs = []
-    for p in range(pix_count):
-        step = p // tile_dests + 1
-        for m in range(mode_count):
-            pairs.append((p * mode_count + (m + step) % mode_count, p * mode_count + m))
-    other_ref = lax.ppermute(own_ref, ("pix", "mode"), pairs)
-
-    first_core = mode_index % 2 == 0
-    one = swap(jnp.where(first_core, two, fields))
-    three = swap(jnp.where(first_core, four, two))
-    band = pl.pallas_call(
+
+    two, early = lax.optimization_barrier((two, early))
+    two_swap = swap(two, even=True, odd=True)
+    four, early = lax.optimization_barrier((four, early))
+    four_swap = swap(four, even=True)
+    parts = pl.pallas_call(
         band_kernel,
-        out_shape=jax.ShapeDtypeStruct((pix_count, 2 * part_cols, width), BF16),
-        in_specs=[VMEM] * 5,
+        out_shape=jax.ShapeDtypeStruct((pix_count, 2 * part_cols + slot_rows, width), BF16),
+        in_specs=[SMEM] + [VMEM] * 8,
         out_specs=VMEM,
         cost_estimate=cost(tiles * tile_flops, 8 * field_bytes),
         compiler_params=pltpu.CompilerParams(vmem_limit_bytes=32 << 20),
-    )(fields, one, two, three, four)
-    band = lax.all_to_all(band, "pix", 0, 0, tiled=True)
+    )((mode_index % 2).reshape(1), fields, own_swap, two, two_swap, four, four_swap, early, counts)
+    parts = lax.all_to_all(parts, "pix", 0, 0, tiled=True)
 
     starts = jnp.stack([(pix_index % tile_dests) * part_cols, pix_index * diag_cols])
     scale = 1.0 / math.sqrt(pix_count * pixel_rows)
@@ -179,11 +203,11 @@
             jax.ShapeDtypeStruct((2, part_cols, width), F32),
             jax.ShapeDtypeStruct((2, diag_cols, width), F32),
         ),
-        in_specs=[SMEM] + [VMEM] * 4,
+        in_specs=[SMEM, VMEM],
         out_specs=(VMEM, VMEM),
         cost_estimate=cost(4 * field_bytes, 6 * field_bytes),
         compiler_params=pltpu.CompilerParams(vmem_limit_bytes=32 << 20),
-    )(starts, early, own_ref, other_ref, band)
+    )(starts, parts)
     return jnp.transpose(band_out, (0, 2, 1)), jnp.transpose(diag_out, (0, 2, 1))
 
 

time: 87.9 us -> 100 us (1.14)
  waiting for transfers between devices: 40.4 us -> 57.1 us
  starting transfers between devices: 36.5 us -> 32.2 us
    ppermute x2, waiting for transfers between devices: 1.98 us -> 13.5 us  [shift(): return lax.ppermute(array, 'mode', pairs)]
    all_to_all x2 -> x1, waiting for transfers between devices: 35.7 us -> 41.6 us  [shards(): parts = lax.all_to_all(parts, 'pix', 0, 0, tiled=True)]
    all_to_all x2 -> x1, starting transfers between devices: 19.1 us -> 16.6 us  [shards(): parts = lax.all_to_all(parts, 'pix', 0, 0, tiled=True)]
    ppermute x3, starting transfers between devices: 6.24 us -> 4.53 us  [swap(): return lax.ppermute(array, 'mode', pairs)]
    pallas_call x1, Pallas kernels: 2.26 us -> 3.77 us  [shards(): pl.pallas_call(band_kernel, out_shape=jax.ShapeDtypeStruct((pix_count, 2...]
  transfers between devices with their start and end apart: 7 -> 6, of which waited for: 5 -> 3; matrix products, arithmetic and copies ran while one was open for 0% -> 0% of each run, Pallas kernels for 5% -> 1%
where the time goes in v2:
time: 100 us; the launch traced here: 99.8 us
  waiting for transfers between devices  57.1 us (57%)
  starting transfers between devices  32.2 us (32%)
  Pallas kernels  8.5 us (8%)
  local copies, waits for them, and re-layouts  1.15 us (1%)
    all_to_all x1, waiting for transfers between devices, shards(): parts = lax.all_to_all(parts, 'pix', 0, 0, tiled=True)  41.6 us
    all_to_all x1, starting transfers between devices, shards(): parts = lax.all_to_all(parts, 'pix', 0, 0, tiled=True)  16.6 us
    ppermute x2, waiting for transfers between devices, shift(): return lax.ppermute(array, 'mode', pairs)  13.5 us
    ppermute x2, starting transfers between devices, shift(): return lax.ppermute(array, 'mode', pairs)  11.1 us
    ppermute x3, starting transfers between devices, swap(): return lax.ppermute(array, 'mode', pairs)  4.53 us
    pallas_call x1, Pallas kernels, shards(): pl.pallas_call(band_kernel, out_shape=jax.ShapeDtypeStruct((pix_count, 2...  3.77 us
    pallas_call x1, Pallas kernels, shards(): pl.pallas_call(fields_kernel, out_shape=jax.ShapeDtypeStruct((2, pixel_ro...  2.14 us
  transfers between devices with their start and end apart: 6, of which 3 were waited for; matrix products, arithmetic and copies ran while one was open for 0% of the time, Pallas kernels for 1%

profile of v2, /device:TPU:6, one launch (start us, length us, event | category | flops | bytes accessed | tf_op | source)
XLA Modules:
  0.0 99.8 jit_solution(6827880124606536545)
XLA Ops:
  0.6 0.0 copy-start.2
  0.6 2.1 %shard_map.41.fields_ref.own_ref = bf16[2,512,256]{2,1,0:T(8,128)(2,1)} custom-call(bf16[4,512,256]{2,1,0:T(8,128)(2,1)} %frames_ref.1), custom_call_target="tpu_custom_call" | custom-call | flops 524288 | bytes 1572864 | tf_op jit(solution)/shard_map/pallas_call | solution.py:161
  2.8 2.7 %collective-permute-start.1 = (bf16[2,512,256]{2,1,0:T(8,128)(2,1)}, bf16[2,512,256]{2,1,0:T(8,128)(2,1)S(1)}, u32[]{:S(2)}, u32[]{:S(2)}) collective-permute-start(bf16[2,512,256]{2,1,0:T(8,128)(2,1)} %shard_map.41.fields_ref.own_ref), channel_id=1, source_target_pairs={{2,0},{3,1},{4,2},{5,3},{6,4},{7,5},{0,6},{1,7},{10,8},{11,9},{12,... | collective-permute-start | bytes 1572872 | tf_op jit(solution)/shard_map/ppermute | solution.py:155
  5.5 8.4 %collective-permute-start.3 = (bf16[2,512,256]{2,1,0:T(8,128)(2,1)}, bf16[2,512,256]{2,1,0:T(8,128)(2,1)S(1)}, u32[]{:S(2)}, u32[]{:S(2)}) collective-permute-start(bf16[2,512,256]{2,1,0:T(8,128)(2,1)} %shard_map.41.fields_ref.own_ref), channel_id=1, source_target_pairs={{4,0},{5,1},{6,2},{7,3},{0,4},{1,5},{2,6},{3,7},{12,8},{13,9},{14,... | collective-permute-start | bytes 1572872 | tf_op jit(solution)/shard_map/ppermute | solution.py:155
  13.9 1.3 %collective-permute-start = (bf16[2,512,256]{2,1,0:T(8,128)(2,1)}, bf16[2,512,256]{2,1,0:T(8,128)(2,1)S(1)}, u32[]{:S(2)}, u32[]{:S(2)}) collective-permute-start(bf16[2,512,256]{2,1,0:T(8,128)(2,1)} %shard_map.41.fields_ref.own_ref), channel_id=1, source_target_pairs={{1,0},{3,2},{5,4},{7,6},{9,8},{11,10},{13,12},{15,14},{17,16},{19,... | collective-permute-start | bytes 1572872 | tf_op jit(solution)/shard_map/ppermute | solution.py:159
  15.2 0.0 copy-done.2
  15.2 0.1 copy.4.pixels_ref
  15.3 0.0 copy-start
  15.3 1.0 %copy-done = bf16[2,512,256]{2,1,0:T(8,128)(2,1)S(1)} copy-done((bf16[2,512,256]{2,1,0:T(8,128)(2,1)S(1)}, bf16[2,512,256]{2,1,0:T(8,128)(2,1)}, u32[]{:S(2)}) %copy-start) | copy-done | bytes 524312
  16.4 0.0 copy-start.1
  16.4 1.1 %shard_map.42 = (bf16[64,16,256]{2,1,0:T(8,128)(2,1)S(1)}, bf16[8,512]{1,0:T(8,128)(2,1)S(1)}) custom-call(s32[1]{0:T(128)} %bitcast.3.base_ref, bf16[2,512,256]{2,1,0:T(8,128)(2,1)S(1)} %copy-done, s32[64,1]{1,0:T(8,128)S(1)} %copy.4.pixels_ref), custom_call_target="tpu_custom_call" | custom-call | flops 1073741824 | bytes 1048576 | tf_op jit(solution)/shard_map/pallas_call | solution.py:172
  17.5 13.5 %collective-permute-done.1.two_ref = bf16[2,512,256]{2,1,0:T(8,128)(2,1)S(1)} collective-permute-done((bf16[2,512,256]{2,1,0:T(8,128)(2,1)}, bf16[2,512,256]{2,1,0:T(8,128)(2,1)S(1)}, u32[]{:S(2)}, u32[]{:S(2)}) %collective-permute-start.1) | collective-permute-done | bytes 524320 | tf_op jit(solution)/shard_map/ppermute | solution.py:155
  31.0 0.0 collective-permute-done.3.four_ref
  31.0 1.3 %collective-permute-start.4 = (bf16[2,512,256]{2,1,0:T(8,128)(2,1)S(1)}, bf16[2,512,256]{2,1,0:T(8,128)(2,1)S(1)}, u32[]{:S(2)}, u32[]{:S(2)}) collective-permute-start(bf16[2,512,256]{2,1,0:T(8,128)(2,1)S(1)} %collective-permute-done.3.four_ref), channel_id=1, source_target_pairs={{0,1},{2,3},{4,5},{6,7},{8,9},{10,11},{12,13},{14,15},{16,17},{18,... | collective-permute-start | bytes 1572872 | tf_op jit(solution)/shard_map/ppermute | solution.py:159
  32.3 1.9 %collective-permute-start.2 = (bf16[2,512,256]{2,1,0:T(8,128)(2,1)S(1)}, bf16[2,512,256]{2,1,0:T(8,128)(2,1)}, u32[]{:S(2)}, u32[]{:S(2)}) collective-permute-start(bf16[2,512,256]{2,1,0:T(8,128)(2,1)S(1)} %collective-permute-done.1.two_ref), channel_id=1, source_target_pairs={{0,1},{1,0},{2,3},{3,2},{4,5},{5,4},{6,7},{7,6},{8,9},{9,8},{10,11... | collective-permute-start | bytes 1572872 | tf_op jit(solution)/shard_map/ppermute | solution.py:159
  34.2 0.0 collective-permute-done.own_swap_ref
  34.3 0.0 collective-permute-done.4.four_swap_ref
  34.3 2.0 %collective-permute-done.2.two_swap_ref = bf16[2,512,256]{2,1,0:T(8,128)(2,1)} collective-permute-done((bf16[2,512,256]{2,1,0:T(8,128)(2,1)S(1)}, bf16[2,512,256]{2,1,0:T(8,128)(2,1)}, u32[]{:S(2)}, u32[]{:S(2)}) %collective-permute-start.2) | collective-permute-done | bytes 524320 | tf_op jit(solution)/shard_map/ppermute | solution.py:159
  36.2 0.0 copy-done.1
  36.2 3.8 %shard_map.43 = bf16[64,48,256]{2,1,0:T(8,128)(2,1)} custom-call(s32[1]{0:T(128)} %bitcast.2.core_ref, bf16[2,512,256]{2,1,0:T(8,128)(2,1)S(1)} %copy-done.1, bf16[2,512,256]{2,1,0:T(8,128)(2,1)S(1)} %collective-permute-done.own_swap_ref, bf16[2,512,256]{2,1,0:T(8,128)(2,1)S(1)} %collective-permute-done.1.two_ref, ...), custom_call_target="tpu_custom_call" | custom-call | flops 1073741824 | bytes 4194304 | tf_op jit(solution)/shard_map/pallas_call | solution.py:188
  40.0 16.6 %all-to-all-start = ((bf16[64,48,256]{2,1,0:T(8,128)(2,1)}), bf16[64,48,256]{2,1,0:T(8,128)(2,1)S(1)}, u32[]{:S(2)}, u32[]{:S(2)}) async-start(bf16[64,48,256]{2,1,0:T(8,128)(2,1)} %shard_map.43), calls=%async_computation | async-start | bytes 3145728 | tf_op jit(solution)/shard_map/all_to_all | solution.py:196
  56.6 0.1 pad_add_fusion.refs_0_
  56.7 41.6 %all-to-all-done.refs_1_ = bf16[64,48,256]{2,1,0:T(8,128)(2,1)S(1)} async-done(((bf16[64,48,256]{2,1,0:T(8,128)(2,1)}), bf16[64,48,256]{2,1,0:T(8,128)(2,1)S(1)}, u32[]{:S(2)}, u32[]{:S(2)}) %all-to-all-start) | async-done | bytes 1572896 | tf_op jit(solution)/shard_map/all_to_all | solution.py:196
  98.3 1.5 %shard_map.44 = (f32[2,16,256]{2,1,0:T(8,128)}, f32[2,4,256]{2,1,0:T(4,128)}) custom-call(s32[2]{0:T(128)S(1)} %pad_add_fusion.refs_0_, bf16[64,48,256]{2,1,0:T(8,128)(2,1)S(1)} %all-to-all-done.refs_1_), custom_call_target="tpu_custom_call" | custom-call | flops 2097152 | bytes 3145728 | tf_op jit(solution)/shard_map/pallas_call | solution.py:200
Async XLA Ops:
  0.6 14.6 %copy-start.2 = (s32[64]{0:T(128)S(1)}, s32[64]{0:T(128)}, u32[]{:S(2)}) copy-start(s32[64]{0:T(128)} %param.3) | copy-start | bytes 772
  2.8 28.2 %collective-permute-start.1 = (bf16[2,512,256]{2,1,0:T(8,128)(2,1)}, bf16[2,512,256]{2,1,0:T(8,128)(2,1)S(1)}, u32[]{:S(2)}, u32[]{:S(2)}) collective-permute-start(bf16[2,512,256]{2,1,0:T(8,128)(2,1)} %shard_map.41.fields_ref.own_ref), channel_id=1, source_target_pairs={{2,0},{3,1},{4,2},{5,3},{6,4},{7,5},{0,6},{1,7},{10,8},{11,9},{12,... | collective-permute-start | bytes 1572872 | tf_op jit(solution)/shard_map/ppermute | solution.py:155
  5.5 25.5 %collective-permute-start.3 = (bf16[2,512,256]{2,1,0:T(8,128)(2,1)}, bf16[2,512,256]{2,1,0:T(8,128)(2,1)S(1)}, u32[]{:S(2)}, u32[]{:S(2)}) collective-permute-start(bf16[2,512,256]{2,1,0:T(8,128)(2,1)} %shard_map.41.fields_ref.own_ref), channel_id=1, source_target_pairs={{4,0},{5,1},{6,2},{7,3},{0,4},{1,5},{2,6},{3,7},{12,8},{13,9},{14,... | collective-permute-start | bytes 1572872 | tf_op jit(solution)/shard_map/ppermute | solution.py:155
  13.9 20.3 %collective-permute-start = (bf16[2,512,256]{2,1,0:T(8,128)(2,1)}, bf16[2,512,256]{2,1,0:T(8,128)(2,1)S(1)}, u32[]{:S(2)}, u32[]{:S(2)}) collective-permute-start(bf16[2,512,256]{2,1,0:T(8,128)(2,1)} %shard_map.41.fields_ref.own_ref), channel_id=1, source_target_pairs={{1,0},{3,2},{5,4},{7,6},{9,8},{11,10},{13,12},{15,14},{17,16},{19,... | collective-permute-start | bytes 1572872 | tf_op jit(solution)/shard_map/ppermute | solution.py:159
  15.3 1.0 %copy-start = (bf16[2,512,256]{2,1,0:T(8,128)(2,1)S(1)}, bf16[2,512,256]{2,1,0:T(8,128)(2,1)}, u32[]{:S(2)}) copy-start(bf16[2,512,256]{2,1,0:T(8,128)(2,1)} %shard_map.41.fields_ref.own_ref) | copy-start | bytes 1572868
  16.4 19.9 %copy-start.1 = (bf16[2,512,256]{2,1,0:T(8,128)(2,1)S(1)}, bf16[2,512,256]{2,1,0:T(8,128)(2,1)}, u32[]{:S(2)}) copy-start(bf16[2,512,256]{2,1,0:T(8,128)(2,1)} %shard_map.41.fields_ref.own_ref) | copy-start | bytes 1572868
  31.0 3.3 %collective-permute-start.4 = (bf16[2,512,256]{2,1,0:T(8,128)(2,1)S(1)}, bf16[2,512,256]{2,1,0:T(8,128)(2,1)S(1)}, u32[]{:S(2)}, u32[]{:S(2)}) collective-permute-start(bf16[2,512,256]{2,1,0:T(8,128)(2,1)S(1)} %collective-permute-done.3.four_ref), channel_id=1, source_target_pairs={{0,1},{2,3},{4,5},{6,7},{8,9},{10,11},{12,13},{14,15},{16,17},{18,... | collective-permute-start | bytes 1572872 | tf_op jit(solution)/shard_map/ppermute | solution.py:159
  32.3 3.9 %collective-permute-start.2 = (bf16[2,512,256]{2,1,0:T(8,128)(2,1)S(1)}, bf16[2,512,256]{2,1,0:T(8,128)(2,1)}, u32[]{:S(2)}, u32[]{:S(2)}) collective-permute-start(bf16[2,512,256]{2,1,0:T(8,128)(2,1)S(1)} %collective-permute-done.1.two_ref), channel_id=1, source_target_pairs={{0,1},{1,0},{2,3},{3,2},{4,5},{5,4},{6,7},{7,6},{8,9},{9,8},{10,11... | collective-permute-start | bytes 1572872 | tf_op jit(solution)/shard_map/ppermute | solution.py:159
  40.0 58.3 %all-to-all-start = ((bf16[64,48,256]{2,1,0:T(8,128)(2,1)}), bf16[64,48,256]{2,1,0:T(8,128)(2,1)S(1)}, u32[]{:S(2)}, u32[]{:S(2)}) async-start(bf16[64,48,256]{2,1,0:T(8,128)(2,1)} %shard_map.43), calls=%async_computation | async-start | bytes 3145728 | tf_op jit(solution)/shard_map/all_to_all | solution.py:196

commit v3 on v2

v3 whole, which is shorter than its diff:
```python
import math

import jax
import jax.numpy as jnp
from jax import lax
from jax.experimental import pallas as pl
from jax.experimental.pallas import tpu as pltpu
from jax.sharding import Mesh
from jax.sharding import PartitionSpec as P

BF16 = jnp.bfloat16
F32 = jnp.float32
VMEM = pl.BlockSpec(memory_space=pltpu.VMEM)
SMEM = pl.BlockSpec(memory_space=pltpu.SMEM)
QUADS, NEAR = 4, 2
PIX = ("zh", "zl", "yh", "yl")


def cost(flops, nbytes):
    return pl.CostEstimate(flops=flops, bytes_accessed=nbytes, transcendentals=0)


def dot_pixels(cols, rows):
    return lax.dot_general(cols, rows, (((0,), (0,)), ((), ())), preferred_element_type=F32)


def gram_t(col_real, col_imag, row_real, row_imag, row_imag_neg):
    real = dot_pixels(col_real, row_real) + dot_pixels(col_imag, row_imag)
    imag = dot_pixels(col_imag, row_real) + dot_pixels(col_real, row_imag_neg)
    return real, imag


def fields_kernel(frames_ref, fields_ref):
    fields_ref[0] = (frames_ref[0].astype(F32) - frames_ref[2].astype(F32)).astype(BF16)
    fields_ref[1] = (frames_ref[3].astype(F32) - frames_ref[1].astype(F32)).astype(BF16)


def split_terms(real, imag):
    row = lax.broadcasted_iota(jnp.int32, real.shape, 0)
    high_real = real.astype(BF16).astype(F32)
    high_imag = imag.astype(BF16).astype(F32)
    terms = jnp.where(row == 0, high_real, real - high_real)
    terms = jnp.where(row == 2, high_imag, terms)
    terms = jnp.where(row == 3, imag - high_imag, terms)
    return jnp.where(row > 3, 0.0, terms)


def ref_terms(counts, real, imag):
    return split_terms(
        jnp.dot(counts, real, preferred_element_type=F32),
        jnp.dot(counts, imag, preferred_element_type=F32),
    )


def store_tile(out_ref, base, parts):
    width = parts[0].shape[0]
    part_cols = width // (QUADS * NEAR * NEAR)
    for zl in range(NEAR):
        for yl in range(NEAR):
            for yh in range(QUADS):
                start = ((zl * QUADS + yh) * NEAR + yl) * part_cols
                for c, part in enumerate(parts):
                    to = base + (2 * yh + c) * part_cols
                    out_ref[zl * NEAR + yl, to : to + part_cols, :] = part[start : start + part_cols].astype(BF16)


def early_kernel(base_ref, fields_ref, two_ref, pixels_ref, out_ref, counts_ref):
    near, rows, width = out_ref.shape
    real, imag = fields_ref[0], fields_ref[1]
    two_real, two_imag = two_ref[0], two_ref[1]
    positions = base_ref[0] + lax.broadcasted_iota(jnp.int32, (pixels_ref.shape[0], real.shape[0]), 1)
    counts = jnp.sum((pixels_ref[...] == positions).astype(F32), axis=0, keepdims=True)
    counts = jnp.broadcast_to(counts, counts_ref.shape).astype(BF16)
    counts_ref[...] = counts
    imag_neg = -imag
    diag = jnp.concatenate(gram_t(real, imag, real, imag, imag_neg), axis=0).astype(BF16)
    total = diag.shape[0]
    at = lax.broadcasted_iota(jnp.int32, (total, total), 0)
    source = lax.broadcasted_iota(jnp.int32, (total, total), 1)
    dests = QUADS * QUADS
    diag_cols = width // (near * dests)
    j, c = at % diag_cols, at // diag_cols % 2
    dest, neighbour = at // (2 * diag_cols) % dests, at // (2 * diag_cols * dests)
    z = dest // QUADS * NEAR + neighbour // NEAR
    y = dest % QUADS * NEAR + neighbour % NEAR
    wanted = c * width + (z * (QUADS * NEAR) + y) * diag_cols + j
    pick = jnp.where(wanted == source, 1.0, 0.0).astype(BF16)
    placed = jnp.dot(pick, diag, preferred_element_type=F32)
    share = total // near
    out_ref[:, :share, :] = placed.reshape(near, share, width).astype(BF16)
    store_tile(out_ref, share, gram_t(two_real, two_imag, real, imag, imag_neg))
    refs = ref_terms(counts, real, imag) + pltpu.roll(ref_terms(counts, two_real, two_imag), 4, 0)
    refs = jnp.concatenate([refs, jnp.zeros_like(refs)], axis=0).astype(BF16)
    out_ref[:, rows - 16 :, :] = jnp.broadcast_to(refs[None], (near, 16, width))


def band_kernel(core_ref, own_ref, own_swap_ref, two_swap_ref, four_ref, four_swap_ref, counts_ref, out_ref):
    near, rows, width = out_ref.shape
    row_real, row_imag = own_ref[0], own_ref[1]
    row_imag_neg = -row_imag
    first_core = core_ref[0] == 0
    counts = counts_ref[...]
    share = 2 * width // near

    def tile(at, real, imag):
        store_tile(out_ref, at * share, gram_t(real, imag, row_real, row_imag, row_imag_neg))
        return ref_terms(counts, real, imag)

    def pick(a_ref, b_ref, part):
        return jnp.where(first_core, a_ref[part], b_ref[part])

    one = tile(0, pick(own_swap_ref, two_swap_ref, 0), pick(own_swap_ref, two_swap_ref, 1))
    three = tile(1, pick(two_swap_ref, four_swap_ref, 0), pick(two_swap_ref, four_swap_ref, 1))
    four = tile(2, four_ref[0], four_ref[1])
    refs = jnp.concatenate([one + pltpu.roll(three, 4, 0), four], axis=0).astype(BF16)
    out_ref[:, rows - 16 :, :] = jnp.broadcast_to(refs[None], (near, 16, width))


def middle_kernel(early_ref, band_ref, out_ref):
    width = out_ref.shape[2]
    share = 2 * width // early_ref.shape[0]
    tile_rows = share // QUADS

    def total(ref, start, count):
        return jnp.sum(ref[:, start : start + count, :].astype(F32), axis=0)

    tiles = (
        total(band_ref, 0, share),
        total(early_ref, share, share),
        total(band_ref, share, share),
        total(band_ref, 2 * share, share),
    )
    early_refs = total(early_ref, 2 * share, 16)
    band_refs = total(band_ref, 3 * share, 16)
    ref_rows = (band_refs[0:4], early_refs[4:8], band_refs[4:8], band_refs[8:12])

    def again(terms):
        shape = (8, width)
        real = jnp.broadcast_to(terms[0:1] + terms[1:2], shape)
        imag = jnp.broadcast_to(terms[2:3] + terms[3:4], shape)
        return split_terms(real, imag)

    own = again(early_refs[0:4])
    diag = total(early_ref, 0, share)
    diag_rows = share // (QUADS * QUADS)
    for zh in range(QUADS):
        dests = pl.ds(zh * QUADS, QUADS)
        out_ref[dests, :tile_rows, :] = tiles[zh].reshape(QUADS, tile_rows, width).astype(BF16)
        refs = own + pltpu.roll(again(ref_rows[zh]), 4, 0)
        part = diag[zh * QUADS * diag_rows : (zh + 1) * QUADS * diag_rows].reshape(QUADS, diag_rows, width)
        rest = jnp.concatenate([part, jnp.broadcast_to(refs[None], (QUADS, 8, width))], axis=1)
        out_ref[dests, tile_rows:, :] = rest.astype(BF16)


def unit_phase(real, imag):
    magnitude = jnp.maximum(jnp.sqrt(real * real + imag * imag), 1.0)
    return real / magnitude, imag / magnitude


def pick_lanes(values, start, count):
    lanes = values.shape[1]
    lane = lax.broadcasted_iota(jnp.int32, (count, lanes), 1)
    row = lax.broadcasted_iota(jnp.int32, (count, lanes), 0)
    return jnp.sum(jnp.where(lane == start + row, values, 0.0), axis=1, keepdims=True)


def rotate(real, imag, row_phase, col_phase, pixel_scale):
    unit_real = row_phase[0] * col_phase[0] + row_phase[1] * col_phase[1]
    unit_imag = row_phase[1] * col_phase[0] - row_phase[0] * col_phase[1]
    return (
        (unit_real * real - unit_imag * imag) * pixel_scale,
        (unit_real * imag + unit_imag * real) * pixel_scale,
    )


def final_kernel(pixel_scale, starts_ref, parts_ref, band_out, diag_out):
    part_cols, diag_cols = band_out.shape[1], diag_out.shape[1]
    sums = jnp.sum(parts_ref[...].astype(F32), axis=0)
    band, rest = sums[: 2 * part_cols], sums[2 * part_cols :]
    diag, refs = rest[: 2 * diag_cols], rest[2 * diag_cols :]
    row_phase = unit_phase(refs[0:1] + refs[1:2], refs[2:3] + refs[3:4])
    other_phase = unit_phase(refs[4:5] + refs[5:6], refs[6:7] + refs[7:8])
    col_phase = [pick_lanes(part, starts_ref[0], part_cols) for part in other_phase]
    band_out[0], band_out[1] = rotate(band[:part_cols], band[part_cols:], row_phase, col_phase, pixel_scale)
    diag_phase = [pick_lanes(part, starts_ref[1], diag_cols) for part in row_phase]
    diag_out[0], diag_out[1] = rotate(diag[:diag_cols], diag[diag_cols:], row_phase, diag_phase, pixel_scale)


def shards(frames, ref_pixels):
    pix_count = lax.axis_size(PIX)
    mode_count = lax.axis_size("mode")
    pix_index = lax.axis_index(PIX)
    mode_index = lax.axis_index("mode")
    pixel_rows, width = frames.shape[1:]
    near, dests = NEAR * NEAR, QUADS * QUADS
    tile_dests = pix_count // QUADS
    part_cols = width // tile_dests
    diag_cols = width // pix_count
    share = 2 * width // near
    field_bytes = 2 * pixel_rows * width * 2
    tile_flops = 8 * pixel_rows * width * width
    params = pltpu.CompilerParams(vmem_limit_bytes=32 << 20)

    def shift(array, step):
        pairs = [((m + step) % mode_count, m) for m in range(mode_count)]
        return lax.ppermute(array, "mode", pairs)

    def swap(array, even=False, odd=False):
        pairs = [(m, m ^ 1) for m in range(mode_count) if (odd if m % 2 else even)]
        return lax.ppermute(array, "mode", pairs)

    fields = pl.pallas_call(
        fields_kernel,
        out_shape=jax.ShapeDtypeStruct((2, pixel_rows, width), BF16),
        in_specs=[VMEM],
        out_specs=VMEM,
        cost_estimate=cost(4 * pixel_rows * width, 3 * field_bytes),
    )(frames)
    two = shift(fields, 2)
    four = shift(fields, 4)
    own_swap = swap(fields, odd=True)
    two, own_swap = lax.optimization_barrier((two, own_swap))
    two_swap = swap(two, even=True, odd=True)
    early, counts = pl.pallas_call(
        early_kernel,
        out_shape=(
            jax.ShapeDtypeStruct((near, 2 * share + 16, width), BF16),
            jax.ShapeDtypeStruct((8, pixel_rows), BF16),
        ),
        in_specs=[SMEM, VMEM, VMEM, VMEM],
        out_specs=(VMEM, VMEM),
        cost_estimate=cost(2 * tile_flops, 4 * field_bytes),
        compiler_params=params,
    )((pix_index * pixel_rows).reshape(1), fields, two, ref_pixels[:, None])
    early = lax.all_to_all(early, ("zl", "yl"), 0, 0, tiled=True)
    four, two_swap, counts = lax.optimization_barrier((four, two_swap, counts))
    four_swap = swap(four, even=True)
    band = pl.pallas_call(
        band_kernel,
        out_shape=jax.ShapeDtypeStruct((near, 3 * share + 16, width), BF16),
        in_specs=[SMEM] + [VMEM] * 6,
        out_specs=VMEM,
        cost_estimate=cost(3 * tile_flops, 8 * field_bytes),
        compiler_params=params,
    )((mode_index % 2).reshape(1), fields, own_swap, two_swap, four, four_swap, counts)
    band = lax.all_to_all(band, ("zl", "yl"), 0, 0, tiled=True)
    parts = pl.pallas_call(
        middle_kernel,
        out_shape=jax.ShapeDtypeStruct((dests, 2 * part_cols + 2 * diag_cols + 8, width), BF16),
        in_specs=[VMEM, VMEM],
        out_specs=VMEM,
        cost_estimate=cost(4 * field_bytes, 4 * field_bytes),
        compiler_params=params,
    )(early, band)
    starts = jnp.stack([(pix_index % tile_dests) * part_cols, pix_index * diag_cols])
    parts, starts = lax.optimization_barrier((parts, starts))
    parts = lax.all_to_all(parts, ("zh", "yh"), 0, 0, tiled=True)

    scale = 1.0 / math.sqrt(pix_count * pixel_rows)
    band_out, diag_out = pl.pallas_call(
        lambda *refs: final_kernel(scale, *refs),
        out_shape=(
            jax.ShapeDtypeStruct((2, part_cols, width), F32),
            jax.ShapeDtypeStruct((2, diag_cols, width), F32),
        ),
        in_specs=[SMEM, VMEM],
        out_specs=(VMEM, VMEM),
        cost_estimate=cost(field_bytes, field_bytes),
        compiler_params=params,
    )(starts, parts)
    return jnp.transpose(band_out, (0, 2, 1)), jnp.transpose(diag_out, (0, 2, 1))


def solution(mesh):
    split = Mesh(mesh.devices.reshape(QUADS, NEAR, QUADS, NEAR, -1), (*PIX, "mode"))
    return jax.shard_map(
        shards,
        mesh=split,
        in_specs=(P(None, PIX, "mode"), P()),
        out_specs=(P(None, "mode", PIX), P(None, "mode", PIX)),
        check_vma=False,
    )
```

time: 100 us -> 99.8 us (level)
  waiting for transfers between devices: 57.1 us -> 24.7 us
  blocking collectives: 0 us -> 30.5 us
  starting transfers between devices: 32.2 us -> 33.6 us
    all_to_all x0 -> x1, blocking collectives: none -> 30.5 us  [shards(): parts = lax.all_to_all(parts, ('zh', 'yh'), 0, 0, tiled=True)]
    all_to_all x1 -> x2, waiting for transfers between devices: 41.6 us -> 14.1 us  [the longest x1 10.8 us: shards(): band = lax.all_to_all(band, ('zl', 'yl'), 0, 0, tiled=True)]
    ppermute x2, waiting for transfers between devices: 13.5 us -> 9.2 us  [shift(): return lax.ppermute(array, 'mode', pairs)]
    pallas_call x2 -> x3, Pallas kernels: 4.88 us -> 4.32 us  [the longest x1 2.13 us: shards(): pl.pallas_call(band_kernel, out_shape=jax.ShapeDtypeStruct((near, 3 * sha...]
    all_to_all x1 -> x2, starting transfers between devices: 16.6 us -> 17 us  [the longest x1 13.5 us: shards(): early = lax.all_to_all(early, ('zl', 'yl'), 0, 0, tiled=True)]
  transfers between devices with their start and end apart: 6 -> 7, of which waited for: 3 -> 4; matrix products, arithmetic and copies ran while one was open for 0% -> 0% of each run, Pallas kernels for 1% -> 4%
where the time goes in v3:
time: 99.8 us; the launch traced here: 99.2 us
  starting transfers between devices  33.6 us (34%)
  blocking collectives  30.5 us (31%)
  waiting for transfers between devices  24.7 us (25%)
  Pallas kernels  7.75 us (8%)
  local copies, waits for them, and re-layouts  1.79 us (2%)
    all_to_all x1, blocking collectives, shards(): parts = lax.all_to_all(parts, ('zh', 'yh'), 0, 0, tiled=True)  30.5 us
    all_to_all x1, starting transfers between devices, shards(): early = lax.all_to_all(early, ('zl', 'yl'), 0, 0, tiled=True)  13.5 us
    ppermute x2, starting transfers between devices, shift(): return lax.ppermute(array, 'mode', pairs)  11.1 us
    all_to_all x1, waiting for transfers between devices, shards(): band = lax.all_to_all(band, ('zl', 'yl'), 0, 0, tiled=True)  10.8 us
    ppermute x2, waiting for transfers between devices, shift(): return lax.ppermute(array, 'mode', pairs)  9.2 us
    ppermute x3, starting transfers between devices, swap(): return lax.ppermute(array, 'mode', pairs)  5.47 us
    all_to_all x1, starting transfers between devices, shards(): band = lax.all_to_all(band, ('zl', 'yl'), 0, 0, tiled=True)  3.5 us
    all_to_all x1, waiting for transfers between devices, shards(): early = lax.all_to_all(early, ('zl', 'yl'), 0, 0, tiled=True)  3.24 us
  transfers between devices with their start and end apart: 7, of which 4 were waited for; matrix products, arithmetic and copies ran while one was open for 0% of the time, Pallas kernels for 4%

profile of v3, /device:TPU:6, one launch (start us, length us, event | category | flops | bytes accessed | tf_op | source)
XLA Modules:
  0.0 99.2 jit_solution(3544383232051731127)
XLA Ops:
  0.6 2.1 %shard_map.41.fields_ref.own_ref = bf16[2,512,256]{2,1,0:T(8,128)(2,1)} custom-call(bf16[4,512,256]{2,1,0:T(8,128)(2,1)} %frames_ref.1), custom_call_target="tpu_custom_call" | custom-call | flops 524288 | bytes 1572864 | tf_op jit(solution)/shard_map/pallas_call | solution.py:212
  2.8 1.3 %collective-permute-start.1 = (bf16[2,512,256]{2,1,0:T(8,128)(2,1)}, bf16[2,512,256]{2,1,0:T(8,128)(2,1)S(1)}, u32[]{:S(2)}, u32[]{:S(2)}) collective-permute-start(bf16[2,512,256]{2,1,0:T(8,128)(2,1)} %shard_map.41.fields_ref.own_ref), channel_id=1, source_target_pairs={{1,0},{3,2},{5,4},{7,6},{9,8},{11,10},{13,12},{15,14},{17,16},{19,... | collective-permute-start | bytes 1572872 | tf_op jit(solution)/shard_map/ppermute | solution.py:210
  4.1 2.7 %collective-permute-start = (bf16[2,512,256]{2,1,0:T(8,128)(2,1)}, bf16[2,512,256]{2,1,0:T(8,128)(2,1)S(1)}, u32[]{:S(2)}, u32[]{:S(2)}) collective-permute-start(bf16[2,512,256]{2,1,0:T(8,128)(2,1)} %shard_map.41.fields_ref.own_ref), channel_id=1, source_target_pairs={{2,0},{3,1},{4,2},{5,3},{6,4},{7,5},{0,6},{1,7},{10,8},{11,9},{12,... | collective-permute-start | bytes 1572872 | tf_op jit(solution)/shard_map/ppermute | solution.py:206
  6.8 8.4 %collective-permute-start.2 = (bf16[2,512,256]{2,1,0:T(8,128)(2,1)}, bf16[2,512,256]{2,1,0:T(8,128)(2,1)S(1)}, u32[]{:S(2)}, u32[]{:S(2)}) collective-permute-start(bf16[2,512,256]{2,1,0:T(8,128)(2,1)} %shard_map.41.fields_ref.own_ref), channel_id=1, source_target_pairs={{4,0},{5,1},{6,2},{7,3},{0,4},{1,5},{2,6},{3,7},{12,8},{13,9},{14,... | collective-permute-start | bytes 1572872 | tf_op jit(solution)/shard_map/ppermute | solution.py:206
  15.2 0.0 collective-permute-done.1.own_swap_ref
  15.2 9.2 %collective-permute-done.two_ref = bf16[2,512,256]{2,1,0:T(8,128)(2,1)S(1)} collective-permute-done((bf16[2,512,256]{2,1,0:T(8,128)(2,1)}, bf16[2,512,256]{2,1,0:T(8,128)(2,1)S(1)}, u32[]{:S(2)}, u32[]{:S(2)}) %collective-permute-start) | collective-permute-done | bytes 524320 | tf_op jit(solution)/shard_map/ppermute | solution.py:206
  24.4 2.1 %collective-permute-start.3 = (bf16[2,512,256]{2,1,0:T(8,128)(2,1)S(1)}, bf16[2,512,256]{2,1,0:T(8,128)(2,1)S(1)}, u32[]{:S(2)}, u32[]{:S(2)}) collective-permute-start(bf16[2,512,256]{2,1,0:T(8,128)(2,1)S(1)} %collective-permute-done.two_ref), channel_id=1, source_target_pairs={{0,1},{1,0},{2,3},{3,2},{4,5},{5,4},{6,7},{7,6},{8,9},{9,8},{10,11... | collective-permute-start | bytes 1572872 | tf_op jit(solution)/shard_map/ppermute | solution.py:210
  26.5 0.0 copy-start.2
  26.5 0.6 copy-done.2
  27.2 0.1 copy.4.pixels_ref
  27.3 0.0 copy-start
  27.3 1.0 %copy-done = bf16[2,512,256]{2,1,0:T(8,128)(2,1)S(1)} copy-done((bf16[2,512,256]{2,1,0:T(8,128)(2,1)S(1)}, bf16[2,512,256]{2,1,0:T(8,128)(2,1)}, u32[]{:S(2)}) %copy-start) | copy-done | bytes 524312
  28.3 2.0 %shard_map.42 = (bf16[4,272,256]{2,1,0:T(8,128)(2,1)}, bf16[8,512]{1,0:T(8,128)(2,1)S(1)}) custom-call(s32[1]{0:T(128)} %bitcast.base_ref, bf16[2,512,256]{2,1,0:T(8,128)(2,1)S(1)} %copy-done, bf16[2,512,256]{2,1,0:T(8,128)(2,1)S(1)} %collective-permute-done.two_ref, s32[64,1]{1,0:T(8,128)S(1)} %copy.4.pixels_ref), custom_call_target="tpu_custom_call" | custom-call | flops 536870912 | bytes 2097152 | tf_op jit(solution)/shard_map/pallas_call | solution.py:224
  30.3 0.0 copy-start.1
  30.3 13.5 %all-to-all-start = ((bf16[4,272,256]{2,1,0:T(8,128)(2,1)}), bf16[4,272,256]{2,1,0:T(8,128)(2,1)S(1)}, u32[]{:S(2)}, u32[]{:S(2)}) async-start(bf16[4,272,256]{2,1,0:T(8,128)(2,1)} %get-tuple-element.14), calls=%async_computation | async-start | bytes 1114112 | tf_op jit(solution)/shard_map/all_to_all | solution.py:235
  43.8 0.0 collective-permute-done.2.four_ref
  43.8 0.0 collective-permute-done.3.two_swap_ref
  43.8 2.1 %collective-permute-start.4 = (bf16[2,512,256]{2,1,0:T(8,128)(2,1)S(1)}, bf16[2,512,256]{2,1,0:T(8,128)(2,1)S(1)}, u32[]{:S(2)}, u32[]{:S(2)}) collective-permute-start(bf16[2,512,256]{2,1,0:T(8,128)(2,1)S(1)} %collective-permute-done.2.four_ref), channel_id=1, source_target_pairs={{0,1},{2,3},{4,5},{6,7},{8,9},{10,11},{12,13},{14,15},{16,17},{18,... | collective-permute-start | bytes 1572872 | tf_op jit(solution)/shard_map/ppermute | solution.py:210
  45.9 1.5 %collective-permute-done.4.four_swap_ref = bf16[2,512,256]{2,1,0:T(8,128)(2,1)S(1)} collective-permute-done((bf16[2,512,256]{2,1,0:T(8,128)(2,1)S(1)}, bf16[2,512,256]{2,1,0:T(8,128)(2,1)S(1)}, u32[]{:S(2)}, u32[]{:S(2)}) %collective-permute-start.4) | collective-permute-done | bytes 524320 | tf_op jit(solution)/shard_map/ppermute | solution.py:210
  47.4 0.0 copy-done.1
  47.4 2.1 %shard_map.43 = bf16[4,400,256]{2,1,0:T(8,128)(2,1)} custom-call(s32[1]{0:T(128)} %bitcast.2.core_ref, bf16[2,512,256]{2,1,0:T(8,128)(2,1)S(1)} %copy-done.1, bf16[2,512,256]{2,1,0:T(8,128)(2,1)S(1)} %collective-permute-done.1.own_swap_ref, bf16[2,512,256]{2,1,0:T(8,128)(2,1)S(1)} %collective-permute-done.3.two_swap_ref, ...), custom_call_target="tpu_custom_call" | custom-call | flops 805306368 | bytes 4194304 | tf_op jit(solution)/shard_map/pallas_call | solution.py:238
  49.6 3.2 %all-to-all-done.early_ref = bf16[4,272,256]{2,1,0:T(8,128)(2,1)S(1)} async-done(((bf16[4,272,256]{2,1,0:T(8,128)(2,1)}), bf16[4,272,256]{2,1,0:T(8,128)(2,1)S(1)}, u32[]{:S(2)}, u32[]{:S(2)}) %all-to-all-start) | async-done | bytes 557088 | tf_op jit(solution)/shard_map/all_to_all | solution.py:235
  52.8 3.5 %all-to-all-start.1 = ((bf16[4,400,256]{2,1,0:T(8,128)(2,1)}), bf16[4,400,256]{2,1,0:T(8,128)(2,1)S(1)}, u32[]{:S(2)}, u32[]{:S(2)}) async-start(bf16[4,400,256]{2,1,0:T(8,128)(2,1)} %shard_map.43), calls=%async_computation.1 | async-start | bytes 1638400 | tf_op jit(solution)/shard_map/all_to_all | solution.py:246
  56.3 0.1 pad_add_fusion.refs_0_
  56.4 10.8 %all-to-all-done.1.band_ref = bf16[4,400,256]{2,1,0:T(8,128)(2,1)S(1)} async-done(((bf16[4,400,256]{2,1,0:T(8,128)(2,1)}), bf16[4,400,256]{2,1,0:T(8,128)(2,1)S(1)}, u32[]{:S(2)}, u32[]{:S(2)}) %all-to-all-start.1) | async-done | bytes 819232 | tf_op jit(solution)/shard_map/all_to_all | solution.py:246
  67.2 0.2 shard_map.44
  67.4 30.5 %all_to_all.15.refs_1_ = bf16[16,48,256]{2,1,0:T(8,128)(2,1)S(1)} all-to-all(bf16[16,48,256]{2,1,0:T(8,128)(2,1)S(1)} %shard_map.44), channel_id=1, replica_groups=mesh['zh'=4,'zl'=2,'yh'=4,'yl'=2,'mode'=8] {'zh','yh'}, dimensions={0} | all-to-all | bytes 786432 | tf_op jit(solution)/shard_map/all_to_all | solution.py:257
  97.9 1.3 %shard_map.45 = (f32[2,16,256]{2,1,0:T(8,128)}, f32[2,4,256]{2,1,0:T(4,128)}) custom-call(s32[2]{0:T(128)S(1)} %pad_add_fusion.refs_0_, bf16[16,48,256]{2,1,0:T(8,128)(2,1)S(1)} %all_to_all.15.refs_1_), custom_call_target="tpu_custom_call" | custom-call | flops 524288 | bytes 524288 | tf_op jit(solution)/shard_map/pallas_call | solution.py:260
Async XLA Ops:
  2.8 12.4 %collective-permute-start.1 = (bf16[2,512,256]{2,1,0:T(8,128)(2,1)}, bf16[2,512,256]{2,1,0:T(8,128)(2,1)S(1)}, u32[]{:S(2)}, u32[]{:S(2)}) collective-permute-start(bf16[2,512,256]{2,1,0:T(8,128)(2,1)} %shard_map.41.fields_ref.own_ref), channel_id=1, source_target_pairs={{1,0},{3,2},{5,4},{7,6},{9,8},{11,10},{13,12},{15,14},{17,16},{19,... | collective-permute-start | bytes 1572872 | tf_op jit(solution)/shard_map/ppermute | solution.py:210
  4.1 20.4 %collective-permute-start = (bf16[2,512,256]{2,1,0:T(8,128)(2,1)}, bf16[2,512,256]{2,1,0:T(8,128)(2,1)S(1)}, u32[]{:S(2)}, u32[]{:S(2)}) collective-permute-start(bf16[2,512,256]{2,1,0:T(8,128)(2,1)} %shard_map.41.fields_ref.own_ref), channel_id=1, source_target_pairs={{2,0},{3,1},{4,2},{5,3},{6,4},{7,5},{0,6},{1,7},{10,8},{11,9},{12,... | collective-permute-start | bytes 1572872 | tf_op jit(solution)/shard_map/ppermute | solution.py:206
  6.8 37.0 %collective-permute-start.2 = (bf16[2,512,256]{2,1,0:T(8,128)(2,1)}, bf16[2,512,256]{2,1,0:T(8,128)(2,1)S(1)}, u32[]{:S(2)}, u32[]{:S(2)}) collective-permute-start(bf16[2,512,256]{2,1,0:T(8,128)(2,1)} %shard_map.41.fields_ref.own_ref), channel_id=1, source_target_pairs={{4,0},{5,1},{6,2},{7,3},{0,4},{1,5},{2,6},{3,7},{12,8},{13,9},{14,... | collective-permute-start | bytes 1572872 | tf_op jit(solution)/shard_map/ppermute | solution.py:206
  24.4 19.4 %collective-permute-start.3 = (bf16[2,512,256]{2,1,0:T(8,128)(2,1)S(1)}, bf16[2,512,256]{2,1,0:T(8,128)(2,1)S(1)}, u32[]{:S(2)}, u32[]{:S(2)}) collective-permute-start(bf16[2,512,256]{2,1,0:T(8,128)(2,1)S(1)} %collective-permute-done.two_ref), channel_id=1, source_target_pairs={{0,1},{1,0},{2,3},{3,2},{4,5},{5,4},{6,7},{7,6},{8,9},{9,8},{10,11... | collective-permute-start | bytes 1572872 | tf_op jit(solution)/shard_map/ppermute | solution.py:210
  26.5 0.7 copy-start.2
  27.3 1.0 %copy-start = (bf16[2,512,256]{2,1,0:T(8,128)(2,1)S(1)}, bf16[2,512,256]{2,1,0:T(8,128)(2,1)}, u32[]{:S(2)}) copy-start(bf16[2,512,256]{2,1,0:T(8,128)(2,1)} %shard_map.41.fields_ref.own_ref) | copy-start | bytes 1572868
  30.3 17.1 %copy-start.1 = (bf16[2,512,256]{2,1,0:T(8,128)(2,1)S(1)}, bf16[2,512,256]{2,1,0:T(8,128)(2,1)}, u32[]{:S(2)}) copy-start(bf16[2,512,256]{2,1,0:T(8,128)(2,1)} %shard_map.41.fields_ref.own_ref) | copy-start | bytes 1572868
  30.3 22.5 %all-to-all-start = ((bf16[4,272,256]{2,1,0:T(8,128)(2,1)}), bf16[4,272,256]{2,1,0:T(8,128)(2,1)S(1)}, u32[]{:S(2)}, u32[]{:S(2)}) async-start(bf16[4,272,256]{2,1,0:T(8,128)(2,1)} %get-tuple-element.14), calls=%async_computation | async-start | bytes 1114112 | tf_op jit(solution)/shard_map/all_to_all | solution.py:235
  43.8 3.6 %collective-permute-start.4 = (bf16[2,512,256]{2,1,0:T(8,128)(2,1)S(1)}, bf16[2,512,256]{2,1,0:T(8,128)(2,1)S(1)}, u32[]{:S(2)}, u32[]{:S(2)}) collective-permute-start(bf16[2,512,256]{2,1,0:T(8,128)(2,1)S(1)} %collective-permute-done.2.four_ref), channel_id=1, source_target_pairs={{0,1},{2,3},{4,5},{6,7},{8,9},{10,11},{12,13},{14,15},{16,17},{18,... | collective-permute-start | bytes 1572872 | tf_op jit(solution)/shard_map/ppermute | solution.py:210
  52.8 14.4 %all-to-all-start.1 = ((bf16[4,400,256]{2,1,0:T(8,128)(2,1)}), bf16[4,400,256]{2,1,0:T(8,128)(2,1)S(1)}, u32[]{:S(2)}, u32[]{:S(2)}) async-start(bf16[4,400,256]{2,1,0:T(8,128)(2,1)} %shard_map.43), calls=%async_computation.1 | async-start | bytes 1638400 | tf_op jit(solution)/shard_map/all_to_all | solution.py:246

commit v4 on v3

--- a/solution.py
+++ b/solution.py
@@ -13,6 +13,7 @@
 VMEM = pl.BlockSpec(memory_space=pltpu.VMEM)
 SMEM = pl.BlockSpec(memory_space=pltpu.SMEM)
 QUADS, NEAR = 4, 2
+REF_ROWS = 32
 PIX = ("zh", "zl", "yh", "yl")
 
 
@@ -64,16 +65,13 @@
                     out_ref[zl * NEAR + yl, to : to + part_cols, :] = part[start : start + part_cols].astype(BF16)
 
 
-def early_kernel(base_ref, fields_ref, two_ref, pixels_ref, out_ref, counts_ref):
-    near, rows, width = out_ref.shape
+def diag_kernel(base_ref, fields_ref, pixels_ref, out_ref, counts_ref):
+    near, share, width = out_ref.shape
     real, imag = fields_ref[0], fields_ref[1]
-    two_real, two_imag = two_ref[0], two_ref[1]
     positions = base_ref[0] + lax.broadcasted_iota(jnp.int32, (pixels_ref.shape[0], real.shape[0]), 1)
     counts = jnp.sum((pixels_ref[...] == positions).astype(F32), axis=0, keepdims=True)
-    counts = jnp.broadcast_to(counts, counts_ref.shape).astype(BF16)
-    counts_ref[...] = counts
-    imag_neg = -imag
-    diag = jnp.concatenate(gram_t(real, imag, real, imag, imag_neg), axis=0).astype(BF16)
+    counts_ref[...] = jnp.broadcast_to(counts, counts_ref.shape).astype(BF16)
+    diag = jnp.concatenate(gram_t(real, imag, real, imag, -imag), axis=0).astype(BF16)
     total = diag.shape[0]
     at = lax.broadcasted_iota(jnp.int32, (total, total), 0)
     source = lax.broadcasted_iota(jnp.int32, (total, total), 1)
@@ -86,53 +84,50 @@
     wanted = c * width + (z * (QUADS * NEAR) + y) * diag_cols + j
     pick = jnp.where(wanted == source, 1.0, 0.0).astype(BF16)
     placed = jnp.dot(pick, diag, preferred_element_type=F32)
-    share = total // near
-    out_ref[:, :share, :] = placed.reshape(near, share, width).astype(BF16)
-    store_tile(out_ref, share, gram_t(two_real, two_imag, real, imag, imag_neg))
-    refs = ref_terms(counts, real, imag) + pltpu.roll(ref_terms(counts, two_real, two_imag), 4, 0)
-    refs = jnp.concatenate([refs, jnp.zeros_like(refs)], axis=0).astype(BF16)
-    out_ref[:, rows - 16 :, :] = jnp.broadcast_to(refs[None], (near, 16, width))
-
-
-def band_kernel(core_ref, own_ref, own_swap_ref, two_swap_ref, four_ref, four_swap_ref, counts_ref, out_ref):
+    out_ref[...] = placed.reshape(near, share, width).astype(BF16)
+
+
+def same_core_kernel(own_ref, two_ref, four_ref, out_ref):
+    row_real, row_imag = own_ref[0], own_ref[1]
+    row_imag_neg = -row_imag
+    share = out_ref.shape[1] // 2
+    store_tile(out_ref, 0, gram_t(two_ref[0], two_ref[1], row_real, row_imag, row_imag_neg))
+    store_tile(out_ref, share, gram_t(four_ref[0], four_ref[1], row_real, row_imag, row_imag_neg))
+
+
+def parts_kernel(
+    core_ref, own_ref, own_swap_ref, two_ref, two_swap_ref, four_ref, four_swap_ref, counts_ref, diag_ref, same_ref, out_ref
+):
     near, rows, width = out_ref.shape
     row_real, row_imag = own_ref[0], own_ref[1]
     row_imag_neg = -row_imag
     first_core = core_ref[0] == 0
     counts = counts_ref[...]
-    share = 2 * width // near
-
-    def tile(at, real, imag):
-        store_tile(out_ref, at * share, gram_t(real, imag, row_real, row_imag, row_imag_neg))
-        return ref_terms(counts, real, imag)
+    share = diag_ref.shape[1]
 
     def pick(a_ref, b_ref, part):
         return jnp.where(first_core, a_ref[part], b_ref[part])
 
-    one = tile(0, pick(own_swap_ref, two_swap_ref, 0), pick(own_swap_ref, two_swap_ref, 1))
-    three = tile(1, pick(two_swap_ref, four_swap_ref, 0), pick(two_swap_ref, four_swap_ref, 1))
-    four = tile(2, four_ref[0], four_ref[1])
-    refs = jnp.concatenate([one + pltpu.roll(three, 4, 0), four], axis=0).astype(BF16)
-    out_ref[:, rows - 16 :, :] = jnp.broadcast_to(refs[None], (near, 16, width))
-
-
-def middle_kernel(early_ref, band_ref, out_ref):
-    width = out_ref.shape[2]
-    share = 2 * width // early_ref.shape[0]
+    one = pick(own_swap_ref, two_swap_ref, 0), pick(own_swap_ref, two_swap_ref, 1)
+    three = pick(two_swap_ref, four_swap_ref, 0), pick(two_swap_ref, four_swap_ref, 1)
+    store_tile(out_ref, 0, gram_t(*one, row_real, row_imag, row_imag_neg))
+    store_tile(out_ref, share, gram_t(*three, row_real, row_imag, row_imag_neg))
+    out_ref[:, 2 * share : 4 * share, :] = same_ref[...]
+    out_ref[:, 4 * share : 5 * share, :] = diag_ref[...]
+    first = ref_terms(counts, row_real, row_imag) + pltpu.roll(ref_terms(counts, *one), 4, 0)
+    second = ref_terms(counts, two_ref[0], two_ref[1]) + pltpu.roll(ref_terms(counts, *three), 4, 0)
+    third = ref_terms(counts, four_ref[0], four_ref[1])
+    refs = jnp.concatenate([first, second, third, jnp.zeros_like(third)], axis=0).astype(BF16)
+    out_ref[:, 5 * share :, :] = jnp.broadcast_to(refs[None], (near, rows - 5 * share, width))
+
+
+def middle_kernel(parts_ref, out_ref):
+    near, _, width = parts_ref.shape
+    share = 2 * width // near
     tile_rows = share // QUADS
 
-    def total(ref, start, count):
-        return jnp.sum(ref[:, start : start + count, :].astype(F32), axis=0)
-
-    tiles = (
-        total(band_ref, 0, share),
-        total(early_ref, share, share),
-        total(band_ref, share, share),
-        total(band_ref, 2 * share, share),
-    )
-    early_refs = total(early_ref, 2 * share, 16)
-    band_refs = total(band_ref, 3 * share, 16)
-    ref_rows = (band_refs[0:4], early_refs[4:8], band_refs[4:8], band_refs[8:12])
+    def total(start, count):
+        return jnp.sum(parts_ref[:, start : start + count, :].astype(F32), axis=0)
 
     def again(terms):
         shape = (8, width)
@@ -140,15 +135,16 @@
         imag = jnp.broadcast_to(terms[2:3] + terms[3:4], shape)
         return split_terms(real, imag)
 
-    own = again(early_refs[0:4])
-    diag = total(early_ref, 0, share)
+    refs = total(5 * share, REF_ROWS)
+    own = again(refs[0:4])
+    diag = total(4 * share, share)
     diag_rows = share // (QUADS * QUADS)
-    for zh in range(QUADS):
+    for zh, at in enumerate((0, 2, 1, 3)):
         dests = pl.ds(zh * QUADS, QUADS)
-        out_ref[dests, :tile_rows, :] = tiles[zh].reshape(QUADS, tile_rows, width).astype(BF16)
-        refs = own + pltpu.roll(again(ref_rows[zh]), 4, 0)
+        out_ref[dests, :tile_rows, :] = total(at * share, share).reshape(QUADS, tile_rows, width).astype(BF16)
+        both = own + pltpu.roll(again(refs[4 * zh + 4 : 4 * zh + 8]), 4, 0)
         part = diag[zh * QUADS * diag_rows : (zh + 1) * QUADS * diag_rows].reshape(QUADS, diag_rows, width)
-        rest = jnp.concatenate([part, jnp.broadcast_to(refs[None], (QUADS, 8, width))], axis=1)
+        rest = jnp.concatenate([part, jnp.broadcast_to(both[None], (QUADS, 8, width))], axis=1)
         out_ref[dests, tile_rows:, :] = rest.astype(BF16)
 
 
@@ -219,39 +215,46 @@
     two = shift(fields, 2)
     four = shift(fields, 4)
     own_swap = swap(fields, odd=True)
-    two, own_swap = lax.optimization_barrier((two, own_swap))
-    two_swap = swap(two, even=True, odd=True)
-    early, counts = pl.pallas_call(
-        early_kernel,
+    diag, counts = pl.pallas_call(
+        diag_kernel,
         out_shape=(
-            jax.ShapeDtypeStruct((near, 2 * share + 16, width), BF16),
+            jax.ShapeDtypeStruct((near, share, width), BF16),
             jax.ShapeDtypeStruct((8, pixel_rows), BF16),
         ),
-        in_specs=[SMEM, VMEM, VMEM, VMEM],
+        in_specs=[SMEM, VMEM, VMEM],
         out_specs=(VMEM, VMEM),
+        cost_estimate=cost(tile_flops, 2 * field_bytes),
+        compiler_params=params,
+    )((pix_index * pixel_rows).reshape(1), fields, ref_pixels[:, None])
+    two, own_swap, diag = lax.optimization_barrier((two, own_swap, diag))
+    two_swap = swap(two, even=True, odd=True)
+    four, two_swap = lax.optimization_barrier((four, two_swap))
+    four_swap = swap(four, even=True)
+    same = pl.pallas_call(
+        same_core_kernel,
+        out_shape=jax.ShapeDtypeStruct((near, 2 * share, width), BF16),
+        in_specs=[VMEM] * 3,
+        out_specs=VMEM,
         cost_estimate=cost(2 * tile_flops, 4 * field_bytes),
         compiler_params=params,
-    )((pix_index * pixel_rows).reshape(1), fields, two, ref_pixels[:, None])
-    early = lax.all_to_all(early, ("zl", "yl"), 0, 0, tiled=True)
-    four, two_swap, counts = lax.optimization_barrier((four, two_swap, counts))
-    four_swap = swap(four, even=True)
-    band = pl.pallas_call(
-        band_kernel,
-        out_shape=jax.ShapeDtypeStruct((near, 3 * share + 16, width), BF16),
-        in_specs=[SMEM] + [VMEM] * 6,
-        out_specs=VMEM,
-        cost_estimate=cost(3 * tile_flops, 8 * field_bytes),
-        compiler_params=params,
-    )((mode_index % 2).reshape(1), fields, own_swap, two_swap, four, four_swap, counts)
-    band = lax.all_to_all(band, ("zl", "yl"), 0, 0, tiled=True)
+    )(fields, two, four)
+    parts = pl.pallas_call(
+        parts_kernel,
+        out_shape=jax.ShapeDtypeStruct((near, 5 * share + REF_ROWS, width), BF16),
+        in_specs=[SMEM] + [VMEM] * 9,
+        out_specs=VMEM,
+        cost_estimate=cost(2 * tile_flops, 8 * field_bytes),
+        compiler_params=params,
+    )((mode_index % 2).reshape(1), fields, own_swap, two, two_swap, four, four_swap, counts, diag, same)
+    parts = lax.all_to_all(parts, ("zl", "yl"), 0, 0, tiled=True)
     parts = pl.pallas_call(
         middle_kernel,
         out_shape=jax.ShapeDtypeStruct((dests, 2 * part_cols + 2 * diag_cols + 8, width), BF16),
-        in_specs=[VMEM, VMEM],
+        in_specs=[VMEM],
         out_specs=VMEM,
         cost_estimate=cost(4 * field_bytes, 4 * field_bytes),
         compiler_params=params,
-    )(early, band)
+    )(parts)
     starts = jnp.stack([(pix_index % tile_dests) * part_cols, pix_index * diag_cols])
     parts, starts = lax.optimization_barrier((parts, starts))
     parts = lax.all_to_all(parts, ("zh", "yh"), 0, 0, tiled=True)

time: 99.8 us -> 97.9 us (0.981)
  starting transfers between devices: 33.6 us -> 20.9 us
  waiting for transfers between devices: 24.7 us -> 35.2 us
    all_to_all x2 -> x1, starting transfers between devices: 17 us -> 4.39 us  [shards(): parts = lax.all_to_all(parts, ('zl', 'yl'), 0, 0, tiled=True)]
    ppermute x2, waiting for transfers between devices: 9.2 us -> 18 us  [shift(): return lax.ppermute(array, 'mode', pairs)]
    all_to_all x2 -> x1, waiting for transfers between devices: 14.1 us -> 17.3 us  [shards(): parts = lax.all_to_all(parts, ('zl', 'yl'), 0, 0, tiled=True)]
    ppermute x3, waiting for transfers between devices: 1.48 us -> 0.01 us  [swap(): return lax.ppermute(array, 'mode', pairs)]
    unnamed x6 -> x8, local copies, waits for them, and re-layouts: 1.7 us -> 2.08 us
    pallas_call x2 -> x3, Pallas kernels: 4.13 us -> 3.74 us  [the longest x1 2.16 us: shards(): pl.pallas_call(parts_kernel, out_shape=jax.ShapeDtypeStruct((near, 5 * sh...]
  transfers between devices with their start and end apart: 7 -> 6, of which waited for: 4 -> 3; matrix products, arithmetic and copies ran while one was open for 0% -> 0% of each run, Pallas kernels for 4% -> 2%
where the time goes in v4:
time: 97.9 us; the launch traced here: 96.8 us
  waiting for transfers between devices  35.2 us (36%)
  blocking collectives  30.2 us (31%)
  starting transfers between devices  20.9 us (21%)
  Pallas kernels  7.37 us (8%)
  local copies, waits for them, and re-layouts  2.18 us (2%)
    all_to_all x1, blocking collectives, shards(): parts = lax.all_to_all(parts, ('zh', 'yh'), 0, 0, tiled=True)  30.2 us
    ppermute x2, waiting for transfers between devices, shift(): return lax.ppermute(array, 'mode', pairs)  18 us
    all_to_all x1, waiting for transfers between devices, shards(): parts = lax.all_to_all(parts, ('zl', 'yl'), 0, 0, tiled=True)  17.3 us
    ppermute x2, starting transfers between devices, shift(): return lax.ppermute(array, 'mode', pairs)  11.1 us
    ppermute x3, starting transfers between devices, swap(): return lax.ppermute(array, 'mode', pairs)  5.43 us
    all_to_all x1, starting transfers between devices, shards(): parts = lax.all_to_all(parts, ('zl', 'yl'), 0, 0, tiled=True)  4.39 us
    pallas_call x1, Pallas kernels, shards(): pl.pallas_call(parts_kernel, out_shape=jax.ShapeDtypeStruct((near, 5 * sh...  2.16 us
    pallas_call x1, Pallas kernels, shards(): pl.pallas_call(fields_kernel, out_shape=jax.ShapeDtypeStruct((2, pixel_ro...  2.16 us
  transfers between devices with their start and end apart: 6, of which 3 were waited for; matrix products, arithmetic and copies ran while one was open for 0% of the time, Pallas kernels for 2%

profile of v4, /device:TPU:6, one launch (start us, length us, event | category | flops | bytes accessed | tf_op | source)
XLA Modules:
  0.0 96.8 jit_solution(15204082370139121199)
XLA Ops:
  0.6 0.0 copy-start.3
  0.6 2.2 %shard_map.41.fields_ref.own_ref = bf16[2,512,256]{2,1,0:T(8,128)(2,1)} custom-call(bf16[4,512,256]{2,1,0:T(8,128)(2,1)} %frames_ref.1), custom_call_target="tpu_custom_call" | custom-call | flops 524288 | bytes 1572864 | tf_op jit(solution)/shard_map/pallas_call | solution.py:208
  2.8 1.3 %collective-permute-start.1 = (bf16[2,512,256]{2,1,0:T(8,128)(2,1)}, bf16[2,512,256]{2,1,0:T(8,128)(2,1)S(1)}, u32[]{:S(2)}, u32[]{:S(2)}) collective-permute-start(bf16[2,512,256]{2,1,0:T(8,128)(2,1)} %shard_map.41.fields_ref.own_ref), channel_id=1, source_target_pairs={{1,0},{3,2},{5,4},{7,6},{9,8},{11,10},{13,12},{15,14},{17,16},{19,... | collective-permute-start | bytes 1572872 | tf_op jit(solution)/shard_map/ppermute | solution.py:206
  4.1 2.7 %collective-permute-start = (bf16[2,512,256]{2,1,0:T(8,128)(2,1)}, bf16[2,512,256]{2,1,0:T(8,128)(2,1)S(1)}, u32[]{:S(2)}, u32[]{:S(2)}) collective-permute-start(bf16[2,512,256]{2,1,0:T(8,128)(2,1)} %shard_map.41.fields_ref.own_ref), channel_id=1, source_target_pairs={{2,0},{3,1},{4,2},{5,3},{6,4},{7,5},{0,6},{1,7},{10,8},{11,9},{12,... | collective-permute-start | bytes 1572872 | tf_op jit(solution)/shard_map/ppermute | solution.py:202
  6.8 8.4 %collective-permute-start.2 = (bf16[2,512,256]{2,1,0:T(8,128)(2,1)}, bf16[2,512,256]{2,1,0:T(8,128)(2,1)S(1)}, u32[]{:S(2)}, u32[]{:S(2)}) collective-permute-start(bf16[2,512,256]{2,1,0:T(8,128)(2,1)} %shard_map.41.fields_ref.own_ref), channel_id=1, source_target_pairs={{4,0},{5,1},{6,2},{7,3},{0,4},{1,5},{2,6},{3,7},{12,8},{13,9},{14,... | collective-permute-start | bytes 1572872 | tf_op jit(solution)/shard_map/ppermute | solution.py:202
  15.2 0.0 copy-done.3
  15.2 0.1 copy.4.pixels_ref
  15.3 0.0 copy-start
  15.3 1.0 %copy-done = bf16[2,512,256]{2,1,0:T(8,128)(2,1)S(1)} copy-done((bf16[2,512,256]{2,1,0:T(8,128)(2,1)S(1)}, bf16[2,512,256]{2,1,0:T(8,128)(2,1)}, u32[]{:S(2)}) %copy-start) | copy-done | bytes 524312
  16.4 0.0 copy-start.2
  16.4 0.8 shard_map.42
  17.2 0.0 collective-permute-done.1.own_swap_ref
  17.2 7.2 %collective-permute-done.two_ref = bf16[2,512,256]{2,1,0:T(8,128)(2,1)S(1)} collective-permute-done((bf16[2,512,256]{2,1,0:T(8,128)(2,1)}, bf16[2,512,256]{2,1,0:T(8,128)(2,1)S(1)}, u32[]{:S(2)}, u32[]{:S(2)}) %collective-permute-start) | collective-permute-done | bytes 524320 | tf_op jit(solution)/shard_map/ppermute | solution.py:202
  24.4 2.1 %collective-permute-start.3 = (bf16[2,512,256]{2,1,0:T(8,128)(2,1)S(1)}, bf16[2,512,256]{2,1,0:T(8,128)(2,1)S(1)}, u32[]{:S(2)}, u32[]{:S(2)}) collective-permute-start(bf16[2,512,256]{2,1,0:T(8,128)(2,1)S(1)} %collective-permute-done.two_ref), channel_id=1, source_target_pairs={{0,1},{1,0},{2,3},{3,2},{4,5},{5,4},{6,7},{7,6},{8,9},{9,8},{10,11... | collective-permute-start | bytes 1572872 | tf_op jit(solution)/shard_map/ppermute | solution.py:206
  26.5 10.8 %collective-permute-done.2.four_ref = bf16[2,512,256]{2,1,0:T(8,128)(2,1)S(1)} collective-permute-done((bf16[2,512,256]{2,1,0:T(8,128)(2,1)}, bf16[2,512,256]{2,1,0:T(8,128)(2,1)S(1)}, u32[]{:S(2)}, u32[]{:S(2)}) %collective-permute-start.2) | collective-permute-done | bytes 524320 | tf_op jit(solution)/shard_map/ppermute | solution.py:202
  37.3 0.0 collective-permute-done.3.two_swap_ref
  37.3 2.0 %collective-permute-start.4 = (bf16[2,512,256]{2,1,0:T(8,128)(2,1)S(1)}, bf16[2,512,256]{2,1,0:T(8,128)(2,1)S(1)}, u32[]{:S(2)}, u32[]{:S(2)}) collective-permute-start(bf16[2,512,256]{2,1,0:T(8,128)(2,1)S(1)} %collective-permute-done.2.four_ref), channel_id=1, source_target_pairs={{0,1},{2,3},{4,5},{6,7},{8,9},{10,11},{12,13},{14,15},{16,17},{18,... | collective-permute-start | bytes 1572872 | tf_op jit(solution)/shard_map/ppermute | solution.py:206
  39.4 0.0 copy-start.1
  39.4 1.0 %copy-done.1 = bf16[2,512,256]{2,1,0:T(8,128)(2,1)S(1)} copy-done((bf16[2,512,256]{2,1,0:T(8,128)(2,1)S(1)}, bf16[2,512,256]{2,1,0:T(8,128)(2,1)}, u32[]{:S(2)}) %copy-start.1) | copy-done | bytes 524312
  40.4 0.8 shard_map.43.same_ref
  41.2 0.0 collective-permute-done.4.four_swap_ref
  41.2 0.0 copy-done.2
  41.2 2.2 %shard_map.44 = bf16[4,672,256]{2,1,0:T(8,128)(2,1)} custom-call(s32[1]{0:T(128)} %bitcast.core_ref, bf16[2,512,256]{2,1,0:T(8,128)(2,1)S(1)} %copy-done.2, bf16[2,512,256]{2,1,0:T(8,128)(2,1)S(1)} %collective-permute-done.1.own_swap_ref, bf16[2,512,256]{2,1,0:T(8,128)(2,1)S(1)} %collective-permute-done.two_ref, ...), custom_call_target="tpu_custom_call" | custom-call | flops 536870912 | bytes 4194304 | tf_op jit(solution)/shard_map/pallas_call | solution.py:241
  43.4 4.4 %all-to-all-start = ((bf16[4,672,256]{2,1,0:T(8,128)(2,1)}), bf16[4,672,256]{2,1,0:T(8,128)(2,1)S(1)}, u32[]{:S(2)}, u32[]{:S(2)}) async-start(bf16[4,672,256]{2,1,0:T(8,128)(2,1)} %shard_map.44), calls=%async_computation | async-start | bytes 2752512 | tf_op jit(solution)/shard_map/all_to_all | solution.py:249
  47.8 0.1 pad_add_fusion.refs_0_
  47.8 17.3 %all-to-all-done.parts_ref = bf16[4,672,256]{2,1,0:T(8,128)(2,1)S(1)} async-done(((bf16[4,672,256]{2,1,0:T(8,128)(2,1)}), bf16[4,672,256]{2,1,0:T(8,128)(2,1)S(1)}, u32[]{:S(2)}, u32[]{:S(2)}) %all-to-all-start) | async-done | bytes 1376288 | tf_op jit(solution)/shard_map/all_to_all | solution.py:249
  65.1 0.2 shard_map.45
  65.3 30.2 %all_to_all.10.refs_1_ = bf16[16,48,256]{2,1,0:T(8,128)(2,1)S(1)} all-to-all(bf16[16,48,256]{2,1,0:T(8,128)(2,1)S(1)} %shard_map.45), channel_id=1, replica_groups=mesh['zh'=4,'zl'=2,'yh'=4,'yl'=2,'mode'=8] {'zh','yh'}, dimensions={0} | all-to-all | bytes 786432 | tf_op jit(solution)/shard_map/all_to_all | solution.py:260
  95.5 1.3 %shard_map.46 = (f32[2,16,256]{2,1,0:T(8,128)}, f32[2,4,256]{2,1,0:T(4,128)}) custom-call(s32[2]{0:T(128)S(1)} %pad_add_fusion.refs_0_, bf16[16,48,256]{2,1,0:T(8,128)(2,1)S(1)} %all_to_all.10.refs_1_), custom_call_target="tpu_custom_call" | custom-call | flops 524288 | bytes 524288 | tf_op jit(solution)/shard_map/pallas_call | solution.py:263
Async XLA Ops:
  0.6 14.6 %copy-start.3 = (s32[64]{0:T(128)S(1)}, s32[64]{0:T(128)}, u32[]{:S(2)}) copy-start(s32[64]{0:T(128)} %param.3) | copy-start | bytes 772
  2.8 14.4 %collective-permute-start.1 = (bf16[2,512,256]{2,1,0:T(8,128)(2,1)}, bf16[2,512,256]{2,1,0:T(8,128)(2,1)S(1)}, u32[]{:S(2)}, u32[]{:S(2)}) collective-permute-start(bf16[2,512,256]{2,1,0:T(8,128)(2,1)} %shard_map.41.fields_ref.own_ref), channel_id=1, source_target_pairs={{1,0},{3,2},{5,4},{7,6},{9,8},{11,10},{13,12},{15,14},{17,16},{19,... | collective-permute-start | bytes 1572872 | tf_op jit(solution)/shard_map/ppermute | solution.py:206
  4.1 20.4 %collective-permute-start = (bf16[2,512,256]{2,1,0:T(8,128)(2,1)}, bf16[2,512,256]{2,1,0:T(8,128)(2,1)S(1)}, u32[]{:S(2)}, u32[]{:S(2)}) collective-permute-start(bf16[2,512,256]{2,1,0:T(8,128)(2,1)} %shard_map.41.fields_ref.own_ref), channel_id=1, source_target_pairs={{2,0},{3,1},{4,2},{5,3},{6,4},{7,5},{0,6},{1,7},{10,8},{11,9},{12,... | collective-permute-start | bytes 1572872 | tf_op jit(solution)/shard_map/ppermute | solution.py:202
  6.8 30.5 %collective-permute-start.2 = (bf16[2,512,256]{2,1,0:T(8,128)(2,1)}, bf16[2,512,256]{2,1,0:T(8,128)(2,1)S(1)}, u32[]{:S(2)}, u32[]{:S(2)}) collective-permute-start(bf16[2,512,256]{2,1,0:T(8,128)(2,1)} %shard_map.41.fields_ref.own_ref), channel_id=1, source_target_pairs={{4,0},{5,1},{6,2},{7,3},{0,4},{1,5},{2,6},{3,7},{12,8},{13,9},{14,... | collective-permute-start | bytes 1572872 | tf_op jit(solution)/shard_map/ppermute | solution.py:202
  15.3 1.0 %copy-start = (bf16[2,512,256]{2,1,0:T(8,128)(2,1)S(1)}, bf16[2,512,256]{2,1,0:T(8,128)(2,1)}, u32[]{:S(2)}) copy-start(bf16[2,512,256]{2,1,0:T(8,128)(2,1)} %shard_map.41.fields_ref.own_ref) | copy-start | bytes 1572868
  16.4 24.8 %copy-start.2 = (bf16[2,512,256]{2,1,0:T(8,128)(2,1)S(1)}, bf16[2,512,256]{2,1,0:T(8,128)(2,1)}, u32[]{:S(2)}) copy-start(bf16[2,512,256]{2,1,0:T(8,128)(2,1)} %shard_map.41.fields_ref.own_ref) | copy-start | bytes 1572868
  24.4 12.9 %collective-permute-start.3 = (bf16[2,512,256]{2,1,0:T(8,128)(2,1)S(1)}, bf16[2,512,256]{2,1,0:T(8,128)(2,1)S(1)}, u32[]{:S(2)}, u32[]{:S(2)}) collective-permute-start(bf16[2,512,256]{2,1,0:T(8,128)(2,1)S(1)} %collective-permute-done.two_ref), channel_id=1, source_target_pairs={{0,1},{1,0},{2,3},{3,2},{4,5},{5,4},{6,7},{7,6},{8,9},{9,8},{10,11... | collective-permute-start | bytes 1572872 | tf_op jit(solution)/shard_map/ppermute | solution.py:206
  37.3 3.9 %collective-permute-start.4 = (bf16[2,512,256]{2,1,0:T(8,128)(2,1)S(1)}, bf16[2,512,256]{2,1,0:T(8,128)(2,1)S(1)}, u32[]{:S(2)}, u32[]{:S(2)}) collective-permute-start(bf16[2,512,256]{2,1,0:T(8,128)(2,1)S(1)} %collective-permute-done.2.four_ref), channel_id=1, source_target_pairs={{0,1},{2,3},{4,5},{6,7},{8,9},{10,11},{12,13},{14,15},{16,17},{18,... | collective-permute-start | bytes 1572872 | tf_op jit(solution)/shard_map/ppermute | solution.py:206
  39.4 1.0 %copy-start.1 = (bf16[2,512,256]{2,1,0:T(8,128)(2,1)S(1)}, bf16[2,512,256]{2,1,0:T(8,128)(2,1)}, u32[]{:S(2)}) copy-start(bf16[2,512,256]{2,1,0:T(8,128)(2,1)} %shard_map.41.fields_ref.own_ref) | copy-start | bytes 1572868
  43.4 21.7 %all-to-all-start = ((bf16[4,672,256]{2,1,0:T(8,128)(2,1)}), bf16[4,672,256]{2,1,0:T(8,128)(2,1)S(1)}, u32[]{:S(2)}, u32[]{:S(2)}) async-start(bf16[4,672,256]{2,1,0:T(8,128)(2,1)} %shard_map.44), calls=%async_computation | async-start | bytes 2752512 | tf_op jit(solution)/shard_map/all_to_all | solution.py:249

commit v5 on v1

v5 whole, which is shorter than its diff:
```python
import math

import jax
import jax.numpy as jnp
from jax import lax
from jax.experimental import pallas as pl
from jax.experimental.pallas import tpu as pltpu
from jax.sharding import PartitionSpec as P

BF16 = jnp.bfloat16
F32 = jnp.float32
VMEM = pl.BlockSpec(memory_space=pltpu.VMEM)
SMEM = pl.BlockSpec(memory_space=pltpu.SMEM)
HBM = pl.BlockSpec(memory_space=pltpu.HBM)
REF_ROWS = 8


def cost(flops, nbytes):
    return pl.CostEstimate(flops=flops, bytes_accessed=nbytes, transcendentals=0)


def dot_pixels(cols, rows):
    return lax.dot_general(cols, rows, (((0,), (0,)), ((), ())), preferred_element_type=F32)


def gram_t(col_real, col_imag, row_real, row_imag, row_imag_neg):
    real = dot_pixels(col_real, row_real) + dot_pixels(col_imag, row_imag)
    imag = dot_pixels(col_imag, row_real) + dot_pixels(col_real, row_imag_neg)
    return real, imag


def fields_kernel(base_ref, frames_ref, pixels_ref, fields_ref, counts_ref, held_ref, list_ref, sems):
    chunks = sems.shape[0] - 1
    size = held_ref.shape[1] // chunks
    entries = pltpu.make_async_copy(pixels_ref, list_ref, sems.at[chunks])
    entries.start()
    copies = []
    for chunk in range(chunks):
        rows = pl.ds(chunk * size, size)
        copies.append(pltpu.make_async_copy(frames_ref.at[:, rows, :], held_ref.at[:, rows, :], sems.at[chunk]))
        copies[-1].start()
    entries.wait()
    position = base_ref[0] + lax.broadcasted_iota(jnp.int32, counts_ref.shape, 1)
    counts = jnp.zeros(counts_ref.shape, F32)
    for entry in range(list_ref.shape[0]):
        counts += jnp.where(position == list_ref[entry], 1.0, 0.0)
    counts_ref[...] = counts.astype(BF16)
    for chunk in range(chunks):
        rows = pl.ds(chunk * size, size)
        copies[chunk].wait()
        fields_ref[0, rows, :] = (held_ref[0, rows, :].astype(F32) - held_ref[2, rows, :].astype(F32)).astype(BF16)
        fields_ref[1, rows, :] = (held_ref[3, rows, :].astype(F32) - held_ref[1, rows, :].astype(F32)).astype(BF16)


def early_kernel(fields_ref, counts_ref, out_ref, held_ref, sem):
    dests, slot_rows, width = out_ref.shape
    diag_cols = width // dests
    real, imag = fields_ref[0], fields_ref[1]
    counts = counts_ref[...]
    ref_real = jnp.dot(counts, real, preferred_element_type=F32)
    ref_imag = jnp.dot(counts, imag, preferred_element_type=F32)
    row = lax.broadcasted_iota(jnp.int32, ref_real.shape, 0)
    high_real = ref_real.astype(BF16).astype(F32)
    high_imag = ref_imag.astype(BF16).astype(F32)
    refs = jnp.where(row == 0, high_real, ref_real - high_real)
    refs = jnp.where(row == 2, high_imag, refs)
    refs = jnp.where(row == 3, ref_imag - high_imag, refs)
    refs = jnp.where(row > 3, 0.0, refs)
    diag_real, diag_imag = gram_t(real, imag, real, imag, -imag)
    rows = jnp.concatenate(
        [diag_real, diag_imag, refs, jnp.zeros((128 - refs.shape[0], width), F32)], axis=0
    ).astype(BF16)
    slot_at = lax.broadcasted_iota(jnp.int32, (dests * slot_rows, rows.shape[0]), 0)
    source = lax.broadcasted_iota(jnp.int32, (dests * slot_rows, rows.shape[0]), 1)
    dest, slot = slot_at // slot_rows, slot_at % slot_rows
    diag_source = (slot // diag_cols) * width + dest * diag_cols + slot % diag_cols
    wanted = jnp.where(slot < 2 * diag_cols, diag_source, 2 * width + slot - 2 * diag_cols)
    pick = jnp.where(wanted == source, 1.0, 0.0).astype(BF16)
    placed = jnp.dot(pick, rows, preferred_element_type=F32)
    held_ref[...] = placed.reshape(dests, slot_rows, width).astype(BF16)
    copy = pltpu.make_async_copy(held_ref, out_ref, sem)
    copy.start()
    copy.wait()


def choose_kernel(core_ref, own_ref, two_ref, four_ref, _, one_ref, three_ref):
    first_core = core_ref[0] == 0

    @pl.when(first_core)
    def _():
        one_ref[...] = two_ref[...]
        three_ref[...] = four_ref[...]

    @pl.when(jnp.logical_not(first_core))
    def _():
        one_ref[...] = own_ref[...]
        three_ref[...] = two_ref[...]


def tile_pair(own_ref, blocks, out_ref, first, held_ref, sems):
    row_real, row_imag = own_ref[0], own_ref[1]
    row_imag_neg = -row_imag
    _, tile_dests, rows, width = held_ref.shape
    part_cols = rows // 2
    copies = []
    for at, block in enumerate(blocks):
        tile = gram_t(block[0], block[1], row_real, row_imag, row_imag_neg)
        for c, part in enumerate(tile):
            cut = part.reshape(tile_dests, part_cols, width).astype(BF16)
            held_ref[at, :, c * part_cols : (c + 1) * part_cols, :] = cut
        dests = pl.ds((2 * at + first) * tile_dests, tile_dests)
        copies.append(pltpu.make_async_copy(held_ref.at[at], out_ref.at[dests], sems.at[at]))
        copies[-1].start()
    for copy in copies:
        copy.wait()


def same_core_kernel(own_ref, two_ref, four_ref, out_ref, held_ref, sems):
    tile_pair(own_ref, (two_ref, four_ref), out_ref, 1, held_ref, sems)


def other_core_kernel(own_ref, one_ref, three_ref, _, out_ref, held_ref, sems):
    tile_pair(own_ref, (one_ref, three_ref), out_ref, 0, held_ref, sems)


def unit_phase(real, imag):
    magnitude = jnp.maximum(jnp.sqrt(real * real + imag * imag), 1.0)
    return real / magnitude, imag / magnitude


def pick_lanes(values, start, count):
    lanes = values.shape[1]
    lane = lax.broadcasted_iota(jnp.int32, (count, lanes), 1)
    row = lax.broadcasted_iota(jnp.int32, (count, lanes), 0)
    return jnp.sum(jnp.where(lane == start + row, values, 0.0), axis=1, keepdims=True)


def rotate(real, imag, row_phase, col_phase, pixel_scale):
    unit_real = row_phase[0] * col_phase[0] + row_phase[1] * col_phase[1]
    unit_imag = row_phase[1] * col_phase[0] - row_phase[0] * col_phase[1]
    return (
        (unit_real * real - unit_imag * imag) * pixel_scale,
        (unit_real * imag + unit_imag * real) * pixel_scale,
    )


def diag_kernel(pixel_scale, starts_ref, early_ref, diag_out, refs_out):
    diag_cols = diag_out.shape[1]
    sums = jnp.sum(early_ref[...].astype(F32), axis=0)
    diag, terms = sums[: 2 * diag_cols], sums[2 * diag_cols :]
    real, imag = terms[0:1] + terms[1:2], terms[2:3] + terms[3:4]
    refs_out[0:1, :] = real
    refs_out[1:2, :] = imag
    row_phase = unit_phase(real, imag)
    diag_phase = [pick_lanes(part, starts_ref[1], diag_cols) for part in row_phase]
    diag_out[0], diag_out[1] = rotate(diag[:diag_cols], diag[diag_cols:], row_phase, diag_phase, pixel_scale)


def final_kernel(pixel_scale, starts_ref, own_ref, other_ref, band_ref, band_out):
    part_cols = band_out.shape[1]
    band = jnp.sum(band_ref[...].astype(F32), axis=0)
    row_phase = unit_phase(own_ref[0:1, :], own_ref[1:2, :])
    other_phase = unit_phase(other_ref[0:1, :], other_ref[1:2, :])
    col_phase = [pick_lanes(part, starts_ref[0], part_cols) for part in other_phase]
    band_out[0], band_out[1] = rotate(band[:part_cols], band[part_cols:], row_phase, col_phase, pixel_scale)


def shards(frames, ref_pixels):
    pix_count = lax.axis_size("pix")
    mode_count = lax.axis_size("mode")
    pix_index = lax.axis_index("pix")
    mode_index = lax.axis_index("mode")
    pixel_rows, width = frames.shape[1:]
    tiles = mode_count // 2
    tile_dests = pix_count // tiles
    part_cols = width // tile_dests
    diag_cols = width // pix_count
    slot_rows = 2 * diag_cols + REF_ROWS
    field_bytes = 2 * pixel_rows * width * 2
    tile_flops = 8 * pixel_rows * width * width
    params = pltpu.CompilerParams(vmem_limit_bytes=32 << 20)

    def shift(array, step):
        pairs = [((m + step) % mode_count, m) for m in range(mode_count)]
        return lax.ppermute(array, "mode", pairs)

    base = (pix_index * pixel_rows).reshape(1)
    core = (mode_index % 2).reshape(1)
    starts = jnp.stack([(pix_index % tile_dests) * part_cols, pix_index * diag_cols])
    scale = 1.0 / math.sqrt(pix_count * pixel_rows)
    fields, counts = pl.pallas_call(
        fields_kernel,
        out_shape=(pltpu.VMEM((2, pixel_rows, width), BF16), pltpu.VMEM((8, pixel_rows), BF16)),
        in_specs=[SMEM, HBM, HBM],
        out_specs=(VMEM, VMEM),
        scratch_shapes=[
            pltpu.VMEM(frames.shape, BF16),
            pltpu.SMEM(ref_pixels.shape, jnp.int32),
            pltpu.SemaphoreType.DMA((5,)),
        ],
        cost_estimate=cost(4 * pixel_rows * width, 3 * field_bytes),
    )(base, frames, ref_pixels)
    two = shift(fields, 2)
    four = shift(fields, 4)
    early = pl.pallas_call(
        early_kernel,
        out_shape=jax.ShapeDtypeStruct((pix_count, slot_rows, width), BF16),
        in_specs=[VMEM, VMEM],
        out_specs=HBM,
        scratch_shapes=[pltpu.VMEM((pix_count, slot_rows, width), BF16), pltpu.SemaphoreType.DMA],
        cost_estimate=cost(4 * tile_flops, 2 * field_bytes),
        compiler_params=params,
    )(fields, counts)

    one, three = pl.pallas_call(
        choose_kernel,
        out_shape=(jax.ShapeDtypeStruct(fields.shape, BF16),) * 2,
        in_specs=[SMEM] + [VMEM] * 3 + [HBM],
        out_specs=(VMEM, VMEM),
        cost_estimate=cost(0, 4 * field_bytes),
        compiler_params=params,
    )(core, fields, two, four, early)
    early = lax.all_to_all(early, "pix", 0, 0, tiled=True)
    swap = [(m, m ^ 1) for m in range(mode_count)]
    one, three = lax.ppermute(one, "mode", swap), lax.ppermute(three, "mode", swap)
    band_shape = jax.ShapeDtypeStruct((pix_count, 2 * part_cols, width), BF16)
    scratch = [pltpu.VMEM((2, tile_dests, 2 * part_cols, width), BF16), pltpu.SemaphoreType.DMA((2,))]
    same = pl.pallas_call(
        same_core_kernel,
        out_shape=band_shape,
        in_specs=[VMEM] * 3,
        out_specs=HBM,
        scratch_shapes=scratch,
        cost_estimate=cost(2 * tile_flops, 4 * field_bytes),
        compiler_params=params,
    )(fields, two, four)
    band = pl.pallas_call(
        other_core_kernel,
        out_shape=band_shape,
        in_specs=[VMEM, VMEM, VMEM, HBM],
        out_specs=HBM,
        scratch_shapes=scratch,
        input_output_aliases={3: 0},
        cost_estimate=cost(2 * tile_flops, 4 * field_bytes),
        compiler_params=params,
    )(fields, one, three, same)
    band = lax.all_to_all(band, "pix", 0, 0, tiled=True)

    diag_out, own_ref = pl.pallas_call(
        lambda *refs: diag_kernel(scale, *refs),
        out_shape=(jax.ShapeDtypeStruct((2, diag_cols, width), F32), jax.ShapeDtypeStruct((2, width), F32)),
        in_specs=[SMEM, VMEM],
        out_specs=(VMEM, VMEM),
        cost_estimate=cost(field_bytes, field_bytes),
        compiler_params=params,
    )(starts, early)
    pairs = []
    for p in range(pix_count):
        step = p // tile_dests + 1
        for m in range(mode_count):
            pairs.append((p * mode_count + (m + step) % mode_count, p * mode_count + m))
    other_ref = lax.ppermute(own_ref, ("pix", "mode"), pairs)
    band_out = pl.pallas_call(
        lambda *refs: final_kernel(scale, *refs),
        out_shape=jax.ShapeDtypeStruct((2, part_cols, width), F32),
        in_specs=[SMEM] + [VMEM] * 3,
        out_specs=VMEM,
        cost_estimate=cost(2 * field_bytes, 2 * field_bytes),
        compiler_params=params,
    )(starts, own_ref, other_ref, band)
    return jnp.transpose(band_out, (0, 2, 1)), jnp.transpose(diag_out, (0, 2, 1))


def solution(mesh):
    return jax.shard_map(
        shards,
        mesh=mesh,
        in_specs=(P(None, "pix", "mode"), P()),
        out_specs=(P(None, "mode", "pix"), P(None, "mode", "pix")),
        check_vma=False,
    )
```

time: 87.9 us -> 86.3 us (0.982)
  local copies, waits for them, and re-layouts: 1.81 us -> 0 us
  waiting for transfers between devices: 40.4 us -> 38.8 us
  Pallas kernels: 7.73 us -> 8.82 us
  starting transfers between devices: 36.5 us -> 37.4 us
    ppermute x2, waiting for transfers between devices: 1.98 us -> 4.54 us  [shift(): return lax.ppermute(array, 'mode', pairs)]
    unnamed x6 -> x0, local copies, waits for them, and re-layouts: 1.7 us -> none
    all_to_all x1, starting transfers between devices: 7.76 us -> 9.32 us  [shards(): band = lax.all_to_all(band, 'pix', 0, 0, tiled=True)]
    all_to_all x1, waiting for transfers between devices: 8.85 us -> 7.3 us  [shards(): early = lax.all_to_all(early, 'pix', 0, 0, tiled=True)]
    ppermute x2, waiting for transfers between devices: 1.51 us -> 0.03 us  [the longest x1 0.03 us: shards(): lax.ppermute(three, 'mode', swap)]
    all_to_all x1, waiting for transfers between devices: 26.9 us -> 25.6 us  [shards(): band = lax.all_to_all(band, 'pix', 0, 0, tiled=True)]
    pallas_call x3 -> x6, Pallas kernels: 5.81 us -> 6.94 us  [the longest x1 1.47 us: shards(): pl.pallas_call(other_core_kernel, out_shape=band_shape, in_specs=[VMEM, V...]
  transfers between devices with their start and end apart: 7 -> 7, of which waited for: 5 -> 4; matrix products, arithmetic and copies ran while one was open for 0% -> 0% of each run, Pallas kernels for 5% -> 7%
where the time goes in v5:
time: 86.3 us; the launch traced here: 85.8 us
  waiting for transfers between devices  38.8 us (45%)
  starting transfers between devices  37.4 us (43%)
  Pallas kernels  8.82 us (10%)
    all_to_all x1, waiting for transfers between devices, shards(): band = lax.all_to_all(band, 'pix', 0, 0, tiled=True)  25.6 us
    all_to_all x1, starting transfers between devices, shards(): early = lax.all_to_all(early, 'pix', 0, 0, tiled=True)  11.3 us
    ppermute x2, starting transfers between devices, shift(): return lax.ppermute(array, 'mode', pairs)  10.5 us
    all_to_all x1, starting transfers between devices, shards(): band = lax.all_to_all(band, 'pix', 0, 0, tiled=True)  9.32 us
    all_to_all x1, waiting for transfers between devices, shards(): early = lax.all_to_all(early, 'pix', 0, 0, tiled=True)  7.3 us
    ppermute x2, waiting for transfers between devices, shift(): return lax.ppermute(array, 'mode', pairs)  4.54 us
    ppermute x1, starting transfers between devices, shards(): lax.ppermute(three, 'mode', swap)  2.41 us
    ppermute x1, starting transfers between devices, shards(): lax.ppermute(one, 'mode', swap)  1.92 us
  transfers between devices with their start and end apart: 7, of which 4 were waited for; matrix products, arithmetic and copies ran while one was open for 0% of the time, Pallas kernels for 7%

profile of v5, /device:TPU:6, one launch (start us, length us, event | category | flops | bytes accessed | tf_op | source)
XLA Modules:
  0.0 85.8 jit_solution(6945433642319471065)
XLA Ops:
  0.6 1.3 %shard_map.41 = (bf16[2,512,256]{2,1,0:T(8,128)(2,1)S(1)}, bf16[8,512]{1,0:T(8,128)(2,1)S(1)}) custom-call(s32[1]{0:T(128)} %bitcast.2.base_ref, bf16[4,512,256]{2,1,0:T(8,128)(2,1)} %frames_ref.1, s32[64]{0:T(128)} %pixels_ref.1), custom_call_target="tpu_custom_call" | custom-call | flops 524288 | bytes 1572864 | tf_op jit(solution)/shard_map/pallas_call | solution.py:191
  1.9 3.3 %collective-permute-start.2 = (bf16[2,512,256]{2,1,0:T(8,128)(2,1)S(1)}, bf16[2,512,256]{2,1,0:T(8,128)(2,1)S(1)}, u32[]{:S(2)}, u32[]{:S(2)}) collective-permute-start(bf16[2,512,256]{2,1,0:T(8,128)(2,1)S(1)} %get-tuple-element.8.fields_ref.own_ref), channel_id=1, source_target_pairs={{4,0},{5,1},{6,2},{7,3},{0,4},{1,5},{2,6},{3,7},{12,8},{13,9},{14,... | collective-permute-start | bytes 1572872 | tf_op jit(solution)/shard_map/ppermute | solution.py:185
  5.2 7.2 %collective-permute-start.1 = (bf16[2,512,256]{2,1,0:T(8,128)(2,1)S(1)}, bf16[2,512,256]{2,1,0:T(8,128)(2,1)S(1)}, u32[]{:S(2)}, u32[]{:S(2)}) collective-permute-start(bf16[2,512,256]{2,1,0:T(8,128)(2,1)S(1)} %get-tuple-element.8.fields_ref.own_ref), channel_id=1, source_target_pairs={{2,0},{3,1},{4,2},{5,3},{6,4},{7,5},{0,6},{1,7},{10,8},{11,9},{12,... | collective-permute-start | bytes 1572872 | tf_op jit(solution)/shard_map/ppermute | solution.py:185
  12.4 1.9 %shard_map.42._ = bf16[64,16,256]{2,1,0:T(8,128)(2,1)} custom-call(bf16[2,512,256]{2,1,0:T(8,128)(2,1)S(1)} %get-tuple-element.8.fields_ref.own_ref, bf16[8,512]{1,0:T(8,128)(2,1)S(1)} %get-tuple-element.9.counts_ref), custom_call_target="tpu_custom_call" | custom-call | flops 1073741824 | bytes 1048576 | tf_op jit(solution)/shard_map/pallas_call | solution.py:205
  14.3 11.3 %all-to-all-start = ((bf16[64,16,256]{2,1,0:T(8,128)(2,1)}), bf16[64,16,256]{2,1,0:T(8,128)(2,1)S(1)}, u32[]{:S(2)}, u32[]{:S(2)}) async-start(bf16[64,16,256]{2,1,0:T(8,128)(2,1)} %shard_map.42._), calls=%async_computation | async-start | bytes 1048576 | tf_op jit(solution)/shard_map/all_to_all | solution.py:223
  25.7 0.0 collective-permute-done.2.four_ref
  25.7 4.5 %collective-permute-done.1.two_ref = bf16[2,512,256]{2,1,0:T(8,128)(2,1)S(1)} collective-permute-done((bf16[2,512,256]{2,1,0:T(8,128)(2,1)S(1)}, bf16[2,512,256]{2,1,0:T(8,128)(2,1)S(1)}, u32[]{:S(2)}, u32[]{:S(2)}) %collective-permute-start.1) | collective-permute-done | bytes 524320 | tf_op jit(solution)/shard_map/ppermute | solution.py:185
  30.2 0.1 shard_map.44
  30.3 1.9 %collective-permute-start.3 = (bf16[2,512,256]{2,1,0:T(8,128)(2,1)S(1)}, bf16[2,512,256]{2,1,0:T(8,128)(2,1)S(1)}, u32[]{:S(2)}, u32[]{:S(2)}) collective-permute-start(bf16[2,512,256]{2,1,0:T(8,128)(2,1)S(1)} %get-tuple-element.11), channel_id=1, source_target_pairs={{0,1},{1,0},{2,3},{3,2},{4,5},{5,4},{6,7},{7,6},{8,9},{9,8},{10,11... | collective-permute-start | bytes 1572872 | tf_op jit(solution)/shard_map/ppermute | solution.py:225
  32.2 2.4 %collective-permute-start.4 = (bf16[2,512,256]{2,1,0:T(8,128)(2,1)S(1)}, bf16[2,512,256]{2,1,0:T(8,128)(2,1)S(1)}, u32[]{:S(2)}, u32[]{:S(2)}) collective-permute-start(bf16[2,512,256]{2,1,0:T(8,128)(2,1)S(1)} %get-tuple-element.12), channel_id=1, source_target_pairs={{0,1},{1,0},{2,3},{3,2},{4,5},{5,4},{6,7},{7,6},{8,9},{9,8},{10,11... | collective-permute-start | bytes 1572872 | tf_op jit(solution)/shard_map/ppermute | solution.py:225
  34.6 1.5 %shard_map.45._ = bf16[64,32,256]{2,1,0:T(8,128)(2,1)} custom-call(bf16[2,512,256]{2,1,0:T(8,128)(2,1)S(1)} %get-tuple-element.8.fields_ref.own_ref, bf16[2,512,256]{2,1,0:T(8,128)(2,1)S(1)} %collective-permute-done.1.two_ref, bf16[2,512,256]{2,1,0:T(8,128)(2,1)S(1)} %collective-permute-done.2.four_ref), custom_call_target="tpu_custom_call" | custom-call | flops 536870912 | bytes 2097152 | tf_op jit(solution)/shard_map/pallas_call | solution.py:228
  36.1 0.0 collective-permute-done.3.one_ref
  36.1 0.0 collective-permute-done.4.three_ref
  36.1 1.5 %shard_map.46 = bf16[64,32,256]{2,1,0:T(8,128)(2,1)} custom-call(bf16[2,512,256]{2,1,0:T(8,128)(2,1)S(1)} %get-tuple-element.8.fields_ref.own_ref, bf16[2,512,256]{2,1,0:T(8,128)(2,1)S(1)} %collective-permute-done.3.one_ref, bf16[2,512,256]{2,1,0:T(8,128)(2,1)S(1)} %collective-permute-done.4.three_ref, ...), custom_call_target="tpu_custom_call", output_to_operand_aliasing={{}: (3, {})} | custom-call | flops 536870912 | bytes 2097152 | tf_op jit(solution)/shard_map/pallas_call | solution.py:237
  37.6 7.3 %all-to-all-done.refs_1_ = bf16[64,16,256]{2,1,0:T(8,128)(2,1)S(1)} async-done(((bf16[64,16,256]{2,1,0:T(8,128)(2,1)}), bf16[64,16,256]{2,1,0:T(8,128)(2,1)S(1)}, u32[]{:S(2)}, u32[]{:S(2)}) %all-to-all-start) | async-done | bytes 524320 | tf_op jit(solution)/shard_map/all_to_all | solution.py:223
  44.9 9.3 %all-to-all-start.1 = ((bf16[64,32,256]{2,1,0:T(8,128)(2,1)}), bf16[64,32,256]{2,1,0:T(8,128)(2,1)S(1)}, u32[]{:S(2)}, u32[]{:S(2)}) async-start(bf16[64,32,256]{2,1,0:T(8,128)(2,1)} %shard_map.46), calls=%async_computation.1 | async-start | bytes 2097152 | tf_op jit(solution)/shard_map/all_to_all | solution.py:247
  54.3 0.1 pad_add_fusion.refs_0_
  54.3 1.3 %shard_map.43 = (f32[2,4,256]{2,1,0:T(4,128)}, f32[2,256]{1,0:T(2,128)S(1)}) custom-call(s32[2]{0:T(128)S(1)} %pad_add_fusion.refs_0_, bf16[64,16,256]{2,1,0:T(8,128)(2,1)S(1)} %all-to-all-done.refs_1_), custom_call_target="tpu_custom_call" | custom-call | flops 524288 | bytes 524288 | tf_op jit(solution)/shard_map/pallas_call | solution.py:249
  55.7 1.9 %collective-permute-start = (f32[2,256]{1,0:T(2,128)S(1)}, f32[2,256]{1,0:T(2,128)S(1)}, u32[]{:S(2)}, u32[]{:S(2)}) collective-permute-start(f32[2,256]{1,0:T(2,128)S(1)} %get-tuple-element.10.refs_1_), channel_id=1, source_target_pairs={{1,0},{2,1},{3,2},{4,3},{5,4},{6,5},{7,6},{0,7},{9,8},{10,9},{11,1... | collective-permute-start | bytes 6152 | tf_op jit(solution)/shard_map/ppermute | solution.py:262
  57.6 1.3 %collective-permute-done.refs_2_ = f32[2,256]{1,0:T(2,128)S(1)} collective-permute-done((f32[2,256]{1,0:T(2,128)S(1)}, f32[2,256]{1,0:T(2,128)S(1)}, u32[]{:S(2)}, u32[]{:S(2)}) %collective-permute-start) | collective-permute-done | bytes 2080 | tf_op jit(solution)/shard_map/ppermute | solution.py:262
  58.9 25.6 %all-to-all-done.1.refs_3_ = bf16[64,32,256]{2,1,0:T(8,128)(2,1)S(1)} async-done(((bf16[64,32,256]{2,1,0:T(8,128)(2,1)}), bf16[64,32,256]{2,1,0:T(8,128)(2,1)S(1)}, u32[]{:S(2)}, u32[]{:S(2)}) %all-to-all-start.1) | async-done | bytes 1048608 | tf_op jit(solution)/shard_map/all_to_all | solution.py:247
  84.5 1.3 %shard_map.47 = f32[2,16,256]{2,1,0:T(8,128)} custom-call(s32[2]{0:T(128)S(1)} %pad_add_fusion.refs_0_, f32[2,256]{1,0:T(2,128)S(1)} %get-tuple-element.10.refs_1_, f32[2,256]{1,0:T(2,128)S(1)} %collective-permute-done.refs_2_, bf16[64,32,256]{2,1,0:T(8,128)(2,1)S(1)} %all-to-all-done.1.refs_3_), custom_call_target="tpu_custom_call" | custom-call | flops 1048576 | bytes 1048576 | tf_op jit(solution)/shard_map/pallas_call | solution.py:263
Async XLA Ops:
  1.9 23.8 %collective-permute-start.2 = (bf16[2,512,256]{2,1,0:T(8,128)(2,1)S(1)}, bf16[2,512,256]{2,1,0:T(8,128)(2,1)S(1)}, u32[]{:S(2)}, u32[]{:S(2)}) collective-permute-start(bf16[2,512,256]{2,1,0:T(8,128)(2,1)S(1)} %get-tuple-element.8.fields_ref.own_ref), channel_id=1, source_target_pairs={{4,0},{5,1},{6,2},{7,3},{0,4},{1,5},{2,6},{3,7},{12,8},{13,9},{14,... | collective-permute-start | bytes 1572872 | tf_op jit(solution)/shard_map/ppermute | solution.py:185
  5.2 25.0 %collective-permute-start.1 = (bf16[2,512,256]{2,1,0:T(8,128)(2,1)S(1)}, bf16[2,512,256]{2,1,0:T(8,128)(2,1)S(1)}, u32[]{:S(2)}, u32[]{:S(2)}) collective-permute-start(bf16[2,512,256]{2,1,0:T(8,128)(2,1)S(1)} %get-tuple-element.8.fields_ref.own_ref), channel_id=1, source_target_pairs={{2,0},{3,1},{4,2},{5,3},{6,4},{7,5},{0,6},{1,7},{10,8},{11,9},{12,... | collective-permute-start | bytes 1572872 | tf_op jit(solution)/shard_map/ppermute | solution.py:185
  14.3 30.6 %all-to-all-start = ((bf16[64,16,256]{2,1,0:T(8,128)(2,1)}), bf16[64,16,256]{2,1,0:T(8,128)(2,1)S(1)}, u32[]{:S(2)}, u32[]{:S(2)}) async-start(bf16[64,16,256]{2,1,0:T(8,128)(2,1)} %shard_map.42._), calls=%async_computation | async-start | bytes 1048576 | tf_op jit(solution)/shard_map/all_to_all | solution.py:223
  30.3 5.8 %collective-permute-start.3 = (bf16[2,512,256]{2,1,0:T(8,128)(2,1)S(1)}, bf16[2,512,256]{2,1,0:T(8,128)(2,1)S(1)}, u32[]{:S(2)}, u32[]{:S(2)}) collective-permute-start(bf16[2,512,256]{2,1,0:T(8,128)(2,1)S(1)} %get-tuple-element.11), channel_id=1, source_target_pairs={{0,1},{1,0},{2,3},{3,2},{4,5},{5,4},{6,7},{7,6},{8,9},{9,8},{10,11... | collective-permute-start | bytes 1572872 | tf_op jit(solution)/shard_map/ppermute | solution.py:225
  32.2 3.9 %collective-permute-start.4 = (bf16[2,512,256]{2,1,0:T(8,128)(2,1)S(1)}, bf16[2,512,256]{2,1,0:T(8,128)(2,1)S(1)}, u32[]{:S(2)}, u32[]{:S(2)}) collective-permute-start(bf16[2,512,256]{2,1,0:T(8,128)(2,1)S(1)} %get-tuple-element.12), channel_id=1, source_target_pairs={{0,1},{1,0},{2,3},{3,2},{4,5},{5,4},{6,7},{7,6},{8,9},{9,8},{10,11... | collective-permute-start | bytes 1572872 | tf_op jit(solution)/shard_map/ppermute | solution.py:225
  44.9 39.5 %all-to-all-start.1 = ((bf16[64,32,256]{2,1,0:T(8,128)(2,1)}), bf16[64,32,256]{2,1,0:T(8,128)(2,1)S(1)}, u32[]{:S(2)}, u32[]{:S(2)}) async-start(bf16[64,32,256]{2,1,0:T(8,128)(2,1)} %shard_map.46), calls=%async_computation.1 | async-start | bytes 2097152 | tf_op jit(solution)/shard_map/all_to_all | solution.py:247
  55.7 3.2 %collective-permute-start = (f32[2,256]{1,0:T(2,128)S(1)}, f32[2,256]{1,0:T(2,128)S(1)}, u32[]{:S(2)}, u32[]{:S(2)}) collective-permute-start(f32[2,256]{1,0:T(2,128)S(1)} %get-tuple-element.10.refs_1_), channel_id=1, source_target_pairs={{1,0},{2,1},{3,2},{4,3},{5,4},{6,5},{7,6},{0,7},{9,8},{10,9},{11,1... | collective-permute-start | bytes 6152 | tf_op jit(solution)/shard_map/ppermute | solution.py:262

commit v6 on v5

--- a/solution.py
+++ b/solution.py
@@ -12,7 +12,6 @@
 VMEM = pl.BlockSpec(memory_space=pltpu.VMEM)
 SMEM = pl.BlockSpec(memory_space=pltpu.SMEM)
 HBM = pl.BlockSpec(memory_space=pltpu.HBM)
-REF_ROWS = 8
 
 
 def cost(flops, nbytes):
@@ -53,9 +52,10 @@
 
 
 def early_kernel(fields_ref, counts_ref, out_ref, held_ref, sem):
-    dests, slot_rows, width = out_ref.shape
+    dests, slot_rows, lanes = out_ref.shape
+    real, imag = fields_ref[0], fields_ref[1]
+    width = real.shape[1]
     diag_cols = width // dests
-    real, imag = fields_ref[0], fields_ref[1]
     counts = counts_ref[...]
     ref_real = jnp.dot(counts, real, preferred_element_type=F32)
     ref_imag = jnp.dot(counts, imag, preferred_element_type=F32)
@@ -66,35 +66,32 @@
     refs = jnp.where(row == 2, high_imag, refs)
     refs = jnp.where(row == 3, ref_imag - high_imag, refs)
     refs = jnp.where(row > 3, 0.0, refs)
-    diag_real, diag_imag = gram_t(real, imag, real, imag, -imag)
-    rows = jnp.concatenate(
-        [diag_real, diag_imag, refs, jnp.zeros((128 - refs.shape[0], width), F32)], axis=0
-    ).astype(BF16)
-    slot_at = lax.broadcasted_iota(jnp.int32, (dests * slot_rows, rows.shape[0]), 0)
-    source = lax.broadcasted_iota(jnp.int32, (dests * slot_rows, rows.shape[0]), 1)
+    half = lanes - width
+    refs = refs[:, :half] + pltpu.roll(refs[:, half:], 4, 0)
+    diag = jnp.concatenate(gram_t(real, imag, real, imag, -imag), axis=0).astype(BF16)
+    slot_at = lax.broadcasted_iota(jnp.int32, (dests * slot_rows, diag.shape[0]), 0)
+    source = lax.broadcasted_iota(jnp.int32, (dests * slot_rows, diag.shape[0]), 1)
     dest, slot = slot_at // slot_rows, slot_at % slot_rows
-    diag_source = (slot // diag_cols) * width + dest * diag_cols + slot % diag_cols
-    wanted = jnp.where(slot < 2 * diag_cols, diag_source, 2 * width + slot - 2 * diag_cols)
+    wanted = (slot // diag_cols) * width + dest * diag_cols + slot % diag_cols
     pick = jnp.where(wanted == source, 1.0, 0.0).astype(BF16)
-    placed = jnp.dot(pick, rows, preferred_element_type=F32)
-    held_ref[...] = placed.reshape(dests, slot_rows, width).astype(BF16)
+    placed = jnp.dot(pick, diag, preferred_element_type=F32)
+    held_ref[:, :, :width] = placed.reshape(dests, slot_rows, width).astype(BF16)
+    held_ref[:, :, width:] = jnp.broadcast_to(refs[None], (dests, slot_rows, half)).astype(BF16)
     copy = pltpu.make_async_copy(held_ref, out_ref, sem)
     copy.start()
     copy.wait()
 
 
-def choose_kernel(core_ref, own_ref, two_ref, four_ref, _, one_ref, three_ref):
+def choose_kernel(core_ref, own_ref, four_ref, _, out_ref):
     first_core = core_ref[0] == 0
 
     @pl.when(first_core)
     def _():
-        one_ref[...] = two_ref[...]
-        three_ref[...] = four_ref[...]
+        out_ref[...] = four_ref[...]
 
     @pl.when(jnp.logical_not(first_core))
     def _():
-        one_ref[...] = own_ref[...]
-        three_ref[...] = two_ref[...]
+        out_ref[...] = own_ref[...]
 
 
 def tile_pair(own_ref, blocks, out_ref, first, held_ref, sems):
@@ -119,8 +116,11 @@
     tile_pair(own_ref, (two_ref, four_ref), out_ref, 1, held_ref, sems)
 
 
-def other_core_kernel(own_ref, one_ref, three_ref, _, out_ref, held_ref, sems):
-    tile_pair(own_ref, (one_ref, three_ref), out_ref, 0, held_ref, sems)
+def other_core_kernel(core_ref, own_ref, two_swap_ref, other_swap_ref, _, out_ref, held_ref, sems):
+    first_core = core_ref[0] == 0
+    one = [jnp.where(first_core, other_swap_ref[part], two_swap_ref[part]) for part in range(2)]
+    three = [jnp.where(first_core, two_swap_ref[part], other_swap_ref[part]) for part in range(2)]
+    tile_pair(own_ref, (one, three), out_ref, 0, held_ref, sems)
 
 
 def unit_phase(real, imag):
@@ -147,8 +147,10 @@
 def diag_kernel(pixel_scale, starts_ref, early_ref, diag_out, refs_out):
     diag_cols = diag_out.shape[1]
     sums = jnp.sum(early_ref[...].astype(F32), axis=0)
-    diag, terms = sums[: 2 * diag_cols], sums[2 * diag_cols :]
-    real, imag = terms[0:1] + terms[1:2], terms[2:3] + terms[3:4]
+    width = refs_out.shape[1]
+    diag, terms = sums[:, :width], sums[:, width:]
+    real = jnp.concatenate([terms[0:1] + terms[1:2], terms[4:5] + terms[5:6]], axis=1)
+    imag = jnp.concatenate([terms[2:3] + terms[3:4], terms[6:7] + terms[7:8]], axis=1)
     refs_out[0:1, :] = real
     refs_out[1:2, :] = imag
     row_phase = unit_phase(real, imag)
@@ -175,7 +177,7 @@
     tile_dests = pix_count // tiles
     part_cols = width // tile_dests
     diag_cols = width // pix_count
-    slot_rows = 2 * diag_cols + REF_ROWS
+    early_shape = (pix_count, 2 * diag_cols, width + width // 2)
     field_bytes = 2 * pixel_rows * width * 2
     tile_flops = 8 * pixel_rows * width * width
     params = pltpu.CompilerParams(vmem_limit_bytes=32 << 20)
@@ -204,25 +206,26 @@
     four = shift(fields, 4)
     early = pl.pallas_call(
         early_kernel,
-        out_shape=jax.ShapeDtypeStruct((pix_count, slot_rows, width), BF16),
+        out_shape=jax.ShapeDtypeStruct(early_shape, BF16),
         in_specs=[VMEM, VMEM],
         out_specs=HBM,
-        scratch_shapes=[pltpu.VMEM((pix_count, slot_rows, width), BF16), pltpu.SemaphoreType.DMA],
+        scratch_shapes=[pltpu.VMEM(early_shape, BF16), pltpu.SemaphoreType.DMA],
         cost_estimate=cost(4 * tile_flops, 2 * field_bytes),
         compiler_params=params,
     )(fields, counts)
 
-    one, three = pl.pallas_call(
+    other_swap = pl.pallas_call(
         choose_kernel,
-        out_shape=(jax.ShapeDtypeStruct(fields.shape, BF16),) * 2,
-        in_specs=[SMEM] + [VMEM] * 3 + [HBM],
-        out_specs=(VMEM, VMEM),
-        cost_estimate=cost(0, 4 * field_bytes),
-        compiler_params=params,
-    )(core, fields, two, four, early)
+        out_shape=jax.ShapeDtypeStruct(fields.shape, BF16),
+        in_specs=[SMEM] + [VMEM] * 2 + [HBM],
+        out_specs=VMEM,
+        cost_estimate=cost(0, 2 * field_bytes),
+        compiler_params=params,
+    )(core, fields, four, early)
     early = lax.all_to_all(early, "pix", 0, 0, tiled=True)
     swap = [(m, m ^ 1) for m in range(mode_count)]
-    one, three = lax.ppermute(one, "mode", swap), lax.ppermute(three, "mode", swap)
+    other_swap = lax.ppermute(other_swap, "mode", swap)
+    two_swap = lax.ppermute(two, "mode", swap)
     band_shape = jax.ShapeDtypeStruct((pix_count, 2 * part_cols, width), BF16)
     scratch = [pltpu.VMEM((2, tile_dests, 2 * part_cols, width), BF16), pltpu.SemaphoreType.DMA((2,))]
     same = pl.pallas_call(
@@ -237,13 +240,13 @@
     band = pl.pallas_call(
         other_core_kernel,
         out_shape=band_shape,
-        in_specs=[VMEM, VMEM, VMEM, HBM],
+        in_specs=[SMEM] + [VMEM] * 3 + [HBM],
         out_specs=HBM,
         scratch_shapes=scratch,
-        input_output_aliases={3: 0},
+        input_output_aliases={4: 0},
         cost_estimate=cost(2 * tile_flops, 4 * field_bytes),
         compiler_params=params,
-    )(fields, one, three, same)
+    )(core, fields, two_swap, other_swap, same)
     band = lax.all_to_all(band, "pix", 0, 0, tiled=True)
 
     diag_out, own_ref = pl.pallas_call(

time: 86.3 us -> 83.8 us (0.971)
  waiting for transfers between devices: 38.8 us -> 36.7 us
    ppermute x2, waiting for transfers between devices: 4.54 us -> 2.87 us  [shift(): return lax.ppermute(array, 'mode', pairs)]
  transfers between devices with their start and end apart: 7 -> 7, of which waited for: 4 -> 5; matrix products, arithmetic and copies ran while one was open for 0% -> 0% of each run, Pallas kernels for 7% -> 7%
where the time goes in v6:
time: 83.8 us; the launch traced here: 83.4 us
  starting transfers between devices  37.3 us (45%)
  waiting for transfers between devices  36.7 us (44%)
  Pallas kernels  8.5 us (10%)
    all_to_all x1, waiting for transfers between devices, shards(): band = lax.all_to_all(band, 'pix', 0, 0, tiled=True)  25.3 us
    all_to_all x1, starting transfers between devices, shards(): early = lax.all_to_all(early, 'pix', 0, 0, tiled=True)  11.3 us
    ppermute x2, starting transfers between devices, shift(): return lax.ppermute(array, 'mode', pairs)  10.5 us
    all_to_all x1, starting transfers between devices, shards(): band = lax.all_to_all(band, 'pix', 0, 0, tiled=True)  9.76 us
    all_to_all x1, waiting for transfers between devices, shards(): early = lax.all_to_all(early, 'pix', 0, 0, tiled=True)  6.85 us
    ppermute x2, waiting for transfers between devices, shift(): return lax.ppermute(array, 'mode', pairs)  2.87 us
    ppermute x1, starting transfers between devices, shards(): other_swap = lax.ppermute(other_swap, 'mode', swap)  1.92 us
    ppermute x1, starting transfers between devices, shards(): two_swap = lax.ppermute(two, 'mode', swap)  1.91 us
  transfers between devices with their start and end apart: 7, of which 5 were waited for; matrix products, arithmetic and copies ran while one was open for 0% of the time, Pallas kernels for 7%

profile of v6, /device:TPU:6, one launch (start us, length us, event | category | flops | bytes accessed | tf_op | source)
XLA Modules:
  0.0 83.4 jit_solution(14796238788173431919)
XLA Ops:
  0.6 1.3 %shard_map.41 = (bf16[2,512,256]{2,1,0:T(8,128)(2,1)S(1)}, bf16[8,512]{1,0:T(8,128)(2,1)S(1)}) custom-call(s32[1]{0:T(128)} %bitcast.2.base_ref, bf16[4,512,256]{2,1,0:T(8,128)(2,1)} %frames_ref.1, s32[64]{0:T(128)} %pixels_ref.1), custom_call_target="tpu_custom_call" | custom-call | flops 524288 | bytes 1572864 | tf_op jit(solution)/shard_map/pallas_call | solution.py:193
  1.9 3.3 %collective-permute-start.3 = (bf16[2,512,256]{2,1,0:T(8,128)(2,1)S(1)}, bf16[2,512,256]{2,1,0:T(8,128)(2,1)S(1)}, u32[]{:S(2)}, u32[]{:S(2)}) collective-permute-start(bf16[2,512,256]{2,1,0:T(8,128)(2,1)S(1)} %get-tuple-element.6.fields_ref.own_ref), channel_id=1, source_target_pairs={{4,0},{5,1},{6,2},{7,3},{0,4},{1,5},{2,6},{3,7},{12,8},{13,9},{14,... | collective-permute-start | bytes 1572872 | tf_op jit(solution)/shard_map/ppermute | solution.py:187
  5.2 7.2 %collective-permute-start.1 = (bf16[2,512,256]{2,1,0:T(8,128)(2,1)S(1)}, bf16[2,512,256]{2,1,0:T(8,128)(2,1)S(1)}, u32[]{:S(2)}, u32[]{:S(2)}) collective-permute-start(bf16[2,512,256]{2,1,0:T(8,128)(2,1)S(1)} %get-tuple-element.6.fields_ref.own_ref), channel_id=1, source_target_pairs={{2,0},{3,1},{4,2},{5,3},{6,4},{7,5},{0,6},{1,7},{10,8},{11,9},{12,... | collective-permute-start | bytes 1572872 | tf_op jit(solution)/shard_map/ppermute | solution.py:187
  12.4 1.6 %shard_map.42._ = bf16[64,8,384]{2,1,0:T(8,128)(2,1)} custom-call(bf16[2,512,256]{2,1,0:T(8,128)(2,1)S(1)} %get-tuple-element.6.fields_ref.own_ref, bf16[8,512]{1,0:T(8,128)(2,1)S(1)} %get-tuple-element.7.counts_ref), custom_call_target="tpu_custom_call" | custom-call | flops 1073741824 | bytes 1048576 | tf_op jit(solution)/shard_map/pallas_call | solution.py:207
  14.0 11.3 %all-to-all-start = ((bf16[64,8,384]{2,1,0:T(8,128)(2,1)}), bf16[64,8,384]{2,1,0:T(8,128)(2,1)S(1)}, u32[]{:S(2)}, u32[]{:S(2)}) async-start(bf16[64,8,384]{2,1,0:T(8,128)(2,1)} %shard_map.42._), calls=%async_computation | async-start | bytes 786432 | tf_op jit(solution)/shard_map/all_to_all | solution.py:225
  25.3 0.0 collective-permute-done.3.four_ref
  25.4 1.9 %collective-permute-start.4 = (bf16[2,512,256]{2,1,0:T(8,128)(2,1)S(1)}, bf16[2,512,256]{2,1,0:T(8,128)(2,1)S(1)}, u32[]{:S(2)}, u32[]{:S(2)}) collective-permute-start(bf16[2,512,256]{2,1,0:T(8,128)(2,1)S(1)} %shard_map.44), channel_id=1, source_target_pairs={{0,1},{1,0},{2,3},{3,2},{4,5},{5,4},{6,7},{7,6},{8,9},{9,8},{10,11... | collective-permute-start | bytes 1572872 | tf_op jit(solution)/shard_map/ppermute | solution.py:227
  27.3 2.9 %collective-permute-done.1.two_ref = bf16[2,512,256]{2,1,0:T(8,128)(2,1)S(1)} collective-permute-done((bf16[2,512,256]{2,1,0:T(8,128)(2,1)S(1)}, bf16[2,512,256]{2,1,0:T(8,128)(2,1)S(1)}, u32[]{:S(2)}, u32[]{:S(2)}) %collective-permute-start.1) | collective-permute-done | bytes 524320 | tf_op jit(solution)/shard_map/ppermute | solution.py:187
  30.2 1.9 %collective-permute-start.2 = (bf16[2,512,256]{2,1,0:T(8,128)(2,1)S(1)}, bf16[2,512,256]{2,1,0:T(8,128)(2,1)S(1)}, u32[]{:S(2)}, u32[]{:S(2)}) collective-permute-start(bf16[2,512,256]{2,1,0:T(8,128)(2,1)S(1)} %collective-permute-done.1.two_ref), channel_id=1, source_target_pairs={{0,1},{1,0},{2,3},{3,2},{4,5},{5,4},{6,7},{7,6},{8,9},{9,8},{10,11... | collective-permute-start | bytes 1572872 | tf_op jit(solution)/shard_map/ppermute | solution.py:228
  32.1 1.5 %shard_map.45._ = bf16[64,32,256]{2,1,0:T(8,128)(2,1)} custom-call(bf16[2,512,256]{2,1,0:T(8,128)(2,1)S(1)} %get-tuple-element.6.fields_ref.own_ref, bf16[2,512,256]{2,1,0:T(8,128)(2,1)S(1)} %collective-permute-done.1.two_ref, bf16[2,512,256]{2,1,0:T(8,128)(2,1)S(1)} %collective-permute-done.3.four_ref), custom_call_target="tpu_custom_call" | custom-call | flops 536870912 | bytes 2097152 | tf_op jit(solution)/shard_map/pallas_call | solution.py:231
  33.6 0.0 collective-permute-done.4.other_swap_ref
  33.6 0.4 collective-permute-done.2.two_swap_ref
  34.0 1.5 %shard_map.46 = bf16[64,32,256]{2,1,0:T(8,128)(2,1)} custom-call(s32[1]{0:T(128)} %bitcast.3.core_ref, bf16[2,512,256]{2,1,0:T(8,128)(2,1)S(1)} %get-tuple-element.6.fields_ref.own_ref, bf16[2,512,256]{2,1,0:T(8,128)(2,1)S(1)} %collective-permute-done.2.two_swap_ref, ...), custom_call_target="tpu_custom_call", output_to_operand_aliasing={{}: (4, {})} | custom-call | flops 536870912 | bytes 2097152 | tf_op jit(solution)/shard_map/pallas_call | solution.py:240
  35.5 6.8 %all-to-all-done.refs_1_ = bf16[64,8,384]{2,1,0:T(8,128)(2,1)S(1)} async-done(((bf16[64,8,384]{2,1,0:T(8,128)(2,1)}), bf16[64,8,384]{2,1,0:T(8,128)(2,1)S(1)}, u32[]{:S(2)}, u32[]{:S(2)}) %all-to-all-start) | async-done | bytes 393248 | tf_op jit(solution)/shard_map/all_to_all | solution.py:225
  42.4 9.8 %all-to-all-start.1 = ((bf16[64,32,256]{2,1,0:T(8,128)(2,1)}), bf16[64,32,256]{2,1,0:T(8,128)(2,1)S(1)}, u32[]{:S(2)}, u32[]{:S(2)}) async-start(bf16[64,32,256]{2,1,0:T(8,128)(2,1)} %shard_map.46), calls=%async_computation.1 | async-start | bytes 2097152 | tf_op jit(solution)/shard_map/all_to_all | solution.py:250
  52.1 0.1 pad_add_fusion.refs_0_
  52.2 1.3 %shard_map.43 = (f32[2,4,256]{2,1,0:T(4,128)}, f32[2,256]{1,0:T(2,128)S(1)}) custom-call(s32[2]{0:T(128)S(1)} %pad_add_fusion.refs_0_, bf16[64,8,384]{2,1,0:T(8,128)(2,1)S(1)} %all-to-all-done.refs_1_), custom_call_target="tpu_custom_call" | custom-call | flops 524288 | bytes 524288 | tf_op jit(solution)/shard_map/pallas_call | solution.py:252
  53.5 1.9 %collective-permute-start = (f32[2,256]{1,0:T(2,128)S(1)}, f32[2,256]{1,0:T(2,128)S(1)}, u32[]{:S(2)}, u32[]{:S(2)}) collective-permute-start(f32[2,256]{1,0:T(2,128)S(1)} %get-tuple-element.8.refs_1_), channel_id=1, source_target_pairs={{1,0},{2,1},{3,2},{4,3},{5,4},{6,5},{7,6},{0,7},{9,8},{10,9},{11,1... | collective-permute-start | bytes 6152 | tf_op jit(solution)/shard_map/ppermute | solution.py:265
  55.4 1.3 %collective-permute-done.refs_2_ = f32[2,256]{1,0:T(2,128)S(1)} collective-permute-done((f32[2,256]{1,0:T(2,128)S(1)}, f32[2,256]{1,0:T(2,128)S(1)}, u32[]{:S(2)}, u32[]{:S(2)}) %collective-permute-start) | collective-permute-done | bytes 2080 | tf_op jit(solution)/shard_map/ppermute | solution.py:265
  56.7 25.3 %all-to-all-done.1.refs_3_ = bf16[64,32,256]{2,1,0:T(8,128)(2,1)S(1)} async-done(((bf16[64,32,256]{2,1,0:T(8,128)(2,1)}), bf16[64,32,256]{2,1,0:T(8,128)(2,1)S(1)}, u32[]{:S(2)}, u32[]{:S(2)}) %all-to-all-start.1) | async-done | bytes 1048608 | tf_op jit(solution)/shard_map/all_to_all | solution.py:250
  82.0 1.3 %shard_map.47 = f32[2,16,256]{2,1,0:T(8,128)} custom-call(s32[2]{0:T(128)S(1)} %pad_add_fusion.refs_0_, f32[2,256]{1,0:T(2,128)S(1)} %get-tuple-element.8.refs_1_, f32[2,256]{1,0:T(2,128)S(1)} %collective-permute-done.refs_2_, bf16[64,32,256]{2,1,0:T(8,128)(2,1)S(1)} %all-to-all-done.1.refs_3_), custom_call_target="tpu_custom_call" | custom-call | flops 1048576 | bytes 1048576 | tf_op jit(solution)/shard_map/pallas_call | solution.py:266
  (1 shorter events, 0.0 us)
Async XLA Ops:
  1.9 23.4 %collective-permute-start.3 = (bf16[2,512,256]{2,1,0:T(8,128)(2,1)S(1)}, bf16[2,512,256]{2,1,0:T(8,128)(2,1)S(1)}, u32[]{:S(2)}, u32[]{:S(2)}) collective-permute-start(bf16[2,512,256]{2,1,0:T(8,128)(2,1)S(1)} %get-tuple-element.6.fields_ref.own_ref), channel_id=1, source_target_pairs={{4,0},{5,1},{6,2},{7,3},{0,4},{1,5},{2,6},{3,7},{12,8},{13,9},{14,... | collective-permute-start | bytes 1572872 | tf_op jit(solution)/shard_map/ppermute | solution.py:187
  5.2 25.0 %collective-permute-start.1 = (bf16[2,512,256]{2,1,0:T(8,128)(2,1)S(1)}, bf16[2,512,256]{2,1,0:T(8,128)(2,1)S(1)}, u32[]{:S(2)}, u32[]{:S(2)}) collective-permute-start(bf16[2,512,256]{2,1,0:T(8,128)(2,1)S(1)} %get-tuple-element.6.fields_ref.own_ref), channel_id=1, source_target_pairs={{2,0},{3,1},{4,2},{5,3},{6,4},{7,5},{0,6},{1,7},{10,8},{11,9},{12,... | collective-permute-start | bytes 1572872 | tf_op jit(solution)/shard_map/ppermute | solution.py:187
  14.0 28.3 %all-to-all-start = ((bf16[64,8,384]{2,1,0:T(8,128)(2,1)}), bf16[64,8,384]{2,1,0:T(8,128)(2,1)S(1)}, u32[]{:S(2)}, u32[]{:S(2)}) async-start(bf16[64,8,384]{2,1,0:T(8,128)(2,1)} %shard_map.42._), calls=%async_computation | async-start | bytes 786432 | tf_op jit(solution)/shard_map/all_to_all | solution.py:225
  25.4 8.2 %collective-permute-start.4 = (bf16[2,512,256]{2,1,0:T(8,128)(2,1)S(1)}, bf16[2,512,256]{2,1,0:T(8,128)(2,1)S(1)}, u32[]{:S(2)}, u32[]{:S(2)}) collective-permute-start(bf16[2,512,256]{2,1,0:T(8,128)(2,1)S(1)} %shard_map.44), channel_id=1, source_target_pairs={{0,1},{1,0},{2,3},{3,2},{4,5},{5,4},{6,7},{7,6},{8,9},{9,8},{10,11... | collective-permute-start | bytes 1572872 | tf_op jit(solution)/shard_map/ppermute | solution.py:227
  30.2 3.8 %collective-permute-start.2 = (bf16[2,512,256]{2,1,0:T(8,128)(2,1)S(1)}, bf16[2,512,256]{2,1,0:T(8,128)(2,1)S(1)}, u32[]{:S(2)}, u32[]{:S(2)}) collective-permute-start(bf16[2,512,256]{2,1,0:T(8,128)(2,1)S(1)} %collective-permute-done.1.two_ref), channel_id=1, source_target_pairs={{0,1},{1,0},{2,3},{3,2},{4,5},{5,4},{6,7},{7,6},{8,9},{9,8},{10,11... | collective-permute-start | bytes 1572872 | tf_op jit(solution)/shard_map/ppermute | solution.py:228
  42.4 39.7 %all-to-all-start.1 = ((bf16[64,32,256]{2,1,0:T(8,128)(2,1)}), bf16[64,32,256]{2,1,0:T(8,128)(2,1)S(1)}, u32[]{:S(2)}, u32[]{:S(2)}) async-start(bf16[64,32,256]{2,1,0:T(8,128)(2,1)} %shard_map.46), calls=%async_computation.1 | async-start | bytes 2097152 | tf_op jit(solution)/shard_map/all_to_all | solution.py:250
  53.5 3.2 %collective-permute-start = (f32[2,256]{1,0:T(2,128)S(1)}, f32[2,256]{1,0:T(2,128)S(1)}, u32[]{:S(2)}, u32[]{:S(2)}) collective-permute-start(f32[2,256]{1,0:T(2,128)S(1)} %get-tuple-element.8.refs_1_), channel_id=1, source_target_pairs={{1,0},{2,1},{3,2},{4,3},{5,4},{6,5},{7,6},{0,7},{9,8},{10,9},{11,1... | collective-permute-start | bytes 6152 | tf_op jit(solution)/shard_map/ppermute | solution.py:265

commit v7 on v6

--- a/solution.py
+++ b/solution.py
@@ -5,10 +5,14 @@
 from jax import lax
 from jax.experimental import pallas as pl
 from jax.experimental.pallas import tpu as pltpu
+from jax.sharding import Mesh
 from jax.sharding import PartitionSpec as P
 
 BF16 = jnp.bfloat16
 F32 = jnp.float32
+QUADS, NEAR = 4, 2
+PIX = ("zh", "zl", "yh", "yl")
+EXCHANGE = ("yh", "zh", "yl", "zl")
 VMEM = pl.BlockSpec(memory_space=pltpu.VMEM)
 SMEM = pl.BlockSpec(memory_space=pltpu.SMEM)
 HBM = pl.BlockSpec(memory_space=pltpu.HBM)
@@ -72,7 +76,9 @@
     slot_at = lax.broadcasted_iota(jnp.int32, (dests * slot_rows, diag.shape[0]), 0)
     source = lax.broadcasted_iota(jnp.int32, (dests * slot_rows, diag.shape[0]), 1)
     dest, slot = slot_at // slot_rows, slot_at % slot_rows
-    wanted = (slot // diag_cols) * width + dest * diag_cols + slot % diag_cols
+    y = dest // (QUADS * NEAR * NEAR) * NEAR + dest // NEAR % NEAR
+    z = dest // (NEAR * NEAR) % QUADS * NEAR + dest % NEAR
+    wanted = (slot // diag_cols) * width + (z * (QUADS * NEAR) + y) * diag_cols + slot % diag_cols
     pick = jnp.where(wanted == source, 1.0, 0.0).astype(BF16)
     placed = jnp.dot(pick, diag, preferred_element_type=F32)
     held_ref[:, :, :width] = placed.reshape(dests, slot_rows, width).astype(BF16)
@@ -82,45 +88,46 @@
     copy.wait()
 
 
-def choose_kernel(core_ref, own_ref, four_ref, _, out_ref):
+def choose_kernel(core_ref, own_ref, near_ref, _, out_ref):
     first_core = core_ref[0] == 0
 
     @pl.when(first_core)
     def _():
-        out_ref[...] = four_ref[...]
+        out_ref[...] = near_ref[...]
 
     @pl.when(jnp.logical_not(first_core))
     def _():
         out_ref[...] = own_ref[...]
 
 
-def tile_pair(own_ref, blocks, out_ref, first, held_ref, sems):
+def tile_pair(own_ref, blocks, out_ref, runs, held_ref, sems):
     row_real, row_imag = own_ref[0], own_ref[1]
     row_imag_neg = -row_imag
-    _, tile_dests, rows, width = held_ref.shape
+    _, _, near, rows, _ = held_ref.shape
     part_cols = rows // 2
     copies = []
     for at, block in enumerate(blocks):
         tile = gram_t(block[0], block[1], row_real, row_imag, row_imag_neg)
-        for c, part in enumerate(tile):
-            cut = part.reshape(tile_dests, part_cols, width).astype(BF16)
-            held_ref[at, :, c * part_cols : (c + 1) * part_cols, :] = cut
-        dests = pl.ds((2 * at + first) * tile_dests, tile_dests)
-        copies.append(pltpu.make_async_copy(held_ref.at[at], out_ref.at[dests], sems.at[at]))
+        for yh in range(QUADS):
+            for dest in range(near):
+                yl, zl = dest // NEAR, dest % NEAR
+                start = ((zl * QUADS + yh) * NEAR + yl) * part_cols
+                for c, part in enumerate(tile):
+                    cut = part[start : start + part_cols].astype(BF16)
+                    held_ref[at, yh, dest, c * part_cols : (c + 1) * part_cols, :] = cut
+        copies.append(pltpu.make_async_copy(held_ref.at[at], out_ref.at[:, runs[at]], sems.at[at]))
         copies[-1].start()
     for copy in copies:
         copy.wait()
 
 
-def same_core_kernel(own_ref, two_ref, four_ref, out_ref, held_ref, sems):
-    tile_pair(own_ref, (two_ref, four_ref), out_ref, 1, held_ref, sems)
-
-
-def other_core_kernel(core_ref, own_ref, two_swap_ref, other_swap_ref, _, out_ref, held_ref, sems):
-    first_core = core_ref[0] == 0
-    one = [jnp.where(first_core, other_swap_ref[part], two_swap_ref[part]) for part in range(2)]
-    three = [jnp.where(first_core, two_swap_ref[part], other_swap_ref[part]) for part in range(2)]
-    tile_pair(own_ref, (one, three), out_ref, 0, held_ref, sems)
+def same_core_kernel(core_ref, own_ref, first_ref, second_ref, out_ref, held_ref, sems):
+    core = core_ref[0]
+    tile_pair(own_ref, (first_ref, second_ref), out_ref, (1 + 2 * core, 3 - 2 * core), held_ref, sems)
+
+
+def other_core_kernel(own_ref, one_ref, three_ref, _, out_ref, held_ref, sems):
+    tile_pair(own_ref, (one_ref, three_ref), out_ref, (0, 2), held_ref, sems)
 
 
 def unit_phase(real, imag):
@@ -168,9 +175,9 @@
 
 
 def shards(frames, ref_pixels):
-    pix_count = lax.axis_size("pix")
+    pix_count = lax.axis_size(PIX)
     mode_count = lax.axis_size("mode")
-    pix_index = lax.axis_index("pix")
+    pix_index = lax.axis_index(PIX)
     mode_index = lax.axis_index("mode")
     pixel_rows, width = frames.shape[1:]
     tiles = mode_count // 2
@@ -182,8 +189,8 @@
     tile_flops = 8 * pixel_rows * width * width
     params = pltpu.CompilerParams(vmem_limit_bytes=32 << 20)
 
-    def shift(array, step):
-        pairs = [((m + step) % mode_count, m) for m in range(mode_count)]
+    def shift(array, even_step, odd_step):
+        pairs = [((m + (odd_step if m % 2 else even_step)) % mode_count, m) for m in range(mode_count)]
         return lax.ppermute(array, "mode", pairs)
 
     base = (pix_index * pixel_rows).reshape(1)
@@ -202,8 +209,8 @@
         ],
         cost_estimate=cost(4 * pixel_rows * width, 3 * field_bytes),
     )(base, frames, ref_pixels)
-    two = shift(fields, 2)
-    four = shift(fields, 4)
+    first = shift(fields, 2, 4)
+    second = shift(fields, 4, 2)
     early = pl.pallas_call(
         early_kernel,
         out_shape=jax.ShapeDtypeStruct(early_shape, BF16),
@@ -214,40 +221,41 @@
         compiler_params=params,
     )(fields, counts)
 
-    other_swap = pl.pallas_call(
+    chosen = pl.pallas_call(
         choose_kernel,
         out_shape=jax.ShapeDtypeStruct(fields.shape, BF16),
         in_specs=[SMEM] + [VMEM] * 2 + [HBM],
         out_specs=VMEM,
         cost_estimate=cost(0, 2 * field_bytes),
         compiler_params=params,
-    )(core, fields, four, early)
-    early = lax.all_to_all(early, "pix", 0, 0, tiled=True)
+    )(core, fields, first, early)
+    early = lax.all_to_all(early, EXCHANGE, 0, 0, tiled=True)
     swap = [(m, m ^ 1) for m in range(mode_count)]
-    other_swap = lax.ppermute(other_swap, "mode", swap)
-    two_swap = lax.ppermute(two, "mode", swap)
-    band_shape = jax.ShapeDtypeStruct((pix_count, 2 * part_cols, width), BF16)
-    scratch = [pltpu.VMEM((2, tile_dests, 2 * part_cols, width), BF16), pltpu.SemaphoreType.DMA((2,))]
+    one = lax.ppermute(chosen, "mode", swap)
+    three = lax.ppermute(second, "mode", swap)
+    near = NEAR * NEAR
+    band_shape = jax.ShapeDtypeStruct((QUADS, tiles, near, 2 * part_cols, width), BF16)
+    scratch = [pltpu.VMEM((2, QUADS, near, 2 * part_cols, width), BF16), pltpu.SemaphoreType.DMA((2,))]
     same = pl.pallas_call(
         same_core_kernel,
         out_shape=band_shape,
-        in_specs=[VMEM] * 3,
+        in_specs=[SMEM] + [VMEM] * 3,
         out_specs=HBM,
         scratch_shapes=scratch,
         cost_estimate=cost(2 * tile_flops, 4 * field_bytes),
         compiler_params=params,
-    )(fields, two, four)
+    )(core, fields, first, second)
     band = pl.pallas_call(
         other_core_kernel,
         out_shape=band_shape,
-        in_specs=[SMEM] + [VMEM] * 3 + [HBM],
+        in_specs=[VMEM] * 3 + [HBM],
         out_specs=HBM,
         scratch_shapes=scratch,
-        input_output_aliases={4: 0},
+        input_output_aliases={3: 0},
         cost_estimate=cost(2 * tile_flops, 4 * field_bytes),
         compiler_params=params,
-    )(core, fields, two_swap, other_swap, same)
-    band = lax.all_to_all(band, "pix", 0, 0, tiled=True)
+    )(fields, one, three, same)
+    band = lax.all_to_all(band.reshape(pix_count, 2 * part_cols, width), EXCHANGE, 0, 0, tiled=True)
 
     diag_out, own_ref = pl.pallas_call(
         lambda *refs: diag_kernel(scale, *refs),
@@ -262,7 +270,7 @@
         step = p // tile_dests + 1
         for m in range(mode_count):
             pairs.append((p * mode_count + (m + step) % mode_count, p * mode_count + m))
-    other_ref = lax.ppermute(own_ref, ("pix", "mode"), pairs)
+    other_ref = lax.ppermute(own_ref, (*PIX, "mode"), pairs)
     band_out = pl.pallas_call(
         lambda *refs: final_kernel(scale, *refs),
         out_shape=jax.ShapeDtypeStruct((2, part_cols, width), F32),
@@ -275,10 +283,11 @@
 
 
 def solution(mesh):
+    split = Mesh(mesh.devices.reshape(QUADS, NEAR, QUADS, NEAR, -1), (*PIX, "mode"))
     return jax.shard_map(
         shards,
-        mesh=mesh,
-        in_specs=(P(None, "pix", "mode"), P()),
-        out_specs=(P(None, "mode", "pix"), P(None, "mode", "pix")),
+        mesh=split,
+        in_specs=(P(None, PIX, "mode"), P()),
+        out_specs=(P(None, "mode", PIX), P(None, "mode", PIX)),
         check_vma=False,
     )

time: 83.8 us -> 82.9 us (0.989)
  waiting for transfers between devices: 36.7 us -> 33.5 us
  starting transfers between devices: 37.3 us -> 38.9 us
    all_to_all x2, waiting for transfers between devices: 32.1 us -> 30.2 us  [the longest x1 24.1 us: shards(): lax.all_to_all(band.reshape(pix_count, 2 * part_cols, width), EXCHANGE, 0...]
    ppermute x2, waiting for transfers between devices: 2.87 us -> 1.64 us  [shift(): return lax.ppermute(array, 'mode', pairs)]
where the time goes in v7:
time: 82.9 us; the launch traced here: 82 us
  starting transfers between devices  38.9 us (47%)
  waiting for transfers between devices  33.5 us (40%)
  Pallas kernels  8.66 us (10%)
    all_to_all x1, waiting for transfers between devices, shards(): lax.all_to_all(band.reshape(pix_count, 2 * part_cols, width), EXCHANGE, 0...  24.1 us
    all_to_all x1, starting transfers between devices, shards(): early = lax.all_to_all(early, EXCHANGE, 0, 0, tiled=True)  11.3 us
    ppermute x2, starting transfers between devices, shift(): return lax.ppermute(array, 'mode', pairs)  10.5 us
    all_to_all x1, starting transfers between devices, shards(): lax.all_to_all(band.reshape(pix_count, 2 * part_cols, width), EXCHANGE, 0...  10.5 us
    all_to_all x1, waiting for transfers between devices, shards(): early = lax.all_to_all(early, EXCHANGE, 0, 0, tiled=True)  6.11 us
    ppermute x1, starting transfers between devices, shards(): three = lax.ppermute(second, 'mode', swap)  2.75 us
    ppermute x1, starting transfers between devices, shards(): one = lax.ppermute(chosen, 'mode', swap)  1.92 us
    ppermute x1, starting transfers between devices, shards(): other_ref = lax.ppermute(own_ref, (*PIX, 'mode'), pairs)  1.91 us
  transfers between devices with their start and end apart: 7, of which 5 were waited for; matrix products, arithmetic and copies ran while one was open for 0% of the time, Pallas kernels for 7%

profile of v7, /device:TPU:6, one launch (start us, length us, event | category | flops | bytes accessed | tf_op | source)
XLA Modules:
  0.0 82.0 jit_solution(4042638495414776601)
XLA Ops:
  0.6 1.3 %shard_map.41 = (bf16[2,512,256]{2,1,0:T(8,128)(2,1)S(1)}, bf16[8,512]{1,0:T(8,128)(2,1)S(1)}) custom-call(s32[1]{0:T(128)} %bitcast.2.base_ref, bf16[4,512,256]{2,1,0:T(8,128)(2,1)} %frames_ref.1, s32[64]{0:T(128)} %pixels_ref.1), custom_call_target="tpu_custom_call" | custom-call | flops 524288 | bytes 1572864 | tf_op jit(solution)/shard_map/pallas_call | solution.py:200
  1.9 3.3 %collective-permute-start.3 = (bf16[2,512,256]{2,1,0:T(8,128)(2,1)S(1)}, bf16[2,512,256]{2,1,0:T(8,128)(2,1)S(1)}, u32[]{:S(2)}, u32[]{:S(2)}) collective-permute-start(bf16[2,512,256]{2,1,0:T(8,128)(2,1)S(1)} %get-tuple-element.6.fields_ref.own_ref), channel_id=1, source_target_pairs={{4,0},{3,1},{6,2},{5,3},{0,4},{7,5},{2,6},{1,7},{12,8},{11,9},{14,... | collective-permute-start | bytes 1572872 | tf_op jit(solution)/shard_map/ppermute | solution.py:194
  5.2 7.2 %collective-permute-start.1 = (bf16[2,512,256]{2,1,0:T(8,128)(2,1)S(1)}, bf16[2,512,256]{2,1,0:T(8,128)(2,1)S(1)}, u32[]{:S(2)}, u32[]{:S(2)}) collective-permute-start(bf16[2,512,256]{2,1,0:T(8,128)(2,1)S(1)} %get-tuple-element.6.fields_ref.own_ref), channel_id=1, source_target_pairs={{2,0},{5,1},{4,2},{7,3},{6,4},{1,5},{0,6},{3,7},{10,8},{13,9},{12,... | collective-permute-start | bytes 1572872 | tf_op jit(solution)/shard_map/ppermute | solution.py:194
  12.5 1.7 %shard_map.42._ = bf16[64,8,384]{2,1,0:T(8,128)(2,1)} custom-call(bf16[2,512,256]{2,1,0:T(8,128)(2,1)S(1)} %get-tuple-element.6.fields_ref.own_ref, bf16[8,512]{1,0:T(8,128)(2,1)S(1)} %get-tuple-element.7.counts_ref), custom_call_target="tpu_custom_call" | custom-call | flops 1073741824 | bytes 1048576 | tf_op jit(solution)/shard_map/pallas_call | solution.py:214
  14.2 11.3 %all-to-all-start = ((bf16[64,8,384]{2,1,0:T(8,128)(2,1)}), bf16[64,8,384]{2,1,0:T(8,128)(2,1)S(1)}, u32[]{:S(2)}, u32[]{:S(2)}) async-start(bf16[64,8,384]{2,1,0:T(8,128)(2,1)} %shard_map.42._), calls=%async_computation | async-start | bytes 786432 | tf_op jit(solution)/shard_map/all_to_all | solution.py:232
  25.5 0.0 collective-permute-done.3.second_ref
  25.5 2.7 %collective-permute-start.4 = (bf16[2,512,256]{2,1,0:T(8,128)(2,1)S(1)}, bf16[2,512,256]{2,1,0:T(8,128)(2,1)S(1)}, u32[]{:S(2)}, u32[]{:S(2)}) collective-permute-start(bf16[2,512,256]{2,1,0:T(8,128)(2,1)S(1)} %collective-permute-done.3.second_ref), channel_id=1, source_target_pairs={{0,1},{1,0},{2,3},{3,2},{4,5},{5,4},{6,7},{7,6},{8,9},{9,8},{10,11... | collective-permute-start | bytes 1572872 | tf_op jit(solution)/shard_map/ppermute | solution.py:235
  28.3 1.6 %collective-permute-done.1.near_ref.first_ref = bf16[2,512,256]{2,1,0:T(8,128)(2,1)S(1)} collective-permute-done((bf16[2,512,256]{2,1,0:T(8,128)(2,1)S(1)}, bf16[2,512,256]{2,1,0:T(8,128)(2,1)S(1)}, u32[]{:S(2)}, u32[]{:S(2)}) %collective-permute-start.1) | collective-permute-done | bytes 524320 | tf_op jit(solution)/shard_map/ppermute | solution.py:194
  30.0 1.9 %collective-permute-start.2 = (bf16[2,512,256]{2,1,0:T(8,128)(2,1)S(1)}, bf16[2,512,256]{2,1,0:T(8,128)(2,1)S(1)}, u32[]{:S(2)}, u32[]{:S(2)}) collective-permute-start(bf16[2,512,256]{2,1,0:T(8,128)(2,1)S(1)} %shard_map.44), channel_id=1, source_target_pairs={{0,1},{1,0},{2,3},{3,2},{4,5},{5,4},{6,7},{7,6},{8,9},{9,8},{10,11... | collective-permute-start | bytes 1572872 | tf_op jit(solution)/shard_map/ppermute | solution.py:234
  31.9 1.5 %shard_map.45._ = bf16[4,4,4,32,256]{4,3,2,1,0:T(8,128)(2,1)} custom-call(s32[1]{0:T(128)} %bitcast.3.core_ref, bf16[2,512,256]{2,1,0:T(8,128)(2,1)S(1)} %get-tuple-element.6.fields_ref.own_ref, bf16[2,512,256]{2,1,0:T(8,128)(2,1)S(1)} %collective-permute-done.1.near_ref.first_ref, bf16[2,512,256]{2,1,0:T(8,128)(2,1)S(1)} %collective-permute-done.3.second_ref), custom_call_target="tpu_custom_call" | custom-call | flops 536870912 | bytes 2097152 | tf_op jit(solution)/shard_map/pallas_call | solution.py:239
  33.4 0.0 collective-permute-done.4.three_ref
  33.4 0.4 collective-permute-done.2.one_ref
  33.8 1.5 %shard_map.46 = bf16[4,4,4,32,256]{4,3,2,1,0:T(8,128)(2,1)} custom-call(bf16[2,512,256]{2,1,0:T(8,128)(2,1)S(1)} %get-tuple-element.6.fields_ref.own_ref, bf16[2,512,256]{2,1,0:T(8,128)(2,1)S(1)} %collective-permute-done.2.one_ref, bf16[2,512,256]{2,1,0:T(8,128)(2,1)S(1)} %collective-permute-done.4.three_ref, ...), custom_call_target="tpu_custom_call", output_to_operand_aliasing={{}: (3, {})} | custom-call | flops 536870912 | bytes 2097152 | tf_op jit(solution)/shard_map/pallas_call | solution.py:248
  35.3 6.1 %all-to-all-done.refs_1_ = bf16[64,8,384]{2,1,0:T(8,128)(2,1)S(1)} async-done(((bf16[64,8,384]{2,1,0:T(8,128)(2,1)}), bf16[64,8,384]{2,1,0:T(8,128)(2,1)S(1)}, u32[]{:S(2)}, u32[]{:S(2)}) %all-to-all-start) | async-done | bytes 393248 | tf_op jit(solution)/shard_map/all_to_all | solution.py:232
  41.4 10.5 %all-to-all-start.1 = ((bf16[64,32,256]{2,1,0:T(8,128)(2,1)}), bf16[64,32,256]{2,1,0:T(8,128)(2,1)S(1)}, u32[]{:S(2)}, u32[]{:S(2)}) async-start(bf16[64,32,256]{2,1,0:T(8,128)(2,1)} %bitcast.4), calls=%async_computation.1 | async-start | bytes 2097152 | tf_op jit(solution)/shard_map/all_to_all | solution.py:258
  51.9 0.1 pad_add_fusion.refs_0_
  52.0 1.3 %shard_map.43 = (f32[2,4,256]{2,1,0:T(4,128)}, f32[2,256]{1,0:T(2,128)S(1)}) custom-call(s32[2]{0:T(128)S(1)} %pad_add_fusion.refs_0_, bf16[64,8,384]{2,1,0:T(8,128)(2,1)S(1)} %all-to-all-done.refs_1_), custom_call_target="tpu_custom_call" | custom-call | flops 524288 | bytes 524288 | tf_op jit(solution)/shard_map/pallas_call | solution.py:260
  53.3 1.9 %collective-permute-start = (f32[2,256]{1,0:T(2,128)S(1)}, f32[2,256]{1,0:T(2,128)S(1)}, u32[]{:S(2)}, u32[]{:S(2)}) collective-permute-start(f32[2,256]{1,0:T(2,128)S(1)} %get-tuple-element.8.refs_1_), channel_id=1, source_target_pairs={{1,0},{2,1},{3,2},{4,3},{5,4},{6,5},{7,6},{0,7},{9,8},{10,9},{11,1... | collective-permute-start | bytes 6152 | tf_op jit(solution)/shard_map/ppermute | solution.py:273
  55.2 1.3 %collective-permute-done.refs_2_ = f32[2,256]{1,0:T(2,128)S(1)} collective-permute-done((f32[2,256]{1,0:T(2,128)S(1)}, f32[2,256]{1,0:T(2,128)S(1)}, u32[]{:S(2)}, u32[]{:S(2)}) %collective-permute-start) | collective-permute-done | bytes 2080 | tf_op jit(solution)/shard_map/ppermute | solution.py:273
  56.5 24.1 %all-to-all-done.1.refs_3_ = bf16[64,32,256]{2,1,0:T(8,128)(2,1)S(1)} async-done(((bf16[64,32,256]{2,1,0:T(8,128)(2,1)}), bf16[64,32,256]{2,1,0:T(8,128)(2,1)S(1)}, u32[]{:S(2)}, u32[]{:S(2)}) %all-to-all-start.1) | async-done | bytes 1048608 | tf_op jit(solution)/shard_map/all_to_all | solution.py:258
  80.6 1.3 %shard_map.47 = f32[2,16,256]{2,1,0:T(8,128)} custom-call(s32[2]{0:T(128)S(1)} %pad_add_fusion.refs_0_, f32[2,256]{1,0:T(2,128)S(1)} %get-tuple-element.8.refs_1_, f32[2,256]{1,0:T(2,128)S(1)} %collective-permute-done.refs_2_, bf16[64,32,256]{2,1,0:T(8,128)(2,1)S(1)} %all-to-all-done.1.refs_3_), custom_call_target="tpu_custom_call" | custom-call | flops 1048576 | bytes 1048576 | tf_op jit(solution)/shard_map/pallas_call | solution.py:274
  (1 shorter events, 0.0 us)
Async XLA Ops:
  1.9 23.6 %collective-permute-start.3 = (bf16[2,512,256]{2,1,0:T(8,128)(2,1)S(1)}, bf16[2,512,256]{2,1,0:T(8,128)(2,1)S(1)}, u32[]{:S(2)}, u32[]{:S(2)}) collective-permute-start(bf16[2,512,256]{2,1,0:T(8,128)(2,1)S(1)} %get-tuple-element.6.fields_ref.own_ref), channel_id=1, source_target_pairs={{4,0},{3,1},{6,2},{5,3},{0,4},{7,5},{2,6},{1,7},{12,8},{11,9},{14,... | collective-permute-start | bytes 1572872 | tf_op jit(solution)/shard_map/ppermute | solution.py:194
  5.2 24.7 %collective-permute-start.1 = (bf16[2,512,256]{2,1,0:T(8,128)(2,1)S(1)}, bf16[2,512,256]{2,1,0:T(8,128)(2,1)S(1)}, u32[]{:S(2)}, u32[]{:S(2)}) collective-permute-start(bf16[2,512,256]{2,1,0:T(8,128)(2,1)S(1)} %get-tuple-element.6.fields_ref.own_ref), channel_id=1, source_target_pairs={{2,0},{5,1},{4,2},{7,3},{6,4},{1,5},{0,6},{3,7},{10,8},{13,9},{12,... | collective-permute-start | bytes 1572872 | tf_op jit(solution)/shard_map/ppermute | solution.py:194
  14.2 27.2 %all-to-all-start = ((bf16[64,8,384]{2,1,0:T(8,128)(2,1)}), bf16[64,8,384]{2,1,0:T(8,128)(2,1)S(1)}, u32[]{:S(2)}, u32[]{:S(2)}) async-start(bf16[64,8,384]{2,1,0:T(8,128)(2,1)} %shard_map.42._), calls=%async_computation | async-start | bytes 786432 | tf_op jit(solution)/shard_map/all_to_all | solution.py:232
  25.5 7.8 %collective-permute-start.4 = (bf16[2,512,256]{2,1,0:T(8,128)(2,1)S(1)}, bf16[2,512,256]{2,1,0:T(8,128)(2,1)S(1)}, u32[]{:S(2)}, u32[]{:S(2)}) collective-permute-start(bf16[2,512,256]{2,1,0:T(8,128)(2,1)S(1)} %collective-permute-done.3.second_ref), channel_id=1, source_target_pairs={{0,1},{1,0},{2,3},{3,2},{4,5},{5,4},{6,7},{7,6},{8,9},{9,8},{10,11... | collective-permute-start | bytes 1572872 | tf_op jit(solution)/shard_map/ppermute | solution.py:235
  30.0 3.8 %collective-permute-start.2 = (bf16[2,512,256]{2,1,0:T(8,128)(2,1)S(1)}, bf16[2,512,256]{2,1,0:T(8,128)(2,1)S(1)}, u32[]{:S(2)}, u32[]{:S(2)}) collective-permute-start(bf16[2,512,256]{2,1,0:T(8,128)(2,1)S(1)} %shard_map.44), channel_id=1, source_target_pairs={{0,1},{1,0},{2,3},{3,2},{4,5},{5,4},{6,7},{7,6},{8,9},{9,8},{10,11... | collective-permute-start | bytes 1572872 | tf_op jit(solution)/shard_map/ppermute | solution.py:234
  41.4 39.2 %all-to-all-start.1 = ((bf16[64,32,256]{2,1,0:T(8,128)(2,1)}), bf16[64,32,256]{2,1,0:T(8,128)(2,1)S(1)}, u32[]{:S(2)}, u32[]{:S(2)}) async-start(bf16[64,32,256]{2,1,0:T(8,128)(2,1)} %bitcast.4), calls=%async_computation.1 | async-start | bytes 2097152 | tf_op jit(solution)/shard_map/all_to_all | solution.py:258
  53.3 3.2 %collective-permute-start = (f32[2,256]{1,0:T(2,128)S(1)}, f32[2,256]{1,0:T(2,128)S(1)}, u32[]{:S(2)}, u32[]{:S(2)}) collective-permute-start(f32[2,256]{1,0:T(2,128)S(1)} %get-tuple-element.8.refs_1_), channel_id=1, source_target_pairs={{1,0},{2,1},{3,2},{4,3},{5,4},{6,5},{7,6},{0,7},{9,8},{10,9},{11,1... | collective-permute-start | bytes 6152 | tf_op jit(solution)/shard_map/ppermute | solution.py:273

commit v8 on v7

--- a/solution.py
+++ b/solution.py
@@ -165,13 +165,21 @@
     diag_out[0], diag_out[1] = rotate(diag[:diag_cols], diag[diag_cols:], row_phase, diag_phase, pixel_scale)
 
 
-def final_kernel(pixel_scale, starts_ref, own_ref, other_ref, band_ref, band_out):
-    part_cols = band_out.shape[1]
-    band = jnp.sum(band_ref[...].astype(F32), axis=0)
+def turn_kernel(pixel_scale, starts_ref, own_ref, other_ref, turn_out):
+    part_cols = turn_out.shape[1]
     row_phase = unit_phase(own_ref[0:1, :], own_ref[1:2, :])
     other_phase = unit_phase(other_ref[0:1, :], other_ref[1:2, :])
     col_phase = [pick_lanes(part, starts_ref[0], part_cols) for part in other_phase]
-    band_out[0], band_out[1] = rotate(band[:part_cols], band[part_cols:], row_phase, col_phase, pixel_scale)
+    turn_out[0] = (row_phase[0] * col_phase[0] + row_phase[1] * col_phase[1]) * pixel_scale
+    turn_out[1] = (row_phase[1] * col_phase[0] - row_phase[0] * col_phase[1]) * pixel_scale
+
+
+def final_kernel(turn_ref, band_ref, band_out):
+    part_cols = band_out.shape[1]
+    real = jnp.sum(band_ref[:, :part_cols, :].astype(F32), axis=0)
+    imag = jnp.sum(band_ref[:, part_cols:, :].astype(F32), axis=0)
+    band_out[0] = turn_ref[0] * real - turn_ref[1] * imag
+    band_out[1] = turn_ref[0] * imag + turn_ref[1] * real
 
 
 def shards(frames, ref_pixels):
@@ -271,14 +279,23 @@
         for m in range(mode_count):
             pairs.append((p * mode_count + (m + step) % mode_count, p * mode_count + m))
     other_ref = lax.ppermute(own_ref, (*PIX, "mode"), pairs)
+    part_shape = jax.ShapeDtypeStruct((2, part_cols, width), F32)
+    turn = pl.pallas_call(
+        lambda *refs: turn_kernel(scale, *refs),
+        out_shape=part_shape,
+        in_specs=[SMEM, VMEM, VMEM],
+        out_specs=VMEM,
+        cost_estimate=cost(field_bytes, field_bytes // 8),
+        compiler_params=params,
+    )(starts, own_ref, other_ref)
     band_out = pl.pallas_call(
-        lambda *refs: final_kernel(scale, *refs),
-        out_shape=jax.ShapeDtypeStruct((2, part_cols, width), F32),
-        in_specs=[SMEM] + [VMEM] * 3,
+        final_kernel,
+        out_shape=part_shape,
+        in_specs=[VMEM, VMEM],
         out_specs=VMEM,
         cost_estimate=cost(2 * field_bytes, 2 * field_bytes),
         compiler_params=params,
-    )(starts, own_ref, other_ref, band)
+    )(turn, band)
     return jnp.transpose(band_out, (0, 2, 1)), jnp.transpose(diag_out, (0, 2, 1))
 
 

time: 82.9 us -> 82.4 us (level)
  transfers between devices with their start and end apart: 7 -> 7, of which waited for: 5 -> 5; matrix products, arithmetic and copies ran while one was open for 0% -> 0% of each run, Pallas kernels for 7% -> 8%
where the time goes in v8:
time: 82.4 us; the launch traced here: 81.4 us
  starting transfers between devices  38.9 us (47%)
  waiting for transfers between devices  32.9 us (40%)
  Pallas kernels  8.75 us (11%)
    all_to_all x1, waiting for transfers between devices, shards(): lax.all_to_all(band.reshape(pix_count, 2 * part_cols, width), EXCHANGE, 0...  23.5 us
    all_to_all x1, starting transfers between devices, shards(): early = lax.all_to_all(early, EXCHANGE, 0, 0, tiled=True)  11.3 us
    ppermute x2, starting transfers between devices, shift(): return lax.ppermute(array, 'mode', pairs)  10.5 us
    all_to_all x1, starting transfers between devices, shards(): lax.all_to_all(band.reshape(pix_count, 2 * part_cols, width), EXCHANGE, 0...  10.5 us
    all_to_all x1, waiting for transfers between devices, shards(): early = lax.all_to_all(early, EXCHANGE, 0, 0, tiled=True)  6.11 us
    ppermute x1, starting transfers between devices, shards(): three = lax.ppermute(second, 'mode', swap)  2.75 us
    ppermute x1, starting transfers between devices, shards(): one = lax.ppermute(chosen, 'mode', swap)  1.92 us
    ppermute x1, starting transfers between devices, shards(): other_ref = lax.ppermute(own_ref, (*PIX, 'mode'), pairs)  1.91 us
  transfers between devices with their start and end apart: 7, of which 5 were waited for; matrix products, arithmetic and copies ran while one was open for 0% of the time, Pallas kernels for 8%

profile of v8, /device:TPU:6, one launch (start us, length us, event | category | flops | bytes accessed | tf_op | source)
XLA Modules:
  0.0 81.4 jit_solution(11785413971867076110)
XLA Ops:
  0.6 1.3 %shard_map.41 = (bf16[2,512,256]{2,1,0:T(8,128)(2,1)S(1)}, bf16[8,512]{1,0:T(8,128)(2,1)S(1)}) custom-call(s32[1]{0:T(128)} %bitcast.2.base_ref, bf16[4,512,256]{2,1,0:T(8,128)(2,1)} %frames_ref.1, s32[64]{0:T(128)} %pixels_ref.1), custom_call_target="tpu_custom_call" | custom-call | flops 524288 | bytes 1572864 | tf_op jit(solution)/shard_map/pallas_call | solution.py:208
  1.9 3.3 %collective-permute-start.3 = (bf16[2,512,256]{2,1,0:T(8,128)(2,1)S(1)}, bf16[2,512,256]{2,1,0:T(8,128)(2,1)S(1)}, u32[]{:S(2)}, u32[]{:S(2)}) collective-permute-start(bf16[2,512,256]{2,1,0:T(8,128)(2,1)S(1)} %get-tuple-element.6.fields_ref.own_ref), channel_id=1, source_target_pairs={{4,0},{3,1},{6,2},{5,3},{0,4},{7,5},{2,6},{1,7},{12,8},{11,9},{14,... | collective-permute-start | bytes 1572872 | tf_op jit(solution)/shard_map/ppermute | solution.py:202
  5.2 7.2 %collective-permute-start.1 = (bf16[2,512,256]{2,1,0:T(8,128)(2,1)S(1)}, bf16[2,512,256]{2,1,0:T(8,128)(2,1)S(1)}, u32[]{:S(2)}, u32[]{:S(2)}) collective-permute-start(bf16[2,512,256]{2,1,0:T(8,128)(2,1)S(1)} %get-tuple-element.6.fields_ref.own_ref), channel_id=1, source_target_pairs={{2,0},{5,1},{4,2},{7,3},{6,4},{1,5},{0,6},{3,7},{10,8},{13,9},{12,... | collective-permute-start | bytes 1572872 | tf_op jit(solution)/shard_map/ppermute | solution.py:202
  12.5 1.7 %shard_map.42._ = bf16[64,8,384]{2,1,0:T(8,128)(2,1)} custom-call(bf16[2,512,256]{2,1,0:T(8,128)(2,1)S(1)} %get-tuple-element.6.fields_ref.own_ref, bf16[8,512]{1,0:T(8,128)(2,1)S(1)} %get-tuple-element.7.counts_ref), custom_call_target="tpu_custom_call" | custom-call | flops 1073741824 | bytes 1048576 | tf_op jit(solution)/shard_map/pallas_call | solution.py:222
  14.2 11.3 %all-to-all-start = ((bf16[64,8,384]{2,1,0:T(8,128)(2,1)}), bf16[64,8,384]{2,1,0:T(8,128)(2,1)S(1)}, u32[]{:S(2)}, u32[]{:S(2)}) async-start(bf16[64,8,384]{2,1,0:T(8,128)(2,1)} %shard_map.42._), calls=%async_computation | async-start | bytes 786432 | tf_op jit(solution)/shard_map/all_to_all | solution.py:240
  25.5 0.0 collective-permute-done.3.second_ref
  25.5 2.7 %collective-permute-start.4 = (bf16[2,512,256]{2,1,0:T(8,128)(2,1)S(1)}, bf16[2,512,256]{2,1,0:T(8,128)(2,1)S(1)}, u32[]{:S(2)}, u32[]{:S(2)}) collective-permute-start(bf16[2,512,256]{2,1,0:T(8,128)(2,1)S(1)} %collective-permute-done.3.second_ref), channel_id=1, source_target_pairs={{0,1},{1,0},{2,3},{3,2},{4,5},{5,4},{6,7},{7,6},{8,9},{9,8},{10,11... | collective-permute-start | bytes 1572872 | tf_op jit(solution)/shard_map/ppermute | solution.py:243
  28.3 1.6 %collective-permute-done.1.near_ref.first_ref = bf16[2,512,256]{2,1,0:T(8,128)(2,1)S(1)} collective-permute-done((bf16[2,512,256]{2,1,0:T(8,128)(2,1)S(1)}, bf16[2,512,256]{2,1,0:T(8,128)(2,1)S(1)}, u32[]{:S(2)}, u32[]{:S(2)}) %collective-permute-start.1) | collective-permute-done | bytes 524320 | tf_op jit(solution)/shard_map/ppermute | solution.py:202
  30.0 1.9 %collective-permute-start.2 = (bf16[2,512,256]{2,1,0:T(8,128)(2,1)S(1)}, bf16[2,512,256]{2,1,0:T(8,128)(2,1)S(1)}, u32[]{:S(2)}, u32[]{:S(2)}) collective-permute-start(bf16[2,512,256]{2,1,0:T(8,128)(2,1)S(1)} %shard_map.45), channel_id=1, source_target_pairs={{0,1},{1,0},{2,3},{3,2},{4,5},{5,4},{6,7},{7,6},{8,9},{9,8},{10,11... | collective-permute-start | bytes 1572872 | tf_op jit(solution)/shard_map/ppermute | solution.py:242
  31.9 1.5 %shard_map.46._ = bf16[4,4,4,32,256]{4,3,2,1,0:T(8,128)(2,1)} custom-call(s32[1]{0:T(128)} %bitcast.3.core_ref, bf16[2,512,256]{2,1,0:T(8,128)(2,1)S(1)} %get-tuple-element.6.fields_ref.own_ref, bf16[2,512,256]{2,1,0:T(8,128)(2,1)S(1)} %collective-permute-done.1.near_ref.first_ref, bf16[2,512,256]{2,1,0:T(8,128)(2,1)S(1)} %collective-permute-done.3.second_ref), custom_call_target="tpu_custom_call" | custom-call | flops 536870912 | bytes 2097152 | tf_op jit(solution)/shard_map/pallas_call | solution.py:247
  33.4 0.0 collective-permute-done.4.three_ref
  33.4 0.4 collective-permute-done.2.one_ref
  33.8 1.5 %shard_map.47 = bf16[4,4,4,32,256]{4,3,2,1,0:T(8,128)(2,1)} custom-call(bf16[2,512,256]{2,1,0:T(8,128)(2,1)S(1)} %get-tuple-element.6.fields_ref.own_ref, bf16[2,512,256]{2,1,0:T(8,128)(2,1)S(1)} %collective-permute-done.2.one_ref, bf16[2,512,256]{2,1,0:T(8,128)(2,1)S(1)} %collective-permute-done.4.three_ref, ...), custom_call_target="tpu_custom_call", output_to_operand_aliasing={{}: (3, {})} | custom-call | flops 536870912 | bytes 2097152 | tf_op jit(solution)/shard_map/pallas_call | solution.py:256
  35.3 6.1 %all-to-all-done.refs_1_ = bf16[64,8,384]{2,1,0:T(8,128)(2,1)S(1)} async-done(((bf16[64,8,384]{2,1,0:T(8,128)(2,1)}), bf16[64,8,384]{2,1,0:T(8,128)(2,1)S(1)}, u32[]{:S(2)}, u32[]{:S(2)}) %all-to-all-start) | async-done | bytes 393248 | tf_op jit(solution)/shard_map/all_to_all | solution.py:240
  41.4 10.5 %all-to-all-start.1 = ((bf16[64,32,256]{2,1,0:T(8,128)(2,1)}), bf16[64,32,256]{2,1,0:T(8,128)(2,1)S(1)}, u32[]{:S(2)}, u32[]{:S(2)}) async-start(bf16[64,32,256]{2,1,0:T(8,128)(2,1)} %bitcast.4), calls=%async_computation.1 | async-start | bytes 2097152 | tf_op jit(solution)/shard_map/all_to_all | solution.py:266
  51.9 0.1 pad_add_fusion.refs_0_
  52.0 1.3 %shard_map.43 = (f32[2,4,256]{2,1,0:T(4,128)}, f32[2,256]{1,0:T(2,128)S(1)}) custom-call(s32[2]{0:T(128)S(1)} %pad_add_fusion.refs_0_, bf16[64,8,384]{2,1,0:T(8,128)(2,1)S(1)} %all-to-all-done.refs_1_), custom_call_target="tpu_custom_call" | custom-call | flops 524288 | bytes 524288 | tf_op jit(solution)/shard_map/pallas_call | solution.py:268
  53.3 1.9 %collective-permute-start = (f32[2,256]{1,0:T(2,128)S(1)}, f32[2,256]{1,0:T(2,128)S(1)}, u32[]{:S(2)}, u32[]{:S(2)}) collective-permute-start(f32[2,256]{1,0:T(2,128)S(1)} %get-tuple-element.8.refs_1_), channel_id=1, source_target_pairs={{1,0},{2,1},{3,2},{4,3},{5,4},{6,5},{7,6},{0,7},{9,8},{10,9},{11,1... | collective-permute-start | bytes 6152 | tf_op jit(solution)/shard_map/ppermute | solution.py:281
  55.2 1.3 %collective-permute-done.refs_2_ = f32[2,256]{1,0:T(2,128)S(1)} collective-permute-done((f32[2,256]{1,0:T(2,128)S(1)}, f32[2,256]{1,0:T(2,128)S(1)}, u32[]{:S(2)}, u32[]{:S(2)}) %collective-permute-start) | collective-permute-done | bytes 2080 | tf_op jit(solution)/shard_map/ppermute | solution.py:281
  56.5 0.6 shard_map.44.turn_ref
  57.1 23.5 %all-to-all-done.1.band_ref = bf16[64,32,256]{2,1,0:T(8,128)(2,1)S(1)} async-done(((bf16[64,32,256]{2,1,0:T(8,128)(2,1)}), bf16[64,32,256]{2,1,0:T(8,128)(2,1)S(1)}, u32[]{:S(2)}, u32[]{:S(2)}) %all-to-all-start.1) | async-done | bytes 1048608 | tf_op jit(solution)/shard_map/all_to_all | solution.py:266
  80.6 0.8 shard_map.48
  (1 shorter events, 0.0 us)
Async XLA Ops:
  1.9 23.6 %collective-permute-start.3 = (bf16[2,512,256]{2,1,0:T(8,128)(2,1)S(1)}, bf16[2,512,256]{2,1,0:T(8,128)(2,1)S(1)}, u32[]{:S(2)}, u32[]{:S(2)}) collective-permute-start(bf16[2,512,256]{2,1,0:T(8,128)(2,1)S(1)} %get-tuple-element.6.fields_ref.own_ref), channel_id=1, source_target_pairs={{4,0},{3,1},{6,2},{5,3},{0,4},{7,5},{2,6},{1,7},{12,8},{11,9},{14,... | collective-permute-start | bytes 1572872 | tf_op jit(solution)/shard_map/ppermute | solution.py:202
  5.2 24.7 %collective-permute-start.1 = (bf16[2,512,256]{2,1,0:T(8,128)(2,1)S(1)}, bf16[2,512,256]{2,1,0:T(8,128)(2,1)S(1)}, u32[]{:S(2)}, u32[]{:S(2)}) collective-permute-start(bf16[2,512,256]{2,1,0:T(8,128)(2,1)S(1)} %get-tuple-element.6.fields_ref.own_ref), channel_id=1, source_target_pairs={{2,0},{5,1},{4,2},{7,3},{6,4},{1,5},{0,6},{3,7},{10,8},{13,9},{12,... | collective-permute-start | bytes 1572872 | tf_op jit(solution)/shard_map/ppermute | solution.py:202
  14.2 27.2 %all-to-all-start = ((bf16[64,8,384]{2,1,0:T(8,128)(2,1)}), bf16[64,8,384]{2,1,0:T(8,128)(2,1)S(1)}, u32[]{:S(2)}, u32[]{:S(2)}) async-start(bf16[64,8,384]{2,1,0:T(8,128)(2,1)} %shard_map.42._), calls=%async_computation | async-start | bytes 786432 | tf_op jit(solution)/shard_map/all_to_all | solution.py:240
  25.5 7.8 %collective-permute-start.4 = (bf16[2,512,256]{2,1,0:T(8,128)(2,1)S(1)}, bf16[2,512,256]{2,1,0:T(8,128)(2,1)S(1)}, u32[]{:S(2)}, u32[]{:S(2)}) collective-permute-start(bf16[2,512,256]{2,1,0:T(8,128)(2,1)S(1)} %collective-permute-done.3.second_ref), channel_id=1, source_target_pairs={{0,1},{1,0},{2,3},{3,2},{4,5},{5,4},{6,7},{7,6},{8,9},{9,8},{10,11... | collective-permute-start | bytes 1572872 | tf_op jit(solution)/shard_map/ppermute | solution.py:243
  30.0 3.8 %collective-permute-start.2 = (bf16[2,512,256]{2,1,0:T(8,128)(2,1)S(1)}, bf16[2,512,256]{2,1,0:T(8,128)(2,1)S(1)}, u32[]{:S(2)}, u32[]{:S(2)}) collective-permute-start(bf16[2,512,256]{2,1,0:T(8,128)(2,1)S(1)} %shard_map.45), channel_id=1, source_target_pairs={{0,1},{1,0},{2,3},{3,2},{4,5},{5,4},{6,7},{7,6},{8,9},{9,8},{10,11... | collective-permute-start | bytes 1572872 | tf_op jit(solution)/shard_map/ppermute | solution.py:242
  41.4 39.2 %all-to-all-start.1 = ((bf16[64,32,256]{2,1,0:T(8,128)(2,1)}), bf16[64,32,256]{2,1,0:T(8,128)(2,1)S(1)}, u32[]{:S(2)}, u32[]{:S(2)}) async-start(bf16[64,32,256]{2,1,0:T(8,128)(2,1)} %bitcast.4), calls=%async_computation.1 | async-start | bytes 2097152 | tf_op jit(solution)/shard_map/all_to_all | solution.py:266
  53.3 3.2 %collective-permute-start = (f32[2,256]{1,0:T(2,128)S(1)}, f32[2,256]{1,0:T(2,128)S(1)}, u32[]{:S(2)}, u32[]{:S(2)}) collective-permute-start(f32[2,256]{1,0:T(2,128)S(1)} %get-tuple-element.8.refs_1_), channel_id=1, source_target_pairs={{1,0},{2,1},{3,2},{4,3},{5,4},{6,5},{7,6},{0,7},{9,8},{10,9},{11,1... | collective-permute-start | bytes 6152 | tf_op jit(solution)/shard_map/ppermute | solution.py:281

commit v9 on v8

--- a/solution.py
+++ b/solution.py
@@ -213,7 +213,7 @@
         scratch_shapes=[
             pltpu.VMEM(frames.shape, BF16),
             pltpu.SMEM(ref_pixels.shape, jnp.int32),
-            pltpu.SemaphoreType.DMA((5,)),
+            pltpu.SemaphoreType.DMA((3,)),
         ],
         cost_estimate=cost(4 * pixel_rows * width, 3 * field_bytes),
     )(base, frames, ref_pixels)

time: 82.4 us -> 82.4 us (level)
  no operation moved by 1% of the time
where the time goes in v9:
time: 82.4 us; the launch traced here: 81.4 us
  starting transfers between devices  38.9 us (47%)
  waiting for transfers between devices  32.9 us (40%)
  Pallas kernels  8.78 us (11%)
    all_to_all x1, waiting for transfers between devices, shards(): lax.all_to_all(band.reshape(pix_count, 2 * part_cols, width), EXCHANGE, 0...  23.5 us
    all_to_all x1, starting transfers between devices, shards(): early = lax.all_to_all(early, EXCHANGE, 0, 0, tiled=True)  11.3 us
    ppermute x2, starting transfers between devices, shift(): return lax.ppermute(array, 'mode', pairs)  10.5 us
    all_to_all x1, starting transfers between devices, shards(): lax.all_to_all(band.reshape(pix_count, 2 * part_cols, width), EXCHANGE, 0...  10.5 us
    all_to_all x1, waiting for transfers between devices, shards(): early = lax.all_to_all(early, EXCHANGE, 0, 0, tiled=True)  6.11 us
    ppermute x1, starting transfers between devices, shards(): three = lax.ppermute(second, 'mode', swap)  2.74 us
    ppermute x1, starting transfers between devices, shards(): one = lax.ppermute(chosen, 'mode', swap)  1.92 us
    ppermute x1, starting transfers between devices, shards(): other_ref = lax.ppermute(own_ref, (*PIX, 'mode'), pairs)  1.91 us
  transfers between devices with their start and end apart: 7, of which 5 were waited for; matrix products, arithmetic and copies ran while one was open for 0% of the time, Pallas kernels for 8%

profile of v9, /device:TPU:6, one launch (start us, length us, event | category | flops | bytes accessed | tf_op | source)
XLA Modules:
  0.0 81.4 jit_solution(1142764605044961950)
XLA Ops:
  0.6 1.3 %shard_map.41 = (bf16[2,512,256]{2,1,0:T(8,128)(2,1)S(1)}, bf16[8,512]{1,0:T(8,128)(2,1)S(1)}) custom-call(s32[1]{0:T(128)} %bitcast.2.base_ref, bf16[4,512,256]{2,1,0:T(8,128)(2,1)} %frames_ref.1, s32[64]{0:T(128)} %pixels_ref.1), custom_call_target="tpu_custom_call" | custom-call | flops 524288 | bytes 1572864 | tf_op jit(solution)/shard_map/pallas_call | solution.py:208
  1.9 3.3 %collective-permute-start.3 = (bf16[2,512,256]{2,1,0:T(8,128)(2,1)S(1)}, bf16[2,512,256]{2,1,0:T(8,128)(2,1)S(1)}, u32[]{:S(2)}, u32[]{:S(2)}) collective-permute-start(bf16[2,512,256]{2,1,0:T(8,128)(2,1)S(1)} %get-tuple-element.6.fields_ref.own_ref), channel_id=1, source_target_pairs={{4,0},{3,1},{6,2},{5,3},{0,4},{7,5},{2,6},{1,7},{12,8},{11,9},{14,... | collective-permute-start | bytes 1572872 | tf_op jit(solution)/shard_map/ppermute | solution.py:202
  5.3 7.2 %collective-permute-start.1 = (bf16[2,512,256]{2,1,0:T(8,128)(2,1)S(1)}, bf16[2,512,256]{2,1,0:T(8,128)(2,1)S(1)}, u32[]{:S(2)}, u32[]{:S(2)}) collective-permute-start(bf16[2,512,256]{2,1,0:T(8,128)(2,1)S(1)} %get-tuple-element.6.fields_ref.own_ref), channel_id=1, source_target_pairs={{2,0},{5,1},{4,2},{7,3},{6,4},{1,5},{0,6},{3,7},{10,8},{13,9},{12,... | collective-permute-start | bytes 1572872 | tf_op jit(solution)/shard_map/ppermute | solution.py:202
  12.5 1.7 %shard_map.42._ = bf16[64,8,384]{2,1,0:T(8,128)(2,1)} custom-call(bf16[2,512,256]{2,1,0:T(8,128)(2,1)S(1)} %get-tuple-element.6.fields_ref.own_ref, bf16[8,512]{1,0:T(8,128)(2,1)S(1)} %get-tuple-element.7.counts_ref), custom_call_target="tpu_custom_call" | custom-call | flops 1073741824 | bytes 1048576 | tf_op jit(solution)/shard_map/pallas_call | solution.py:222
  14.2 11.3 %all-to-all-start = ((bf16[64,8,384]{2,1,0:T(8,128)(2,1)}), bf16[64,8,384]{2,1,0:T(8,128)(2,1)S(1)}, u32[]{:S(2)}, u32[]{:S(2)}) async-start(bf16[64,8,384]{2,1,0:T(8,128)(2,1)} %shard_map.42._), calls=%async_computation | async-start | bytes 786432 | tf_op jit(solution)/shard_map/all_to_all | solution.py:240
  25.5 0.0 collective-permute-done.3.second_ref
  25.6 2.7 %collective-permute-start.4 = (bf16[2,512,256]{2,1,0:T(8,128)(2,1)S(1)}, bf16[2,512,256]{2,1,0:T(8,128)(2,1)S(1)}, u32[]{:S(2)}, u32[]{:S(2)}) collective-permute-start(bf16[2,512,256]{2,1,0:T(8,128)(2,1)S(1)} %collective-permute-done.3.second_ref), channel_id=1, source_target_pairs={{0,1},{1,0},{2,3},{3,2},{4,5},{5,4},{6,7},{7,6},{8,9},{9,8},{10,11... | collective-permute-start | bytes 1572872 | tf_op jit(solution)/shard_map/ppermute | solution.py:243
  28.3 1.6 %collective-permute-done.1.near_ref.first_ref = bf16[2,512,256]{2,1,0:T(8,128)(2,1)S(1)} collective-permute-done((bf16[2,512,256]{2,1,0:T(8,128)(2,1)S(1)}, bf16[2,512,256]{2,1,0:T(8,128)(2,1)S(1)}, u32[]{:S(2)}, u32[]{:S(2)}) %collective-permute-start.1) | collective-permute-done | bytes 524320 | tf_op jit(solution)/shard_map/ppermute | solution.py:202
  30.0 1.9 %collective-permute-start.2 = (bf16[2,512,256]{2,1,0:T(8,128)(2,1)S(1)}, bf16[2,512,256]{2,1,0:T(8,128)(2,1)S(1)}, u32[]{:S(2)}, u32[]{:S(2)}) collective-permute-start(bf16[2,512,256]{2,1,0:T(8,128)(2,1)S(1)} %shard_map.45), channel_id=1, source_target_pairs={{0,1},{1,0},{2,3},{3,2},{4,5},{5,4},{6,7},{7,6},{8,9},{9,8},{10,11... | collective-permute-start | bytes 1572872 | tf_op jit(solution)/shard_map/ppermute | solution.py:242
  31.9 1.5 %shard_map.46._ = bf16[4,4,4,32,256]{4,3,2,1,0:T(8,128)(2,1)} custom-call(s32[1]{0:T(128)} %bitcast.3.core_ref, bf16[2,512,256]{2,1,0:T(8,128)(2,1)S(1)} %get-tuple-element.6.fields_ref.own_ref, bf16[2,512,256]{2,1,0:T(8,128)(2,1)S(1)} %collective-permute-done.1.near_ref.first_ref, bf16[2,512,256]{2,1,0:T(8,128)(2,1)S(1)} %collective-permute-done.3.second_ref), custom_call_target="tpu_custom_call" | custom-call | flops 536870912 | bytes 2097152 | tf_op jit(solution)/shard_map/pallas_call | solution.py:247
  33.4 0.0 collective-permute-done.4.three_ref
  33.4 0.4 collective-permute-done.2.one_ref
  33.8 1.5 %shard_map.47 = bf16[4,4,4,32,256]{4,3,2,1,0:T(8,128)(2,1)} custom-call(bf16[2,512,256]{2,1,0:T(8,128)(2,1)S(1)} %get-tuple-element.6.fields_ref.own_ref, bf16[2,512,256]{2,1,0:T(8,128)(2,1)S(1)} %collective-permute-done.2.one_ref, bf16[2,512,256]{2,1,0:T(8,128)(2,1)S(1)} %collective-permute-done.4.three_ref, ...), custom_call_target="tpu_custom_call", output_to_operand_aliasing={{}: (3, {})} | custom-call | flops 536870912 | bytes 2097152 | tf_op jit(solution)/shard_map/pallas_call | solution.py:256
  35.3 6.1 %all-to-all-done.refs_1_ = bf16[64,8,384]{2,1,0:T(8,128)(2,1)S(1)} async-done(((bf16[64,8,384]{2,1,0:T(8,128)(2,1)}), bf16[64,8,384]{2,1,0:T(8,128)(2,1)S(1)}, u32[]{:S(2)}, u32[]{:S(2)}) %all-to-all-start) | async-done | bytes 393248 | tf_op jit(solution)/shard_map/all_to_all | solution.py:240
  41.4 10.5 %all-to-all-start.1 = ((bf16[64,32,256]{2,1,0:T(8,128)(2,1)}), bf16[64,32,256]{2,1,0:T(8,128)(2,1)S(1)}, u32[]{:S(2)}, u32[]{:S(2)}) async-start(bf16[64,32,256]{2,1,0:T(8,128)(2,1)} %bitcast.4), calls=%async_computation.1 | async-start | bytes 2097152 | tf_op jit(solution)/shard_map/all_to_all | solution.py:266
  51.9 0.1 pad_add_fusion.refs_0_
  52.0 1.3 %shard_map.43 = (f32[2,4,256]{2,1,0:T(4,128)}, f32[2,256]{1,0:T(2,128)S(1)}) custom-call(s32[2]{0:T(128)S(1)} %pad_add_fusion.refs_0_, bf16[64,8,384]{2,1,0:T(8,128)(2,1)S(1)} %all-to-all-done.refs_1_), custom_call_target="tpu_custom_call" | custom-call | flops 524288 | bytes 524288 | tf_op jit(solution)/shard_map/pallas_call | solution.py:268
  53.3 1.9 %collective-permute-start = (f32[2,256]{1,0:T(2,128)S(1)}, f32[2,256]{1,0:T(2,128)S(1)}, u32[]{:S(2)}, u32[]{:S(2)}) collective-permute-start(f32[2,256]{1,0:T(2,128)S(1)} %get-tuple-element.8.refs_1_), channel_id=1, source_target_pairs={{1,0},{2,1},{3,2},{4,3},{5,4},{6,5},{7,6},{0,7},{9,8},{10,9},{11,1... | collective-permute-start | bytes 6152 | tf_op jit(solution)/shard_map/ppermute | solution.py:281
  55.2 1.3 %collective-permute-done.refs_2_ = f32[2,256]{1,0:T(2,128)S(1)} collective-permute-done((f32[2,256]{1,0:T(2,128)S(1)}, f32[2,256]{1,0:T(2,128)S(1)}, u32[]{:S(2)}, u32[]{:S(2)}) %collective-permute-start) | collective-permute-done | bytes 2080 | tf_op jit(solution)/shard_map/ppermute | solution.py:281
  56.5 0.6 shard_map.44.turn_ref
  57.2 23.5 %all-to-all-done.1.band_ref = bf16[64,32,256]{2,1,0:T(8,128)(2,1)S(1)} async-done(((bf16[64,32,256]{2,1,0:T(8,128)(2,1)}), bf16[64,32,256]{2,1,0:T(8,128)(2,1)S(1)}, u32[]{:S(2)}, u32[]{:S(2)}) %all-to-all-start.1) | async-done | bytes 1048608 | tf_op jit(solution)/shard_map/all_to_all | solution.py:266
  80.6 0.8 shard_map.48
  (1 shorter events, 0.0 us)
Async XLA Ops:
  1.9 23.6 %collective-permute-start.3 = (bf16[2,512,256]{2,1,0:T(8,128)(2,1)S(1)}, bf16[2,512,256]{2,1,0:T(8,128)(2,1)S(1)}, u32[]{:S(2)}, u32[]{:S(2)}) collective-permute-start(bf16[2,512,256]{2,1,0:T(8,128)(2,1)S(1)} %get-tuple-element.6.fields_ref.own_ref), channel_id=1, source_target_pairs={{4,0},{3,1},{6,2},{5,3},{0,4},{7,5},{2,6},{1,7},{12,8},{11,9},{14,... | collective-permute-start | bytes 1572872 | tf_op jit(solution)/shard_map/ppermute | solution.py:202
  5.3 24.7 %collective-permute-start.1 = (bf16[2,512,256]{2,1,0:T(8,128)(2,1)S(1)}, bf16[2,512,256]{2,1,0:T(8,128)(2,1)S(1)}, u32[]{:S(2)}, u32[]{:S(2)}) collective-permute-start(bf16[2,512,256]{2,1,0:T(8,128)(2,1)S(1)} %get-tuple-element.6.fields_ref.own_ref), channel_id=1, source_target_pairs={{2,0},{5,1},{4,2},{7,3},{6,4},{1,5},{0,6},{3,7},{10,8},{13,9},{12,... | collective-permute-start | bytes 1572872 | tf_op jit(solution)/shard_map/ppermute | solution.py:202
  14.2 27.2 %all-to-all-start = ((bf16[64,8,384]{2,1,0:T(8,128)(2,1)}), bf16[64,8,384]{2,1,0:T(8,128)(2,1)S(1)}, u32[]{:S(2)}, u32[]{:S(2)}) async-start(bf16[64,8,384]{2,1,0:T(8,128)(2,1)} %shard_map.42._), calls=%async_computation | async-start | bytes 786432 | tf_op jit(solution)/shard_map/all_to_all | solution.py:240
  25.6 7.8 %collective-permute-start.4 = (bf16[2,512,256]{2,1,0:T(8,128)(2,1)S(1)}, bf16[2,512,256]{2,1,0:T(8,128)(2,1)S(1)}, u32[]{:S(2)}, u32[]{:S(2)}) collective-permute-start(bf16[2,512,256]{2,1,0:T(8,128)(2,1)S(1)} %collective-permute-done.3.second_ref), channel_id=1, source_target_pairs={{0,1},{1,0},{2,3},{3,2},{4,5},{5,4},{6,7},{7,6},{8,9},{9,8},{10,11... | collective-permute-start | bytes 1572872 | tf_op jit(solution)/shard_map/ppermute | solution.py:243
  30.0 3.8 %collective-permute-start.2 = (bf16[2,512,256]{2,1,0:T(8,128)(2,1)S(1)}, bf16[2,512,256]{2,1,0:T(8,128)(2,1)S(1)}, u32[]{:S(2)}, u32[]{:S(2)}) collective-permute-start(bf16[2,512,256]{2,1,0:T(8,128)(2,1)S(1)} %shard_map.45), channel_id=1, source_target_pairs={{0,1},{1,0},{2,3},{3,2},{4,5},{5,4},{6,7},{7,6},{8,9},{9,8},{10,11... | collective-permute-start | bytes 1572872 | tf_op jit(solution)/shard_map/ppermute | solution.py:242
  41.4 39.2 %all-to-all-start.1 = ((bf16[64,32,256]{2,1,0:T(8,128)(2,1)}), bf16[64,32,256]{2,1,0:T(8,128)(2,1)S(1)}, u32[]{:S(2)}, u32[]{:S(2)}) async-start(bf16[64,32,256]{2,1,0:T(8,128)(2,1)} %bitcast.4), calls=%async_computation.1 | async-start | bytes 2097152 | tf_op jit(solution)/shard_map/all_to_all | solution.py:266
  53.3 3.2 %collective-permute-start = (f32[2,256]{1,0:T(2,128)S(1)}, f32[2,256]{1,0:T(2,128)S(1)}, u32[]{:S(2)}, u32[]{:S(2)}) collective-permute-start(f32[2,256]{1,0:T(2,128)S(1)} %get-tuple-element.8.refs_1_), channel_id=1, source_target_pairs={{1,0},{2,1},{3,2},{4,3},{5,4},{6,5},{7,6},{0,7},{9,8},{10,9},{11,1... | collective-permute-start | bytes 6152 | tf_op jit(solution)/shard_map/ppermute | solution.py:281
